TPU v7x, 32 devices: a whole 2x2x4 slice. The times are simulated.
32 devices in a mesh: pipe: 8 (over y, x, core), expert: 4 (over z).
Axes of the slice: x: 2, y: 2, z: 4, core: 2. Of those that a mesh axis runs over, the one named last changes fastest.
Arguments:
- tokens: bfloat16 [8, 256, 3584], P('pipe', 'expert'), may hold values from -6 to 6
- cotangent: bfloat16 [8, 256, 3584], P('pipe', 'expert'), may hold values from -6 to 6
- router_gate: float32 [8, 256], P('pipe', 'expert'), may hold values from 0.3 to 1
- routes: int32 [8, 256, 1], P('pipe', 'expert'), may hold values from 0 to 1; in each aligned block of 64 rows (0 to 63, 64 to 127, ..., all dimensions but the last counted through in order) at most 34 rows name the same one
- up_weight: bfloat16 [8, 3584, 2048], P('pipe', None, 'expert'), as said below
- down_weight: bfloat16 [8, 2048, 3584], P('pipe', 'expert'), as said below
Outputs:
- input_grad: bfloat16 [8, 256, 3584], P('pipe', 'expert')
- grad_up: bfloat16 [8, 1792, 2048], P('pipe', None, 'expert')
- grad_down: bfloat16 [8, 2048, 1792], P('pipe', 'expert')
Inputs may be any that keep to these rules, and one draw needn't show every extreme that they name: `routes`: among the 64 tokens of one device no expert is named more than 34 times, and some device names some expert exactly 34 times. up_weight[p] equals up_weight[7 - p]. down_weight[p] equals down_weight[7 - p].
All inputs are finite; a program needn't handle non-finite values.
Results may differ from a plain program's by a relative error of at most 0.0085.
Values may be sent and summed in bfloat16 or wider, within the bound.
No kernel may reach another device: no remote copies, remote signals or barrier semaphores. Data moves between devices by JAX's collectives and lax.ppermute only.
A program may use at most 64 MiB of HBM per device.

v0:
```python
import jax
import jax.numpy as jnp
from jax import lax
from jax.sharding import PartitionSpec as P

EXPERTS = 2
CAP = 34


def partner(value, axis, bit):
    mask = 2**bit
    pairs = [(source, source ^ mask) for source in range(lax.axis_size(axis))]
    return lax.ppermute(value, axis, pairs)


def slot_numbers(route_ids, expert_count):
    member = (route_ids[..., None] == jnp.arange(expert_count, dtype=jnp.int32)).astype(jnp.int32)
    before = jnp.cumsum(member, axis=-2) - member
    return jnp.sum(before * member, axis=-1)


def per_device(tokens, cotangent, router_gate, routes, up_weight, down_weight):
    owners = lax.axis_size("expert")
    ranks = lax.axis_size("pipe")
    group = owners // EXPERTS
    inputs = tokens[0]
    tok_count = inputs.shape[0]
    model_width = inputs.shape[1]
    route_ids = routes[0, :, 0]
    scaled = (router_gate[0][:, None] * cotangent[0].astype(jnp.float32)).astype(jnp.bfloat16)
    slots = slot_numbers(route_ids, EXPERTS)
    own_place = jnp.logical_and(
        route_ids[None, None, :] == jnp.arange(EXPERTS, dtype=jnp.int32)[:, None, None],
        slots[None, None, :] == jnp.arange(CAP, dtype=jnp.int32)[None, :, None],
    )
    place_half = own_place.astype(jnp.bfloat16)
    bucket_x = jnp.einsum(
        "ect,td->ecd", place_half, inputs, preferred_element_type=jnp.float32
    ).astype(jnp.bfloat16)
    bucket_g = jnp.einsum(
        "ect,td->ecd", place_half, scaled, preferred_element_type=jnp.float32
    ).astype(jnp.bfloat16)
    send_x = jnp.repeat(bucket_x, group, axis=0).reshape(owners * CAP, model_width)
    send_g = jnp.repeat(bucket_g, group, axis=0).reshape(owners * CAP, model_width)
    rows_x, rows_g = (
        lax.all_to_all(send_x, "expert", split_axis=0, concat_axis=0, tiled=True),
        lax.all_to_all(send_g, "expert", split_axis=0, concat_axis=0, tiled=True),
    )
    up_local = up_weight[0]
    down_local = down_weight[0]
    pre = jnp.dot(rows_x, up_local, preferred_element_type=jnp.float32)
    act = jax.nn.silu(pre).astype(jnp.bfloat16)
    dact = lax.dot_general(
        rows_g, down_local, (((1,), (1,)), ((), ())), preferred_element_type=jnp.float32
    )
    sigma = jax.nn.sigmoid(pre)
    dpre = (dact * sigma * (1.0 + pre * (1.0 - sigma))).astype(jnp.bfloat16)
    down_flip = lax.dot_general(
        rows_g, act, (((0,), (0,)), ((), ())), preferred_element_type=jnp.float32
    ).astype(jnp.bfloat16)
    up_term = lax.dot_general(
        rows_x, dpre, (((0,), (0,)), ((), ())), preferred_element_type=jnp.float32
    ).astype(jnp.bfloat16)
    part_dx = lax.dot_general(
        dpre, up_local, (((1,), (1,)), ((), ())), preferred_element_type=jnp.float32
    ).astype(jnp.bfloat16)
    returned = lax.all_to_all(part_dx, "expert", split_axis=0, concat_axis=0, tiled=True)
    summed = jnp.sum(
        returned.reshape(EXPERTS, group, CAP, model_width).astype(jnp.float32), axis=1
    ).reshape(EXPERTS * CAP, model_width)
    place_full = own_place.reshape(EXPERTS * CAP, tok_count).astype(jnp.float32)
    input_grad = lax.dot_general(
        place_full,
        summed,
        (((0,), (0,)), ((), ())),
        precision=lax.Precision.HIGHEST,
        preferred_element_type=jnp.float32,
    ).astype(jnp.bfloat16)
    half = model_width // 2
    upper = (lax.axis_index("pipe") >= ranks // 2).astype(jnp.int32)
    lower = 1 - upper
    own_up = lax.dynamic_slice_in_dim(up_term, upper * half, half, 0)
    own_down = lax.dynamic_slice_in_dim(down_flip, upper * half, half, 0)
    sent_up = lax.dynamic_slice_in_dim(up_term, lower * half, half, 0)
    sent_down = lax.dynamic_slice_in_dim(down_flip, lower * half, half, 0)
    bit_count = ranks.bit_length() - 1
    for bit_index in range(bit_count):
        sent_up, sent_down = partner((sent_up, sent_down), "pipe", bit_index)
    grad_up = (own_up.astype(jnp.float32) + sent_up.astype(jnp.float32)).astype(jnp.bfloat16)
    grad_down = (
        (own_down.astype(jnp.float32) + sent_down.astype(jnp.float32)).astype(jnp.bfloat16).T
    )
    return (input_grad[None], grad_up[None], grad_down[None])


def solution(mesh):
    placed = (
        P("pipe", "expert", None),
        P("pipe", "expert", None),
        P("pipe", "expert"),
        P("pipe", "expert", None),
        P("pipe", None, "expert"),
        P("pipe", "expert", None),
    )
    return jax.shard_map(
        per_device,
        mesh=mesh,
        in_specs=placed,
        out_specs=(P("pipe", "expert", None), P("pipe", None, "expert"), P("pipe", "expert", None)),
        check_vma=False,
    )
```

profile of v0, /device:TPU:0, one launch (start us, length us, event | category | flops | bytes accessed | tf_op | source)
XLA Modules:
  0.0 209.6 jit_solution(17914526661978648876)
XLA Ops:
  0.6 0.0 copy-start
  0.6 0.8 fusion.28
  1.4 0.7 iota_compare_fusion.2
  2.1 0.1 reduce_window_sum.11
  2.2 0.8 select_reduce_fusion
  3.0 0.0 copy-done
  3.0 0.3 convolution_convert_fusion.3
  3.3 0.0 copy-start.5
  3.4 0.0 copy-start.6
  3.4 1.1 broadcast_in_dim.20
  4.4 6.3 %all-to-all-start.1 = ((bf16[4,34,3584]{2,1,0:T(8,128)(2,1)}), bf16[4,34,3584]{2,1,0:T(8,128)(2,1)S(1)}, u32[]{:S(2)}, u32[]{:S(2)}) async-start(bf16[4,34,3584]{2,1,0:T(8,128)(2,1)} %bitcast.8), calls=%async_computation.1 | async-start | bytes 2293760 | tf_op jit(solution)/shard_map/all_to_all | solution.py:46
  10.8 0.0 copy-done.5
  10.8 0.0 copy-done.6
  10.8 0.4 convolution_convert_fusion.4
  11.2 27.5 %all-to-all-done.1 = bf16[4,34,3584]{2,1,0:T(8,128)(2,1)S(1)} async-done(((bf16[4,34,3584]{2,1,0:T(8,128)(2,1)}), bf16[4,34,3584]{2,1,0:T(8,128)(2,1)S(1)}, u32[]{:S(2)}, u32[]{:S(2)}) %all-to-all-start.1) | async-done | bytes 974880 | tf_op jit(solution)/shard_map/all_to_all | solution.py:46
  38.6 1.1 broadcast_in_dim.19
  39.7 4.3 %all-to-all-start = ((bf16[4,34,3584]{2,1,0:T(8,128)(2,1)}), bf16[4,34,3584]{2,1,0:T(8,128)(2,1)}, u32[]{:S(2)}, u32[]{:S(2)}) async-start(bf16[4,34,3584]{2,1,0:T(8,128)(2,1)} %bitcast.4), calls=%async_computation | async-start | bytes 2293760 | tf_op jit(solution)/shard_map/all_to_all | solution.py:47
  44.0 0.3 all_to_all.27
  44.3 2.7 %fusion.3 = f32[136,512]{1,0:T(8,128)S(1)} fusion(bf16[136,3584]{1,0:T(8,128)(2,1)S(1)} %all_to_all.27, bf16[1,3584,512]{2,1,0:T(8,128)(2,1)} %param.10), kind=kOutput, calls=%fused_computation.9 | convolution fusion | flops 499122176 | bytes 4923392 | tf_op jit(solution)/shard_map/dot_general | solution.py:51
  47.0 24.4 %all-to-all-done = bf16[4,34,3584]{2,1,0:T(8,128)(2,1)} async-done(((bf16[4,34,3584]{2,1,0:T(8,128)(2,1)}), bf16[4,34,3584]{2,1,0:T(8,128)(2,1)}, u32[]{:S(2)}, u32[]{:S(2)}) %all-to-all-start) | async-done | bytes 974880 | tf_op jit(solution)/shard_map/all_to_all | solution.py:47
  71.4 1.5 all_to_all.24
  73.0 1.2 convolution_convert_fusion
  74.2 0.0 copy-start.3
  74.2 0.0 copy-start.7
  74.2 0.1 constant_dynamic-slice_fusion.1
  74.4 1.7 copy-done.3
  76.1 0.0 collective-permute-start.3
  76.1 1.5 copy-done.7
  77.6 1.3 fusion.15
  78.9 1.2 convolution_convert_fusion.1
  80.2 0.0 copy-start.1
  80.2 0.0 copy-start.2
  80.2 0.1 constant_dynamic-slice_fusion
  80.3 1.7 copy-done.1
  82.0 0.0 collective-permute-start
  82.0 0.0 collective-permute-done.3
  82.0 1.5 collective-permute-start.4
  83.5 2.4 %collective-permute-done = bf16[1792,512]{1,0:T(8,128)(2,1)} collective-permute-done((bf16[1792,512]{1,0:T(8,128)(2,1)S(1)}, bf16[1792,512]{1,0:T(8,128)(2,1)}, u32[]{:S(2)}, u32[]{:S(2)}) %collective-permute-start) | collective-permute-done | bytes 1835040 | tf_op jit(solution)/shard_map/ppermute | solution.py:13
  86.0 1.5 collective-permute-start.1
  87.4 37.6 %collective-permute-done.4 = bf16[1792,512]{1,0:T(8,128)(2,1)} collective-permute-done((bf16[1792,512]{1,0:T(8,128)(2,1)S(1)}, bf16[1792,512]{1,0:T(8,128)(2,1)}, u32[]{:S(2)}, u32[]{:S(2)}) %collective-permute-start.4) | collective-permute-done | bytes 1835040 | tf_op jit(solution)/shard_map/ppermute | solution.py:13
  125.0 1.5 collective-permute-start.5
  126.6 0.0 copy-done.2
  126.6 1.3 convolution_convert_fusion.2
  127.9 1.3 all_to_all.28
  129.2 3.5 %all-to-all-start.2 = ((bf16[4,34,3584]{2,1,0:T(8,128)(2,1)}), bf16[4,34,3584]{2,1,0:T(8,128)(2,1)S(1)}, u32[]{:S(2)}, u32[]{:S(2)}) async-start(bf16[4,34,3584]{2,1,0:T(8,128)(2,1)} %all_to_all.28), calls=%async_computation.2 | async-start | bytes 2293760 | tf_op jit(solution)/shard_map/all_to_all | solution.py:67
  132.7 31.2 %collective-permute-done.1 = bf16[1792,512]{1,0:T(8,128)(2,1)} collective-permute-done((bf16[1792,512]{1,0:T(8,128)(2,1)}, bf16[1792,512]{1,0:T(8,128)(2,1)}, u32[]{:S(2)}, u32[]{:S(2)}) %collective-permute-start.1) | collective-permute-done | bytes 1835040 | tf_op jit(solution)/shard_map/ppermute | solution.py:13
  163.9 1.5 collective-permute-start.2
  165.4 0.0 all-to-all-done.2
  165.4 0.0 copy-start.4
  165.4 0.2 convert_reduce_fusion
  165.6 1.4 fusion.1
  167.1 0.0 collective-permute-done.5
  167.1 0.6 copy-done.4
  167.6 2.0 fusion.8
  169.7 2.4 %copy.10 = bf16[1,512,1792]{2,1,0:T(8,128)(2,1)} copy(bf16[1,512,1792]{1,2,0:T(8,128)(2,1)S(1)} %fusion.8) | data formatting | bytes 3670016
  172.1 33.7 %collective-permute-done.2 = bf16[1792,512]{1,0:T(8,128)(2,1)} collective-permute-done((bf16[1792,512]{1,0:T(8,128)(2,1)}, bf16[1792,512]{1,0:T(8,128)(2,1)}, u32[]{:S(2)}, u32[]{:S(2)}) %collective-permute-start.2) | collective-permute-done | bytes 1835040 | tf_op jit(solution)/shard_map/ppermute | solution.py:13
  205.8 3.8 %fusion.7 = bf16[1,1792,512]{2,1,0:T(8,128)(2,1)} fusion(bf16[1792,512]{1,0:T(8,128)(2,1)} %collective-permute-done.2, bf16[3584,512]{1,0:T(8,128)(2,1)} %copy-done.1, s32[]{:T(128)S(6)} %mul.41), kind=kLoop, calls=%fused_computation.16 | loop fusion | flops 3670016 | bytes 5505028 | tf_op jit(solution)/shard_map/broadcast_in_dim | solution.py:93
  (1 shorter events, 0.0 us)
Async XLA Ops:
  0.6 2.4 %copy-start = (bf16[1,64,3584]{2,1,0:T(8,128)(2,1)S(1)}, bf16[1,64,3584]{2,1,0:T(8,128)(2,1)}, u32[]{:S(2)}) copy-start(bf16[1,64,3584]{2,1,0:T(8,128)(2,1)} %param.6) | copy-start | bytes 1376260
  3.3 7.5 %copy-start.5 = (bf16[1,64,3584]{2,1,0:T(8,128)(2,1)S(1)}, bf16[1,64,3584]{2,1,0:T(8,128)(2,1)}, u32[]{:S(2)}) copy-start(bf16[1,64,3584]{2,1,0:T(8,128)(2,1)} %param.7) | copy-start | bytes 1376260
  3.4 7.4 %copy-start.6 = (f32[1,64]{1,0:T(1,128)S(1)}, f32[1,64]{1,0:T(1,128)}, u32[]{:S(2)}) copy-start(f32[1,64]{1,0:T(1,128)} %param.8) | copy-start | bytes 772
  4.4 34.2 %all-to-all-start.1 = ((bf16[4,34,3584]{2,1,0:T(8,128)(2,1)}), bf16[4,34,3584]{2,1,0:T(8,128)(2,1)S(1)}, u32[]{:S(2)}, u32[]{:S(2)}) async-start(bf16[4,34,3584]{2,1,0:T(8,128)(2,1)} %bitcast.8), calls=%async_computation.1 | async-start | bytes 2293760 | tf_op jit(solution)/shard_map/all_to_all | solution.py:46
  39.7 31.7 %all-to-all-start = ((bf16[4,34,3584]{2,1,0:T(8,128)(2,1)}), bf16[4,34,3584]{2,1,0:T(8,128)(2,1)}, u32[]{:S(2)}, u32[]{:S(2)}) async-start(bf16[4,34,3584]{2,1,0:T(8,128)(2,1)} %bitcast.4), calls=%async_computation | async-start | bytes 2293760 | tf_op jit(solution)/shard_map/all_to_all | solution.py:47
  74.2 1.9 copy-start.3
  74.2 3.4 %copy-start.7 = (bf16[1,512,3584]{2,1,0:T(8,128)(2,1)S(1)}, bf16[1,512,3584]{2,1,0:T(8,128)(2,1)}, u32[]{:S(2)}) copy-start(bf16[1,512,3584]{2,1,0:T(8,128)(2,1)} %param.11) | copy-start | bytes 11010052
  76.1 5.9 %collective-permute-start.3 = (bf16[1792,512]{1,0:T(8,128)(2,1)S(1)}, bf16[1792,512]{1,0:T(8,128)(2,1)S(1)}, u32[]{:S(2)}, u32[]{:S(2)}) collective-permute-start(bf16[1792,512]{1,0:T(8,128)(2,1)S(1)} %constant_dynamic-slice_fusion.1), channel_id=1, source_target_pairs={{0,4},{4,0},{8,12},{12,8},{16,20},{20,16},{24,28},{28,24},{1,5},{5... | collective-permute-start | bytes 5505032 | tf_op jit(solution)/shard_map/ppermute | solution.py:13
  80.2 1.9 copy-start.1
  80.2 46.4 %copy-start.2 = (bf16[1,3584,512]{2,1,0:T(8,128)(2,1)S(1)}, bf16[1,3584,512]{2,1,0:T(8,128)(2,1)}, u32[]{:S(2)}) copy-start(bf16[1,3584,512]{2,1,0:T(8,128)(2,1)} %param.10) | copy-start | bytes 11010052
  82.0 3.9 %collective-permute-start = (bf16[1792,512]{1,0:T(8,128)(2,1)S(1)}, bf16[1792,512]{1,0:T(8,128)(2,1)}, u32[]{:S(2)}, u32[]{:S(2)}) collective-permute-start(bf16[1792,512]{1,0:T(8,128)(2,1)S(1)} %constant_dynamic-slice_fusion), channel_id=1, source_target_pairs={{0,4},{4,0},{8,12},{12,8},{16,20},{20,16},{24,28},{28,24},{1,5},{5... | collective-permute-start | bytes 5505032 | tf_op jit(solution)/shard_map/ppermute | solution.py:13
  82.0 43.0 %collective-permute-start.4 = (bf16[1792,512]{1,0:T(8,128)(2,1)S(1)}, bf16[1792,512]{1,0:T(8,128)(2,1)}, u32[]{:S(2)}, u32[]{:S(2)}) collective-permute-start(bf16[1792,512]{1,0:T(8,128)(2,1)S(1)} %collective-permute-done.3), channel_id=1, source_target_pairs={{0,8},{4,12},{8,0},{12,4},{16,24},{20,28},{24,16},{28,20},{1,9},{5... | collective-permute-start | bytes 5505032 | tf_op jit(solution)/shard_map/ppermute | solution.py:13
  86.0 77.9 %collective-permute-start.1 = (bf16[1792,512]{1,0:T(8,128)(2,1)}, bf16[1792,512]{1,0:T(8,128)(2,1)}, u32[]{:S(2)}, u32[]{:S(2)}) collective-permute-start(bf16[1792,512]{1,0:T(8,128)(2,1)} %collective-permute-done), channel_id=1, source_target_pairs={{0,8},{4,12},{8,0},{12,4},{16,24},{20,28},{24,16},{28,20},{1,9},{5... | collective-permute-start | bytes 5505032 | tf_op jit(solution)/shard_map/ppermute | solution.py:13
  125.0 42.0 %collective-permute-start.5 = (bf16[1792,512]{1,0:T(8,128)(2,1)}, bf16[1792,512]{1,0:T(8,128)(2,1)}, u32[]{:S(2)}, u32[]{:S(2)}) collective-permute-start(bf16[1792,512]{1,0:T(8,128)(2,1)} %collective-permute-done.4), channel_id=1, source_target_pairs={{0,16},{4,20},{8,24},{12,28},{16,0},{20,4},{24,8},{28,12},{1,17},{... | collective-permute-start | bytes 5505032 | tf_op jit(solution)/shard_map/ppermute | solution.py:13
  129.2 36.3 %all-to-all-start.2 = ((bf16[4,34,3584]{2,1,0:T(8,128)(2,1)}), bf16[4,34,3584]{2,1,0:T(8,128)(2,1)S(1)}, u32[]{:S(2)}, u32[]{:S(2)}) async-start(bf16[4,34,3584]{2,1,0:T(8,128)(2,1)} %all_to_all.28), calls=%async_computation.2 | async-start | bytes 2293760 | tf_op jit(solution)/shard_map/all_to_all | solution.py:67
  163.9 41.9 %collective-permute-start.2 = (bf16[1792,512]{1,0:T(8,128)(2,1)}, bf16[1792,512]{1,0:T(8,128)(2,1)}, u32[]{:S(2)}, u32[]{:S(2)}) collective-permute-start(bf16[1792,512]{1,0:T(8,128)(2,1)} %collective-permute-done.1), channel_id=1, source_target_pairs={{0,16},{4,20},{8,24},{12,28},{16,0},{20,4},{24,8},{28,12},{1,17},{... | collective-permute-start | bytes 5505032 | tf_op jit(solution)/shard_map/ppermute | solution.py:13
  165.4 2.2 %copy-start.4 = (bf16[3584,512]{1,0:T(8,128)(2,1)S(1)}, bf16[3584,512]{1,0:T(8,128)(2,1)}, u32[]{:S(2)}) copy-start(bf16[3584,512]{1,0:T(8,128)(2,1)} %copy-done.3) | copy-start | bytes 11010052
where the time goes:
time: 210 us
  waiting for transfers between devices  157 us (75%)
  starting transfers between devices  20.2 us (10%)
  local copies, waits for them, and re-layouts  13.5 us (6%)
  matrix products  9.91 us (5%)
  other arithmetic  8.41 us (4%)
    ppermute x6, waiting for transfers between devices, partner(): return lax.ppermute(value, axis, pairs)  105 us
    all_to_all x1, waiting for transfers between devices, per_device(): lax.all_to_all(send_x, 'expert', split_axis=0, concat_axis=0, tiled=True)  27.5 us
    all_to_all x1, waiting for transfers between devices, per_device(): lax.all_to_all(send_g, 'expert', split_axis=0, concat_axis=0, tiled=True)  24.4 us
    unnamed x17, local copies, waits for them, and re-layouts  7.92 us
    all_to_all x1, starting transfers between devices, per_device(): lax.all_to_all(send_x, 'expert', split_axis=0, concat_axis=0, tiled=True)  6.35 us
    ppermute x6, starting transfers between devices, partner(): return lax.ppermute(value, axis, pairs)  6.04 us
    broadcast_in_dim x2, other arithmetic, per_device(): return (input_grad[None], grad_up[None], grad_down[None])  5.84 us
    all_to_all x1, starting transfers between devices, per_device(): lax.all_to_all(send_g, 'expert', split_axis=0, concat_axis=0, tiled=True)  4.26 us
  transfers between devices with their start and end apart: 9, of which 6 were waited for; matrix products, arithmetic and copies ran while one was open for 6% of the time, Pallas kernels for 0%

commit v1 on v0

v1 whole, which is shorter than its diff:
```python
import functools

import jax
import jax.numpy as jnp
from jax import lax
from jax.experimental import pallas as pl
from jax.experimental.pallas import tpu as pltpu
from jax.sharding import PartitionSpec as P

EXPERTS = 2
CAP = 34
FOLD = 8
MAIN = CAP // FOLD * FOLD
REM = CAP - MAIN
CHUNKS = FOLD // REM
VMEM_LIMIT = 24 * 1024 * 1024
F32 = jnp.float32
BF16 = jnp.bfloat16


def dot(a, b, dims=((1,), (0,))):
    return lax.dot_general(a, b, (dims, ((), ())), preferred_element_type=F32)


def vmem():
    return pl.BlockSpec(memory_space=pltpu.VMEM)


def smem():
    return pl.BlockSpec(memory_space=pltpu.SMEM)


def call(kernel, outs, flops, moved, name, **more):
    return functools.partial(
        pl.pallas_call,
        kernel,
        out_shape=outs,
        name=name,
        compiler_params=pltpu.CompilerParams(vmem_limit_bytes=VMEM_LIMIT),
        cost_estimate=pl.CostEstimate(flops=flops, bytes_accessed=moved, transcendentals=0),
        **more,
    )()


def route_masks(mine_ref, routes_ref):
    routes = routes_ref[...]
    tok = routes.shape[1]
    own = routes == mine_ref[0]
    own_f = jnp.where(own, 1.0, 0.0).astype(F32)
    earlier = lax.broadcasted_iota(jnp.int32, (tok, tok), 0) < lax.broadcasted_iota(jnp.int32, (tok, tok), 1)
    count_own = dot(jnp.broadcast_to(own_f, (8, tok)).astype(BF16), jnp.where(earlier, 1.0, 0.0).astype(BF16))[0:1]
    index = lax.broadcasted_iota(jnp.int32, (1, tok), 1)
    count_own = count_own.astype(jnp.int32)
    slot = jnp.where(own, count_own, index - count_own)
    rows = 2 * MAIN + 2 * FOLD
    row = lax.broadcasted_iota(jnp.int32, (rows, tok), 0)
    slot = jnp.broadcast_to(slot, (rows, tok))
    own = jnp.broadcast_to(jnp.where(own, 1, 0), (rows, tok))
    side = jnp.where(row < 2 * MAIN, row // MAIN, (row - 2 * MAIN) // FOLD)
    place = lax.rem(row, FOLD)
    hit_side = own == 1 - side
    masks = []
    for chunk in range(CHUNKS):
        folded = jnp.where(place // REM == chunk, MAIN + lax.rem(place, REM), -1)
        wanted = jnp.where(row < 2 * MAIN, lax.rem(row, MAIN), folded)
        masks.append(jnp.where(jnp.logical_and(hit_side, slot == wanted), 1.0, 0.0).astype(BF16))
    return masks


def split_rows(masks, source, own_ref, other_ref):
    width = source.shape[1] // CHUNKS
    fold_own = fold_other = None
    for chunk in range(CHUNKS):
        part = dot(masks[chunk], source[:, chunk * width:(chunk + 1) * width])
        own_ref[chunk * MAIN:(chunk + 1) * MAIN, :] = part[:MAIN].astype(BF16)
        other_ref[chunk * MAIN:(chunk + 1) * MAIN, :] = part[MAIN:2 * MAIN].astype(BF16)
        a, b = part[2 * MAIN:2 * MAIN + FOLD], part[2 * MAIN + FOLD:]
        fold_own = a if fold_own is None else fold_own + a
        fold_other = b if fold_other is None else fold_other + b
    own_ref[CHUNKS * MAIN:, :] = fold_own.astype(BF16)
    other_ref[CHUNKS * MAIN:, :] = fold_other.astype(BF16)


def route_x_kernel(mine_ref, routes_ref, tokens_ref, own_ref, other_ref):
    split_rows(route_masks(mine_ref, routes_ref), tokens_ref[...], own_ref, other_ref)


def route_g_kernel(mine_ref, routes_ref, gate_ref, cot_ref, own_ref, other_ref):
    tok = gate_ref.shape[1]
    eye = lax.broadcasted_iota(jnp.int32, (tok, tok), 0) == lax.broadcasted_iota(jnp.int32, (tok, tok), 1)
    gate = jnp.sum(jnp.where(eye, jnp.broadcast_to(gate_ref[...], (tok, tok)), 0.0), axis=1, keepdims=True)
    scaled = (gate * cot_ref[...].astype(F32)).astype(BF16)
    split_rows(route_masks(mine_ref, routes_ref), scaled, own_ref, other_ref)


def fold_pick(owners, chunk):
    shape = (owners * REM, owners * FOLD)
    row = lax.broadcasted_iota(jnp.int32, shape, 0)
    col = lax.broadcasted_iota(jnp.int32, shape, 1)
    want = row // REM * FOLD + chunk * REM + lax.rem(row, REM)
    return jnp.where(col == want, 1.0, 0.0).astype(BF16)


def join_rows(payloads, rows_ref):
    owners = len(payloads)
    folds = jnp.concatenate([ref[CHUNKS * MAIN:, :].astype(F32) for ref in payloads], axis=0).astype(BF16)
    for chunk in range(CHUNKS):
        for r, ref in enumerate(payloads):
            rows_ref[chunk, r * MAIN:(r + 1) * MAIN, :] = ref[chunk * MAIN:(chunk + 1) * MAIN, :]
        rows_ref[chunk, owners * MAIN:, :] = dot(fold_pick(owners, chunk), folds).astype(BF16)


def pre_kernel(owners, upper_ref, *refs):
    payloads, (up_ref, pre_ref, keep_ref, send_ref, rows) = refs[:owners], refs[owners:]
    join_rows(payloads, rows)
    half = CHUNKS // 2
    upper = upper_ref[0]
    keep_ref[...] = rows[pl.ds(upper * half, half)]
    send_ref[...] = rows[pl.ds((1 - upper) * half, half)]
    width = rows.shape[2]
    total = None
    for chunk in range(CHUNKS):
        part = dot(rows[chunk], up_ref[chunk * width:(chunk + 1) * width, :])
        total = part if total is None else total + part
    pre_ref[...] = total


def join_g_kernel(owners, upper_ref, *refs):
    payloads, (rows_ref, keep_ref, send_ref) = refs[:owners], refs[owners:]
    join_rows(payloads, rows_ref)
    half = CHUNKS // 2
    upper = upper_ref[0]
    keep_ref[...] = rows_ref[pl.ds(upper * half, half)]
    send_ref[...] = rows_ref[pl.ds((1 - upper) * half, half)]


def hidden_kernel(rows_ref, pre_ref, down_ref, hidden_ref):
    width = rows_ref.shape[2]
    total = None
    for chunk in range(CHUNKS):
        part = dot(rows_ref[chunk], down_ref[:, chunk * width:(chunk + 1) * width], ((1,), (1,)))
        total = part if total is None else total + part
    pre = pre_ref[...]
    sigma = 1.0 / (1.0 + jnp.exp(-pre))
    hidden_ref[0] = (total * sigma * (1.0 + pre * (1.0 - sigma))).astype(BF16)
    hidden_ref[1] = (pre * sigma).astype(BF16)


def back_kernel(owners, hidden_ref, up_ref, *outs):
    dpre = hidden_ref[0]
    width = up_ref.shape[0] // CHUNKS
    folds = None
    for chunk in range(CHUNKS):
        part = dot(dpre, up_ref[chunk * width:(chunk + 1) * width, :], ((1,), (1,))).astype(BF16)
        for r in range(owners):
            outs[r][chunk * MAIN:(chunk + 1) * MAIN, :] = part[r * MAIN:(r + 1) * MAIN]
        fold = dot(fold_pick(owners, chunk), part[owners * MAIN:], ((0,), (0,)))
        folds = fold if folds is None else folds + fold
    for r in range(owners):
        outs[r][CHUNKS * MAIN:, :] = folds[r * FOLD:(r + 1) * FOLD].astype(BF16)


def grad_kernel(hid_a, hid_b, xa, xb, ga, gb, up_ref, down_ref):
    step = pl.program_id(0)
    del step
    t = ((0,), (0,))
    up_ref[...] = (dot(xa[0], hid_a[0], t) + dot(xb[0], hid_b[0], t)).astype(BF16)
    down_ref[...] = (dot(hid_a[1], ga[0], t) + dot(hid_b[1], gb[0], t)).astype(BF16)


def final_kernel(owners, group, mine_ref, routes_ref, *refs):
    parts, out_ref = refs[:owners], refs[owners]
    masks = route_masks(mine_ref, routes_ref)
    width = out_ref.shape[1] // CHUNKS

    def sides(lo, hi):
        own = sum(ref[lo:hi, :].astype(F32) for ref in parts[:group])
        other = sum(ref[lo:hi, :].astype(F32) for ref in parts[group:])
        return [own, other]

    folds = sides(CHUNKS * MAIN, CHUNKS * MAIN + FOLD)
    for chunk in range(CHUNKS):
        rows = jnp.concatenate(sides(chunk * MAIN, (chunk + 1) * MAIN) + folds, axis=0).astype(BF16)
        out_ref[:, chunk * width:(chunk + 1) * width] = dot(masks[chunk], rows, ((0,), (0,))).astype(BF16)


def per_device(tokens, cotangent, router_gate, routes, up_weight, down_weight):
    owners = lax.axis_size("expert")
    ranks = lax.axis_size("pipe")
    group = owners // EXPERTS
    tok, model = tokens.shape[1:]
    hidden = up_weight.shape[2]
    width = model // CHUNKS
    rows = owners * CAP
    half = CHUNKS // 2
    mine = (lax.axis_index("expert") // group).astype(jnp.int32).reshape(1)
    upper = (lax.axis_index("pipe") >= ranks // 2).astype(jnp.int32).reshape(1)
    ids = routes.reshape(1, tok)
    up, down = up_weight[0], down_weight[0]

    payload = jax.ShapeDtypeStruct((CHUNKS * MAIN + FOLD, width), BF16)
    halves = jax.ShapeDtypeStruct((half, rows, width), BF16)

    def swap(value, r):
        return lax.ppermute(value, "expert", [(q, q ^ r) for q in range(owners)])

    def mirror(value):
        return lax.ppermute(value, "pipe", [(i, ranks - 1 - i) for i in range(ranks)])

    def deal(own, other):
        got = {r: swap(own if r < group else other, r) for r in reversed(range(1, owners))}
        return [own] + [got[r] for r in range(1, owners)]

    small = 1 << 20
    x_own, x_other = call(
        route_x_kernel, (payload, payload), small, small, "route_x", in_specs=[smem(), vmem(), vmem()], out_specs=(vmem(), vmem())
    )(mine, ids, tokens[0])
    x_parts = deal(x_own, x_other)
    g_own, g_other = call(
        route_g_kernel, (payload, payload), small, small, "route_g", in_specs=[smem()] + [vmem()] * 3, out_specs=(vmem(), vmem())
    )(mine, ids, router_gate, cotangent[0])
    g_parts = deal(g_own, g_other)

    flops = 2 * rows * model * hidden
    moved = 2 * model * hidden
    pre, x_keep, x_send = call(
        functools.partial(pre_kernel, owners),
        (jax.ShapeDtypeStruct((rows, hidden), F32), halves, halves),
        flops, moved, "pre",
        in_specs=[smem()] + [vmem()] * (owners + 1),
        out_specs=(vmem(),) * 3,
        scratch_shapes=[pltpu.VMEM((CHUNKS, rows, width), BF16)],
    )(upper, *x_parts, up)
    x_far = mirror(x_send)
    g_rows, g_keep, g_send = call(
        functools.partial(join_g_kernel, owners),
        (jax.ShapeDtypeStruct((CHUNKS, rows, width), BF16), halves, halves),
        small, small, "join_g",
        in_specs=[smem()] + [vmem()] * owners,
        out_specs=(vmem(),) * 3,
    )(upper, *g_parts)
    g_far = mirror(g_send)
    hid = call(
        hidden_kernel, jax.ShapeDtypeStruct((2, rows, hidden), BF16), flops, moved, "hidden", in_specs=[vmem()] * 3, out_specs=vmem()
    )(g_rows, pre, down)
    hid_far = mirror(hid)
    back = call(
        functools.partial(back_kernel, owners), (payload,) * owners, flops, moved, "back",
        in_specs=[vmem()] * 2, out_specs=(vmem(),) * owners,
    )(hid, up)
    got = {r: swap(back[r], r) for r in reversed(range(1, owners))}
    back_parts = [back[0]] + [got[r] for r in range(1, owners)]

    whole = pl.BlockSpec((2, rows, hidden), lambda k: (0, 0, 0))
    chunk = pl.BlockSpec((1, rows, width), lambda k: (k, 0, 0))
    grad_up, grad_down = call(
        grad_kernel,
        (jax.ShapeDtypeStruct((model // 2, hidden), BF16), jax.ShapeDtypeStruct((hidden, model // 2), BF16)),
        2 * flops, moved, "grad",
        grid=(half,),
        in_specs=[whole, whole] + [chunk] * 4,
        out_specs=(pl.BlockSpec((width, hidden), lambda k: (k, 0)), pl.BlockSpec((hidden, width), lambda k: (0, k))),
    )(hid, hid_far, x_keep, x_far, g_keep, g_far)
    input_grad = call(
        functools.partial(final_kernel, owners, group), jax.ShapeDtypeStruct((tok, model), BF16), small, small, "final",
        in_specs=[smem()] + [vmem()] * (owners + 1), out_specs=vmem(),
    )(mine, ids, *back_parts)
    return (input_grad[None], grad_up[None], grad_down[None])


def solution(mesh):
    placed = (
        P("pipe", "expert", None),
        P("pipe", "expert", None),
        P("pipe", "expert"),
        P("pipe", "expert", None),
        P("pipe", None, "expert"),
        P("pipe", "expert", None),
    )
    return jax.shard_map(
        per_device,
        mesh=mesh,
        in_specs=placed,
        out_specs=(P("pipe", "expert", None), P("pipe", None, "expert"), P("pipe", "expert", None)),
        check_vma=False,
    )
```

time: 210 us -> 93.6 us (0.45)
  waiting for transfers between devices: 157 us -> 50.2 us
  matrix products: 9.91 us -> 0 us
  Pallas kernels: 0 us -> 9.77 us
  other arithmetic: 8.41 us -> 0 us
  local copies, waits for them, and re-layouts: 13.5 us -> 6.51 us
  starting transfers between devices: 20.2 us -> 26.1 us
    ppermute x6 -> x12, waiting for transfers between devices: 105 us -> 50.2 us  [the longest x9 43.8 us: swap(): return lax.ppermute(value, 'expert', [(q, q ^ r) for q in range(owners)])]
    all_to_all x3 -> x0, waiting for transfers between devices: 51.9 us -> none  [the longest x1 27.5 us: per_device(): lax.all_to_all(send_x, 'expert', split_axis=0, concat_axis=0, tiled=True)]
    ppermute x6 -> x12, starting transfers between devices: 6.04 us -> 26.1 us  [the longest x9 22.9 us: swap(): return lax.ppermute(value, 'expert', [(q, q ^ r) for q in range(owners)])]
    all_to_all x3 -> x0, starting transfers between devices: 14.1 us -> none  [the longest x1 6.35 us: per_device(): lax.all_to_all(send_x, 'expert', split_axis=0, concat_axis=0, tiled=True)]
    dot_general x8 -> x0, matrix products: 9.91 us -> none  [the longest x1 2.71 us: per_device(): pre = jnp.dot(rows_x, up_local, preferred_element_type=jnp.float32)]
    pallas_call x0 -> x8, Pallas kernels: none -> 9.77 us  [the longest x1 3.44 us: per_device(): call(grad_kernel, (jax.ShapeDtypeStruct((model // 2, hidden), BF16), jax....]
    broadcast_in_dim x2 -> x0, other arithmetic: 5.84 us -> none  [per_device(): return (input_grad[None], grad_up[None], grad_down[None])]
    all_to_all x3 -> x0, local copies, waits for them, and re-layouts: 3.11 us -> none  [the longest x1 1.54 us: per_device(): lax.all_to_all(send_g, 'expert', split_axis=0, concat_axis=0, tiled=True)]
  transfers between devices with their start and end apart: 9 -> 12, of which waited for: 6 -> 7; matrix products, arithmetic and copies ran while one was open for 6% -> 0% of each run, Pallas kernels for 0% -> 2%
where the time goes in v1:
time: 93.6 us; the launch traced here: 93.3 us
  waiting for transfers between devices  50.2 us (54%)
  starting transfers between devices  26.1 us (28%)
  Pallas kernels  9.77 us (10%)
  local copies, waits for them, and re-layouts  6.51 us (7%)
    ppermute x9, waiting for transfers between devices, swap(): return lax.ppermute(value, 'expert', [(q, q ^ r) for q in range(owners)])  43.8 us
    ppermute x9, starting transfers between devices, swap(): return lax.ppermute(value, 'expert', [(q, q ^ r) for q in range(owners)])  22.9 us
    unnamed x16, local copies, waits for them, and re-layouts  6.51 us
    ppermute x3, waiting for transfers between devices, mirror(): lax.ppermute(value, 'pipe', [(i, ranks - 1 - i) for i in range(ranks)])  6.46 us
    pallas_call x1, Pallas kernels, per_device(): call(grad_kernel, (jax.ShapeDtypeStruct((model // 2, hidden), BF16), jax....  3.44 us
    ppermute x3, starting transfers between devices, mirror(): lax.ppermute(value, 'pipe', [(i, ranks - 1 - i) for i in range(ranks)])  3.16 us
  transfers between devices with their start and end apart: 12, of which 7 were waited for; matrix products, arithmetic and copies ran while one was open for 0% of the time, Pallas kernels for 2%

profile of v1, /device:TPU:0, one launch (start us, length us, event | category | flops | bytes accessed | tf_op | source)
XLA Modules:
  0.0 93.3 jit_solution(14995776784369420691)
XLA Ops:
  0.6 0.0 copy-start.4
  0.7 1.0 %copy-done.4 = bf16[1,64,3584]{2,1,0:T(8,128)(2,1)S(1)} copy-done((bf16[1,64,3584]{2,1,0:T(8,128)(2,1)S(1)}, bf16[1,64,3584]{2,1,0:T(8,128)(2,1)}, u32[]{:S(2)}) %copy-start.4) | copy-done | bytes 458776
  1.7 0.0 copy-start.5
  1.7 0.7 copy-done.5
  2.3 0.0 copy-start.7
  2.3 0.7 copy-done.7
  3.0 0.4 route_g.1
  3.4 3.1 %collective-permute-start = (bf16[136,896]{1,0:T(8,128)(2,1)S(1)}, bf16[136,896]{1,0:T(8,128)(2,1)S(1)}, u32[]{:S(2)}, u32[]{:S(2)}) collective-permute-start(bf16[136,896]{1,0:T(8,128)(2,1)S(1)} %get-tuple-element.19.refs_0_), channel_id=1, source_target_pairs={{0,1},{1,0},{2,3},{3,2},{4,5},{5,4},{6,7},{7,6},{8,9},{9,8},{10,11... | collective-permute-start | bytes 731144 | tf_op jit(solution)/shard_map/ppermute | solution.py:205
  6.5 2.6 %collective-permute-start.1 = (bf16[136,896]{1,0:T(8,128)(2,1)S(1)}, bf16[136,896]{1,0:T(8,128)(2,1)S(1)}, u32[]{:S(2)}, u32[]{:S(2)}) collective-permute-start(bf16[136,896]{1,0:T(8,128)(2,1)S(1)} %get-tuple-element.20), channel_id=1, source_target_pairs={{0,2},{1,3},{2,0},{3,1},{4,6},{5,7},{6,4},{7,5},{8,10},{9,11},{10,... | collective-permute-start | bytes 731144 | tf_op jit(solution)/shard_map/ppermute | solution.py:205
  9.1 0.0 collective-permute-start.2
  9.1 0.0 copy-start.3
  9.1 1.0 %copy-done.3 = bf16[1,64,3584]{2,1,0:T(8,128)(2,1)S(1)} copy-done((bf16[1,64,3584]{2,1,0:T(8,128)(2,1)S(1)}, bf16[1,64,3584]{2,1,0:T(8,128)(2,1)}, u32[]{:S(2)}) %copy-start.3) | copy-done | bytes 458776
  10.1 0.4 route_x.1
  10.6 1.0 %collective-permute-start.3 = (bf16[136,896]{1,0:T(8,128)(2,1)S(1)}, bf16[136,896]{1,0:T(8,128)(2,1)S(1)}, u32[]{:S(2)}, u32[]{:S(2)}) collective-permute-start(bf16[136,896]{1,0:T(8,128)(2,1)S(1)} %get-tuple-element.22.refs_0_), channel_id=1, source_target_pairs={{0,1},{1,0},{2,3},{3,2},{4,5},{5,4},{6,7},{7,6},{8,9},{9,8},{10,11... | collective-permute-start | bytes 731144 | tf_op jit(solution)/shard_map/ppermute | solution.py:205
  11.5 3.5 %collective-permute-start.4 = (bf16[136,896]{1,0:T(8,128)(2,1)S(1)}, bf16[136,896]{1,0:T(8,128)(2,1)S(1)}, u32[]{:S(2)}, u32[]{:S(2)}) collective-permute-start(bf16[136,896]{1,0:T(8,128)(2,1)S(1)} %get-tuple-element.23), channel_id=1, source_target_pairs={{0,2},{1,3},{2,0},{3,1},{4,6},{5,7},{6,4},{7,5},{8,10},{9,11},{10,... | collective-permute-start | bytes 731144 | tf_op jit(solution)/shard_map/ppermute | solution.py:205
  15.0 2.7 %collective-permute-done.refs_1_ = bf16[136,896]{1,0:T(8,128)(2,1)S(1)} collective-permute-done((bf16[136,896]{1,0:T(8,128)(2,1)S(1)}, bf16[136,896]{1,0:T(8,128)(2,1)S(1)}, u32[]{:S(2)}, u32[]{:S(2)}) %collective-permute-start) | collective-permute-done | bytes 243744 | tf_op jit(solution)/shard_map/ppermute | solution.py:205
  17.8 4.5 %collective-permute-start.5 = (bf16[136,896]{1,0:T(8,128)(2,1)S(1)}, bf16[136,896]{1,0:T(8,128)(2,1)S(1)}, u32[]{:S(2)}, u32[]{:S(2)}) collective-permute-start(bf16[136,896]{1,0:T(8,128)(2,1)S(1)} %get-tuple-element.23), channel_id=1, source_target_pairs={{0,3},{1,2},{2,1},{3,0},{4,7},{5,6},{6,5},{7,4},{8,11},{9,10},{10,... | collective-permute-start | bytes 731144 | tf_op jit(solution)/shard_map/ppermute | solution.py:205
  22.3 4.4 %collective-permute-done.1.refs_2_ = bf16[136,896]{1,0:T(8,128)(2,1)S(1)} collective-permute-done((bf16[136,896]{1,0:T(8,128)(2,1)S(1)}, bf16[136,896]{1,0:T(8,128)(2,1)S(1)}, u32[]{:S(2)}, u32[]{:S(2)}) %collective-permute-start.1) | collective-permute-done | bytes 243744 | tf_op jit(solution)/shard_map/ppermute | solution.py:205
  26.7 0.0 collective-permute-done.2.refs_3_
  26.7 0.2 join_g.1
  26.9 1.6 %collective-permute-done.3.refs_1_ = bf16[136,896]{1,0:T(8,128)(2,1)S(1)} collective-permute-done((bf16[136,896]{1,0:T(8,128)(2,1)S(1)}, bf16[136,896]{1,0:T(8,128)(2,1)S(1)}, u32[]{:S(2)}, u32[]{:S(2)}) %collective-permute-start.3) | collective-permute-done | bytes 243744 | tf_op jit(solution)/shard_map/ppermute | solution.py:205
  28.6 19.0 %collective-permute-done.4.refs_2_ = bf16[136,896]{1,0:T(8,128)(2,1)S(1)} collective-permute-done((bf16[136,896]{1,0:T(8,128)(2,1)S(1)}, bf16[136,896]{1,0:T(8,128)(2,1)S(1)}, u32[]{:S(2)}, u32[]{:S(2)}) %collective-permute-start.4) | collective-permute-done | bytes 243744 | tf_op jit(solution)/shard_map/ppermute | solution.py:205
  47.6 0.0 collective-permute-done.5.refs_3_
  47.6 0.0 copy-start
  47.6 2.0 %copy-done = bf16[1,3584,512]{2,1,0:T(8,128)(2,1)S(1)} copy-done((bf16[1,3584,512]{2,1,0:T(8,128)(2,1)S(1)}, bf16[1,3584,512]{2,1,0:T(8,128)(2,1)}, u32[]{:S(2)}) %copy-start) | copy-done | bytes 3670040
  49.6 0.0 copy-start.2
  49.6 0.9 pre.1
  50.6 0.0 copy-start.1
  50.6 1.1 %copy-done.2 = bf16[1,512,3584]{2,1,0:T(8,128)(2,1)S(1)} copy-done((bf16[1,512,3584]{2,1,0:T(8,128)(2,1)S(1)}, bf16[1,512,3584]{2,1,0:T(8,128)(2,1)}, u32[]{:S(2)}) %copy-start.2) | copy-done | bytes 3670040
  51.7 0.0 copy-start.6
  51.7 1.3 %hidden.1.hidden_ref.hid_a = bf16[2,136,512]{2,1,0:T(8,128)(2,1)S(1)} custom-call(bf16[4,136,896]{2,1,0:T(8,128)(2,1)S(1)} %get-tuple-element.21.rows_ref, f32[136,512]{1,0:T(8,128)S(1)} %get-tuple-element.24.pre_ref, bf16[512,3584]{1,0:T(8,128)(2,1)S(1)} %bitcast.12), custom_call_target="tpu_custom_call" | custom-call | flops 499122176 | bytes 3670016 | tf_op jit(solution)/shard_map/hidden/pallas_call | solution.py:243
  53.0 0.0 copy-done.1
  53.0 1.8 %back.1 = (bf16[136,896]{1,0:T(8,128)(2,1)S(1)}, bf16[136,896]{1,0:T(8,128)(2,1)S(1)}, bf16[136,896]{1,0:T(8,128)(2,1)S(1)}, bf16[136,896]{1,0:T(8,128)(2,1)S(1)}) custom-call(bf16[2,136,512]{2,1,0:T(8,128)(2,1)S(1)} %hidden.1.hidden_ref.hid_a, bf16[3584,512]{1,0:T(8,128)(2,1)S(1)} %bitcast.11), custom_call_target="tpu_custom_call" | custom-call | flops 499122176 | bytes 3670016 | tf_op jit(solution)/shard_map/back/pallas_call | solution.py:247
  54.8 4.4 %collective-permute-start.6 = (bf16[136,896]{1,0:T(8,128)(2,1)S(1)}, bf16[136,896]{1,0:T(8,128)(2,1)S(1)}, u32[]{:S(2)}, u32[]{:S(2)}) collective-permute-start(bf16[136,896]{1,0:T(8,128)(2,1)S(1)} %get-tuple-element.26), channel_id=1, source_target_pairs={{0,1},{1,0},{2,3},{3,2},{4,5},{5,4},{6,7},{7,6},{8,9},{9,8},{10,11... | collective-permute-start | bytes 731144 | tf_op jit(solution)/shard_map/ppermute | solution.py:205
  59.2 0.5 collective-permute-start.10
  59.7 2.1 %collective-permute-start.11 = (bf16[2,136,896]{2,1,0:T(8,128)(2,1)S(1)}, bf16[2,136,896]{2,1,0:T(8,128)(2,1)S(1)}, u32[]{:S(2)}, u32[]{:S(2)}) collective-permute-start(bf16[2,136,896]{2,1,0:T(8,128)(2,1)S(1)} %get-tuple-element.32), channel_id=1, source_target_pairs={{0,28},{4,24},{8,20},{12,16},{16,12},{20,8},{24,4},{28,0},{1,29},{... | collective-permute-start | bytes 1462280 | tf_op jit(solution)/shard_map/ppermute | solution.py:208
  61.9 0.5 collective-permute-start.9
  62.4 1.3 %collective-permute-start.7 = (bf16[136,896]{1,0:T(8,128)(2,1)S(1)}, bf16[136,896]{1,0:T(8,128)(2,1)S(1)}, u32[]{:S(2)}, u32[]{:S(2)}) collective-permute-start(bf16[136,896]{1,0:T(8,128)(2,1)S(1)} %get-tuple-element.27), channel_id=1, source_target_pairs={{0,2},{1,3},{2,0},{3,1},{4,6},{5,7},{6,4},{7,5},{8,10},{9,11},{10,... | collective-permute-start | bytes 731144 | tf_op jit(solution)/shard_map/ppermute | solution.py:205
  63.7 0.3 collective-permute-done.6.refs_1_
  64.0 2.5 %collective-permute-start.8 = (bf16[136,896]{1,0:T(8,128)(2,1)S(1)}, bf16[136,896]{1,0:T(8,128)(2,1)S(1)}, u32[]{:S(2)}, u32[]{:S(2)}) collective-permute-start(bf16[136,896]{1,0:T(8,128)(2,1)S(1)} %get-tuple-element.28), channel_id=1, source_target_pairs={{0,3},{1,2},{2,1},{3,0},{4,7},{5,6},{6,5},{7,4},{8,11},{9,10},{10,... | collective-permute-start | bytes 731144 | tf_op jit(solution)/shard_map/ppermute | solution.py:205
  66.5 15.7 %collective-permute-done.7.refs_2_ = bf16[136,896]{1,0:T(8,128)(2,1)S(1)} collective-permute-done((bf16[136,896]{1,0:T(8,128)(2,1)S(1)}, bf16[136,896]{1,0:T(8,128)(2,1)S(1)}, u32[]{:S(2)}, u32[]{:S(2)}) %collective-permute-start.7) | collective-permute-done | bytes 243744 | tf_op jit(solution)/shard_map/ppermute | solution.py:205
  82.2 0.0 collective-permute-done.8.refs_3_
  82.2 0.0 copy-done.6
  82.2 1.2 %final.1 = bf16[64,3584]{1,0:T(8,128)(2,1)} custom-call(s32[1]{0:T(128)} %bitcast.mine_ref, s32[1,64]{1,0:T(1,128)S(1)} %bitcast.17, bf16[136,896]{1,0:T(8,128)(2,1)S(1)} %get-tuple-element.25.refs_0_, bf16[136,896]{1,0:T(8,128)(2,1)S(1)} %collective-permute-done.6.refs_1_, bf16[136,896]{1,0:T(8,128)(2,1)S(1)} %collective-permute-done.7.refs_2_, ...), custom_call_target="tpu_custom_call" | custom-call | flops 1048576 | bytes 1048576 | tf_op jit(solution)/shard_map/final/pallas_call | solution.py:264
  83.4 6.5 %collective-permute-done.9.hid_b = bf16[2,136,512]{2,1,0:T(8,128)(2,1)S(1)} collective-permute-done((bf16[2,136,512]{2,1,0:T(8,128)(2,1)S(1)}, bf16[2,136,512]{2,1,0:T(8,128)(2,1)S(1)}, u32[]{:S(2)}, u32[]{:S(2)}) %collective-permute-start.9) | collective-permute-done | bytes 278560 | tf_op jit(solution)/shard_map/ppermute | solution.py:208
  89.9 0.0 collective-permute-done.10.xb
  89.9 0.0 collective-permute-done.11.gb
  89.9 3.4 %grad.1 = (bf16[1792,512]{1,0:T(8,128)(2,1)}, bf16[512,1792]{1,0:T(8,128)(2,1)}) custom-call(bf16[2,136,512]{2,1,0:T(8,128)(2,1)S(1)} %hidden.1.hidden_ref.hid_a, bf16[2,136,512]{2,1,0:T(8,128)(2,1)S(1)} %collective-permute-done.9.hid_b, bf16[2,136,896]{2,1,0:T(8,128)(2,1)S(1)} %get-tuple-element.29.xa, bf16[2,136,896]{2,1,0:T(8,128)(2,1)S(1)} %collective-permute-done.10.xb, ...), custom_call_target="tpu_custom_call" | custom-call | flops 998244352 | bytes 3670016 | tf_op jit(solution)/shard_map/grad/pallas_call | solution.py:256
Async XLA Ops:
  0.6 1.0 %copy-start.4 = (bf16[1,64,3584]{2,1,0:T(8,128)(2,1)S(1)}, bf16[1,64,3584]{2,1,0:T(8,128)(2,1)}, u32[]{:S(2)}) copy-start(bf16[1,64,3584]{2,1,0:T(8,128)(2,1)} %param.7) | copy-start | bytes 1376260
  1.7 0.7 copy-start.5
  2.3 0.7 copy-start.7
  3.4 14.4 %collective-permute-start = (bf16[136,896]{1,0:T(8,128)(2,1)S(1)}, bf16[136,896]{1,0:T(8,128)(2,1)S(1)}, u32[]{:S(2)}, u32[]{:S(2)}) collective-permute-start(bf16[136,896]{1,0:T(8,128)(2,1)S(1)} %get-tuple-element.19.refs_0_), channel_id=1, source_target_pairs={{0,1},{1,0},{2,3},{3,2},{4,5},{5,4},{6,7},{7,6},{8,9},{9,8},{10,11... | collective-permute-start | bytes 731144 | tf_op jit(solution)/shard_map/ppermute | solution.py:205
  6.5 20.2 %collective-permute-start.1 = (bf16[136,896]{1,0:T(8,128)(2,1)S(1)}, bf16[136,896]{1,0:T(8,128)(2,1)S(1)}, u32[]{:S(2)}, u32[]{:S(2)}) collective-permute-start(bf16[136,896]{1,0:T(8,128)(2,1)S(1)} %get-tuple-element.20), channel_id=1, source_target_pairs={{0,2},{1,3},{2,0},{3,1},{4,6},{5,7},{6,4},{7,5},{8,10},{9,11},{10,... | collective-permute-start | bytes 731144 | tf_op jit(solution)/shard_map/ppermute | solution.py:205
  9.1 17.6 %collective-permute-start.2 = (bf16[136,896]{1,0:T(8,128)(2,1)S(1)}, bf16[136,896]{1,0:T(8,128)(2,1)S(1)}, u32[]{:S(2)}, u32[]{:S(2)}) collective-permute-start(bf16[136,896]{1,0:T(8,128)(2,1)S(1)} %get-tuple-element.20), channel_id=1, source_target_pairs={{0,3},{1,2},{2,1},{3,0},{4,7},{5,6},{6,5},{7,4},{8,11},{9,10},{10,... | collective-permute-start | bytes 731144 | tf_op jit(solution)/shard_map/ppermute | solution.py:205
  9.1 1.0 %copy-start.3 = (bf16[1,64,3584]{2,1,0:T(8,128)(2,1)S(1)}, bf16[1,64,3584]{2,1,0:T(8,128)(2,1)}, u32[]{:S(2)}) copy-start(bf16[1,64,3584]{2,1,0:T(8,128)(2,1)} %param.6) | copy-start | bytes 1376260
  10.6 18.0 %collective-permute-start.3 = (bf16[136,896]{1,0:T(8,128)(2,1)S(1)}, bf16[136,896]{1,0:T(8,128)(2,1)S(1)}, u32[]{:S(2)}, u32[]{:S(2)}) collective-permute-start(bf16[136,896]{1,0:T(8,128)(2,1)S(1)} %get-tuple-element.22.refs_0_), channel_id=1, source_target_pairs={{0,1},{1,0},{2,3},{3,2},{4,5},{5,4},{6,7},{7,6},{8,9},{9,8},{10,11... | collective-permute-start | bytes 731144 | tf_op jit(solution)/shard_map/ppermute | solution.py:205
  11.5 36.0 %collective-permute-start.4 = (bf16[136,896]{1,0:T(8,128)(2,1)S(1)}, bf16[136,896]{1,0:T(8,128)(2,1)S(1)}, u32[]{:S(2)}, u32[]{:S(2)}) collective-permute-start(bf16[136,896]{1,0:T(8,128)(2,1)S(1)} %get-tuple-element.23), channel_id=1, source_target_pairs={{0,2},{1,3},{2,0},{3,1},{4,6},{5,7},{6,4},{7,5},{8,10},{9,11},{10,... | collective-permute-start | bytes 731144 | tf_op jit(solution)/shard_map/ppermute | solution.py:205
  17.8 29.8 %collective-permute-start.5 = (bf16[136,896]{1,0:T(8,128)(2,1)S(1)}, bf16[136,896]{1,0:T(8,128)(2,1)S(1)}, u32[]{:S(2)}, u32[]{:S(2)}) collective-permute-start(bf16[136,896]{1,0:T(8,128)(2,1)S(1)} %get-tuple-element.23), channel_id=1, source_target_pairs={{0,3},{1,2},{2,1},{3,0},{4,7},{5,6},{6,5},{7,4},{8,11},{9,10},{10,... | collective-permute-start | bytes 731144 | tf_op jit(solution)/shard_map/ppermute | solution.py:205
  47.6 2.0 %copy-start = (bf16[1,3584,512]{2,1,0:T(8,128)(2,1)S(1)}, bf16[1,3584,512]{2,1,0:T(8,128)(2,1)}, u32[]{:S(2)}) copy-start(bf16[1,3584,512]{2,1,0:T(8,128)(2,1)} %param.10) | copy-start | bytes 11010052
  49.6 2.0 %copy-start.2 = (bf16[1,512,3584]{2,1,0:T(8,128)(2,1)S(1)}, bf16[1,512,3584]{2,1,0:T(8,128)(2,1)}, u32[]{:S(2)}) copy-start(bf16[1,512,3584]{2,1,0:T(8,128)(2,1)} %param.11) | copy-start | bytes 11010052
  50.6 2.5 %copy-start.1 = (bf16[1,3584,512]{2,1,0:T(8,128)(2,1)S(1)}, bf16[1,3584,512]{2,1,0:T(8,128)(2,1)}, u32[]{:S(2)}) copy-start(bf16[1,3584,512]{2,1,0:T(8,128)(2,1)} %param.10) | copy-start | bytes 11010052
  51.7 30.5 %copy-start.6 = (s32[1,64,1]{1,2,0:T(1,128)S(1)}, s32[1,64,1]{1,2,0:T(1,128)}, u32[]{:S(2)}) copy-start(s32[1,64,1]{1,2,0:T(1,128)} %param.9) | copy-start | bytes 772
  54.8 9.2 %collective-permute-start.6 = (bf16[136,896]{1,0:T(8,128)(2,1)S(1)}, bf16[136,896]{1,0:T(8,128)(2,1)S(1)}, u32[]{:S(2)}, u32[]{:S(2)}) collective-permute-start(bf16[136,896]{1,0:T(8,128)(2,1)S(1)} %get-tuple-element.26), channel_id=1, source_target_pairs={{0,1},{1,0},{2,3},{3,2},{4,5},{5,4},{6,7},{7,6},{8,9},{9,8},{10,11... | collective-permute-start | bytes 731144 | tf_op jit(solution)/shard_map/ppermute | solution.py:205
  59.2 30.7 %collective-permute-start.10 = (bf16[2,136,896]{2,1,0:T(8,128)(2,1)S(1)}, bf16[2,136,896]{2,1,0:T(8,128)(2,1)S(1)}, u32[]{:S(2)}, u32[]{:S(2)}) collective-permute-start(bf16[2,136,896]{2,1,0:T(8,128)(2,1)S(1)} %get-tuple-element.30), channel_id=1, source_target_pairs={{0,28},{4,24},{8,20},{12,16},{16,12},{20,8},{24,4},{28,0},{1,29},{... | collective-permute-start | bytes 1462280 | tf_op jit(solution)/shard_map/ppermute | solution.py:208
  59.7 30.1 %collective-permute-start.11 = (bf16[2,136,896]{2,1,0:T(8,128)(2,1)S(1)}, bf16[2,136,896]{2,1,0:T(8,128)(2,1)S(1)}, u32[]{:S(2)}, u32[]{:S(2)}) collective-permute-start(bf16[2,136,896]{2,1,0:T(8,128)(2,1)S(1)} %get-tuple-element.32), channel_id=1, source_target_pairs={{0,28},{4,24},{8,20},{12,16},{16,12},{20,8},{24,4},{28,0},{1,29},{... | collective-permute-start | bytes 1462280 | tf_op jit(solution)/shard_map/ppermute | solution.py:208
  61.9 28.0 %collective-permute-start.9 = (bf16[2,136,512]{2,1,0:T(8,128)(2,1)S(1)}, bf16[2,136,512]{2,1,0:T(8,128)(2,1)S(1)}, u32[]{:S(2)}, u32[]{:S(2)}) collective-permute-start(bf16[2,136,512]{2,1,0:T(8,128)(2,1)S(1)} %hidden.1.hidden_ref.hid_a), channel_id=1, source_target_pairs={{0,28},{4,24},{8,20},{12,16},{16,12},{20,8},{24,4},{28,0},{1,29},{... | collective-permute-start | bytes 835592 | tf_op jit(solution)/shard_map/ppermute | solution.py:208
  62.4 19.8 %collective-permute-start.7 = (bf16[136,896]{1,0:T(8,128)(2,1)S(1)}, bf16[136,896]{1,0:T(8,128)(2,1)S(1)}, u32[]{:S(2)}, u32[]{:S(2)}) collective-permute-start(bf16[136,896]{1,0:T(8,128)(2,1)S(1)} %get-tuple-element.27), channel_id=1, source_target_pairs={{0,2},{1,3},{2,0},{3,1},{4,6},{5,7},{6,4},{7,5},{8,10},{9,11},{10,... | collective-permute-start | bytes 731144 | tf_op jit(solution)/shard_map/ppermute | solution.py:205
  64.0 18.2 %collective-permute-start.8 = (bf16[136,896]{1,0:T(8,128)(2,1)S(1)}, bf16[136,896]{1,0:T(8,128)(2,1)S(1)}, u32[]{:S(2)}, u32[]{:S(2)}) collective-permute-start(bf16[136,896]{1,0:T(8,128)(2,1)S(1)} %get-tuple-element.28), channel_id=1, source_target_pairs={{0,3},{1,2},{2,1},{3,0},{4,7},{5,6},{6,5},{7,4},{8,11},{9,10},{10,... | collective-permute-start | bytes 731144 | tf_op jit(solution)/shard_map/ppermute | solution.py:205

commit v2 on v1

v2 whole, which is shorter than its diff:
```python
import functools

import jax
import jax.numpy as jnp
from jax import lax
from jax.experimental import pallas as pl
from jax.experimental.pallas import tpu as pltpu
from jax.sharding import PartitionSpec as P


EXPERTS = 2
CAP = 34
FOLD = 8
MAIN = CAP // FOLD * FOLD
REM = CAP - MAIN
CHUNKS = FOLD // REM
LINE = 4
VMEM_LIMIT = 24 * 1024 * 1024
F32 = jnp.float32
BF16 = jnp.bfloat16


def dot(a, b, dims=((1,), (0,))):
    return lax.dot_general(a, b, (dims, ((), ())), preferred_element_type=F32)


def vmem():
    return pl.BlockSpec(memory_space=pltpu.VMEM)


def smem():
    return pl.BlockSpec(memory_space=pltpu.SMEM)


def in_hbm(value):
    return pltpu.with_memory_space_constraint(value, pltpu.HBM)


def call(kernel, outs, flops, moved, **more):
    return pl.pallas_call(
        kernel,
        out_shape=outs,
        compiler_params=pltpu.CompilerParams(vmem_limit_bytes=VMEM_LIMIT),
        cost_estimate=pl.CostEstimate(flops=flops, bytes_accessed=moved, transcendentals=0),
        **more,
    )


def route_masks(mine_ref, routes_ref):
    routes = routes_ref[...]
    tok = routes.shape[1]
    own = routes == mine_ref[0]
    own_f = jnp.where(own, 1.0, 0.0).astype(F32)
    earlier = lax.broadcasted_iota(jnp.int32, (tok, tok), 0) < lax.broadcasted_iota(jnp.int32, (tok, tok), 1)
    count_own = dot(jnp.broadcast_to(own_f, (8, tok)).astype(BF16), jnp.where(earlier, 1.0, 0.0).astype(BF16))[0:1]
    index = lax.broadcasted_iota(jnp.int32, (1, tok), 1)
    count_own = count_own.astype(jnp.int32)
    slot = jnp.where(own, count_own, index - count_own)
    rows = 2 * MAIN + 2 * FOLD
    row = lax.broadcasted_iota(jnp.int32, (rows, tok), 0)
    slot = jnp.broadcast_to(slot, (rows, tok))
    own = jnp.broadcast_to(jnp.where(own, 1, 0), (rows, tok))
    side = jnp.where(row < 2 * MAIN, row // MAIN, (row - 2 * MAIN) // FOLD)
    place = lax.rem(row, FOLD)
    hit_side = own == 1 - side
    masks = []
    for chunk in range(CHUNKS):
        folded = jnp.where(place // REM == chunk, MAIN + lax.rem(place, REM), -1)
        wanted = jnp.where(row < 2 * MAIN, lax.rem(row, MAIN), folded)
        masks.append(jnp.where(jnp.logical_and(hit_side, slot == wanted), 1.0, 0.0).astype(BF16))
    return masks


def split_rows(masks, source, own_ref, other_ref):
    width = source.shape[1] // CHUNKS
    fold_own = fold_other = None
    for chunk in range(CHUNKS):
        part = dot(masks[chunk], source[:, chunk * width:(chunk + 1) * width])
        own_ref[chunk * MAIN:(chunk + 1) * MAIN, :] = part[:MAIN].astype(BF16)
        other_ref[chunk * MAIN:(chunk + 1) * MAIN, :] = part[MAIN:2 * MAIN].astype(BF16)
        a, b = part[2 * MAIN:2 * MAIN + FOLD], part[2 * MAIN + FOLD:]
        fold_own = a if fold_own is None else fold_own + a
        fold_other = b if fold_other is None else fold_other + b
    own_ref[CHUNKS * MAIN:, :] = fold_own.astype(BF16)
    other_ref[CHUNKS * MAIN:, :] = fold_other.astype(BF16)


def hbm():
    return pl.BlockSpec(memory_space=pltpu.HBM)


def route_kernel(mine_ref, ids_hbm, gate_hbm, tokens_hbm, cot_hbm, x_own, x_other, g_own, g_other, ids, gate, tokens, cot, sems):
    copies = [
        pltpu.make_async_copy(src, dst, sems.at[i])
        for i, (src, dst) in enumerate([(ids_hbm, ids), (tokens_hbm, tokens), (gate_hbm, gate), (cot_hbm, cot)])
    ]
    for copy in copies:
        copy.start()
    copies[0].wait()
    masks = route_masks(mine_ref, ids)
    copies[1].wait()
    split_rows(masks, tokens[...], x_own, x_other)
    tok = gate.shape[1]
    eye = lax.broadcasted_iota(jnp.int32, (tok, tok), 0) == lax.broadcasted_iota(jnp.int32, (tok, tok), 1)
    copies[2].wait()
    column = jnp.sum(jnp.where(eye, jnp.broadcast_to(gate[...], (tok, tok)), 0.0), axis=1, keepdims=True)
    copies[3].wait()
    scaled = (column * cot[...].astype(F32)).astype(BF16)
    split_rows(masks, scaled, g_own, g_other)


def fold_rows(count):
    return -(-count * REM // FOLD) * FOLD


def row_count(count):
    return count * MAIN + fold_rows(count)


def fold_pick(count, chunk):
    shape = (fold_rows(count), count * FOLD)
    row = lax.broadcasted_iota(jnp.int32, shape, 0)
    col = lax.broadcasted_iota(jnp.int32, shape, 1)
    want = row // REM * FOLD + chunk * REM + lax.rem(row, REM)
    return jnp.where(col == want, 1.0, 0.0).astype(BF16)


def join_rows(payloads, rows_ref, base=0):
    count = len(payloads)
    folds = jnp.concatenate([ref[CHUNKS * MAIN:, :].astype(F32) for ref in payloads], axis=0).astype(BF16)
    last = base + count * MAIN
    for chunk in range(CHUNKS):
        for r, ref in enumerate(payloads):
            rows_ref[chunk, base + r * MAIN:base + (r + 1) * MAIN, :] = ref[chunk * MAIN:(chunk + 1) * MAIN, :]
        rows_ref[chunk, last:last + fold_rows(count), :] = dot(fold_pick(count, chunk), folds).astype(BF16)


def pre_kernel(sizes, upper_ref, *refs):
    count = sum(sizes)
    payloads, (up_hbm, down_hbm, pre_ref, keep_ref, send_ref, up_ref, down_ref, rows, sems) = refs[:count], refs[count:]
    load_up = pltpu.make_async_copy(up_hbm, up_ref, sems.at[0])
    load_down = pltpu.make_async_copy(down_hbm, down_ref, sems.at[1])
    load_up.start()
    load_down.start()
    base = first = 0
    for size in sizes:
        join_rows(payloads[first:first + size], rows, base)
        first, base = first + size, base + row_count(size)
    half = CHUNKS // 2
    upper = upper_ref[0]
    keep_ref[...] = rows[pl.ds(upper * half, half)]
    send_ref[...] = rows[pl.ds((1 - upper) * half, half)]
    width = rows.shape[2]
    load_up.wait()
    total = None
    for chunk in range(CHUNKS):
        part = dot(rows[chunk], up_ref[chunk * width:(chunk + 1) * width, :])
        total = part if total is None else total + part
    pre_ref[...] = total
    load_down.wait()


def group_kernel(size, base, upper_ref, *refs):
    payloads, (pre_ref, up_ref, down_ref, keep_ref, send_ref) = refs[:size], refs[size:size + 5]
    outs, rows = refs[size + 5:-1], refs[-1]
    join_rows(payloads, rows)
    width = rows.shape[2]
    half = CHUNKS // 2
    upper = upper_ref[0]
    keep_ref[:, :, :width] = rows[pl.ds(upper * half, half)]
    send_ref[:, :, :width] = rows[pl.ds((1 - upper) * half, half)]
    dact = None
    for chunk in range(CHUNKS):
        part = dot(rows[chunk], down_ref[:, chunk * width:(chunk + 1) * width], ((1,), (1,)))
        dact = part if dact is None else dact + part
    pre = pre_ref[base:base + rows.shape[1], :]
    sigma = 1.0 / (1.0 + jnp.exp(-pre))
    dpre = (dact * sigma * (1.0 + pre * (1.0 - sigma))).astype(BF16)
    act = (pre * sigma).astype(BF16)
    for ref in (keep_ref, send_ref):
        ref[0, :, width:] = dpre
        ref[1, :, width:] = act
    folds = None
    for chunk in range(CHUNKS):
        part = dot(dpre, up_ref[chunk * width:(chunk + 1) * width, :], ((1,), (1,))).astype(BF16)
        for r in range(size):
            outs[r][chunk * MAIN:(chunk + 1) * MAIN, :] = part[r * MAIN:(r + 1) * MAIN]
        fold = dot(fold_pick(size, chunk), part[size * MAIN:], ((0,), (0,)))
        folds = fold if folds is None else folds + fold
    for r in range(size):
        outs[r][CHUNKS * MAIN:, :] = folds[r * FOLD:(r + 1) * FOLD].astype(BF16)


def add_kernel(a_ref, b_ref, out_ref):
    out_ref[...] = (a_ref[...].astype(F32) + b_ref[...].astype(F32)).astype(BF16)


def grad_kernel(groups, x_keep, x_far, *refs):
    packs, (up_ref, down_ref) = refs[:2 * groups], refs[2 * groups:]
    width = x_keep.shape[2]
    chunk = pl.program_id(0)
    across = ((0,), (0,))

    def side(x_ref, refs):
        dpre = jnp.concatenate([ref[0, :, width:] for ref in refs], axis=0)
        act = jnp.concatenate([ref[1, :, width:] for ref in refs], axis=0)
        g = jnp.concatenate([ref[chunk, :, :width] for ref in refs], axis=0)
        return dot(x_ref[0], dpre, across), dot(act, g, across)

    up_own, down_own = side(x_keep, packs[:groups])
    up_far, down_far = side(x_far, packs[groups:])
    up_ref[...] = (up_own + up_far).astype(BF16)
    down_ref[...] = (down_own + down_far).astype(BF16)


def final_kernel(own_count, mine_ref, routes_ref, *refs):
    own_refs, other_refs, out_ref = refs[:own_count], refs[own_count:-1], refs[-1]
    masks = route_masks(mine_ref, routes_ref)
    width = out_ref.shape[1] // CHUNKS

    def sides(lo, hi):
        return [sum(ref[lo:hi, :].astype(F32) for ref in side) for side in (own_refs, other_refs)]

    folds = sides(CHUNKS * MAIN, CHUNKS * MAIN + FOLD)
    for chunk in range(CHUNKS):
        rows = jnp.concatenate(sides(chunk * MAIN, (chunk + 1) * MAIN) + folds, axis=0).astype(BF16)
        out_ref[:, chunk * width:(chunk + 1) * width] = dot(masks[chunk], rows, ((0,), (0,))).astype(BF16)


def per_device(tokens, cotangent, router_gate, routes, up_weight, down_weight):
    owners = lax.axis_size("expert")
    ranks = lax.axis_size("pipe")
    group = owners // EXPERTS
    tok, model = tokens.shape[1:]
    hidden = up_weight.shape[2]
    width = model // CHUNKS
    half = CHUNKS // 2
    here = lax.axis_index("expert")
    mine = (here // group).astype(jnp.int32).reshape(1)
    upper = (lax.axis_index("pipe") >= ranks // 2).astype(jnp.int32).reshape(1)
    ids = routes.reshape(1, tok)
    up, down = up_weight[0], down_weight[0]

    line = owners == LINE
    groups = [[0, 1, 3], [2]] if line else [list(range(owners))]
    sizes = [len(sources) for sources in groups]
    rows = sum(map(row_count, sizes))

    def held(shape, dtype=BF16):
        return pltpu.VMEM(shape, dtype)

    payload = held((CHUNKS * MAIN + FOLD, width))
    halves = held((half, rows, width))

    def send(value, pairs):
        return lax.ppermute(value, "expert", pairs)

    def swap(value, r):
        return send(value, [(q, q ^ r) for q in range(owners)])

    def mirror(value):
        return lax.ppermute(value, "pipe", [(i, ranks - 1 - i) for i in range(ranks)])

    def deal(own, other):
        if not line:
            return {0: own} | {r: swap(own if r < group else other, r) for r in reversed(range(1, owners))}
        across = swap(other, 3)
        beside = swap(own, 1)
        inner = jnp.logical_and(here > 0, here < owners - 1)
        relayed = send(jnp.where(inner, across, other), [(0, 2), (3, 1), (1, 0), (2, 3)])
        return {0: own, 1: beside, 2: relayed, 3: across}

    small = 1 << 20
    x_own, x_other, g_own, g_other = call(
        route_kernel, (payload,) * 4, small, small,
        in_specs=[smem()] + [hbm()] * 4,
        out_specs=(vmem(),) * 4,
        scratch_shapes=[
            pltpu.VMEM((1, tok), jnp.int32),
            pltpu.VMEM((1, tok), F32),
            pltpu.VMEM((tok, model), BF16),
            pltpu.VMEM((tok, model), BF16),
            pltpu.SemaphoreType.DMA((4,)),
        ],
    )(mine, *map(in_hbm, (ids, router_gate, tokens[0], cotangent[0])))
    x_parts = deal(x_own, x_other)
    g_parts = deal(g_own, g_other)

    flops = 2 * rows * model * hidden
    moved = 2 * model * hidden
    pre, x_keep, x_send, up_here, down_here = call(
        functools.partial(pre_kernel, sizes),
        (held((rows, hidden), F32), halves, halves, held((model, hidden)), held((hidden, model))),
        flops, moved,
        in_specs=[smem()] + [vmem()] * owners + [hbm()] * 2,
        out_specs=(vmem(),) * 5,
        scratch_shapes=[pltpu.VMEM((CHUNKS, rows, width), BF16), pltpu.SemaphoreType.DMA((2,))],
    )(upper, *[x_parts[r] for sources in groups for r in sources], in_hbm(up), in_hbm(down))
    x_far = mirror(x_send)

    back, keeps, sends, base = {}, [], [], 0
    for sources in groups:
        size = len(sources)
        pack = held((2, row_count(size), width + hidden))
        keep, sent, *parts = call(
            functools.partial(group_kernel, size, base), (pack, pack) + (payload,) * size, 2 * flops, 2 * moved,
            in_specs=[smem()] + [vmem()] * (size + 3),
            out_specs=(vmem(),) * (size + 2),
            scratch_shapes=[pltpu.VMEM((CHUNKS, row_count(size), width), BF16)],
        )(upper, *[g_parts[r] for r in sources], pre, up_here, down_here)
        back |= dict(zip(sources, parts))
        keeps.append(keep)
        sends.append(sent)
        base += row_count(size)
    fars = [mirror(sent) for sent in sends]

    if line:
        for_far = send(back[3], [(0, 1), (3, 2)])
        across = send(back[3], [(1, 2), (2, 1)])
        both = call(add_kernel, payload, small, small, in_specs=[vmem()] * 2, out_specs=vmem())(back[2], for_far)
        skipped = swap(both, 2)
        beside = swap(back[1], 1)
        own_side, other_side = [back[0], beside], [across, skipped]
    else:
        got = [back[0]] + [swap(back[r], r) for r in range(1, owners)]
        own_side, other_side = got[:group], got[group:]

    x_chunk = pl.BlockSpec((1, rows, width), lambda k: (k, 0, 0))
    grad_up, grad_down = call(
        functools.partial(grad_kernel, len(groups)),
        (jax.ShapeDtypeStruct((model // 2, hidden), BF16), jax.ShapeDtypeStruct((hidden, model // 2), BF16)),
        2 * flops, moved,
        grid=(half,),
        in_specs=[x_chunk, x_chunk] + [vmem()] * (2 * len(groups)),
        out_specs=(pl.BlockSpec((width, hidden), lambda k: (k, 0)), pl.BlockSpec((hidden, width), lambda k: (0, k))),
    )(x_keep, x_far, *keeps, *fars)
    input_grad = call(
        functools.partial(final_kernel, len(own_side)), jax.ShapeDtypeStruct((tok, model), BF16), small, small,
        in_specs=[smem()] + [vmem()] * (owners + 1), out_specs=vmem(),
    )(mine, ids, *own_side, *other_side)
    return (input_grad[None], grad_up[None], grad_down[None])


def solution(mesh):
    placed = (
        P("pipe", "expert", None),
        P("pipe", "expert", None),
        P("pipe", "expert"),
        P("pipe", "expert", None),
        P("pipe", None, "expert"),
        P("pipe", "expert", None),
    )

    return jax.shard_map(
        per_device,
        mesh=mesh,
        in_specs=placed,
        out_specs=(P("pipe", "expert", None), P("pipe", None, "expert"), P("pipe", "expert", None)),
        check_vma=False,
    )
```

time: 93.6 us -> 77.2 us (0.82)
  waiting for transfers between devices: 50.2 us -> 27.2 us
  starting transfers between devices: 26.1 us -> 33.7 us
  local copies, waits for them, and re-layouts: 6.51 us -> 0.01 us
  Pallas kernels: 9.77 us -> 15.4 us
    ppermute x9 -> x10, waiting for transfers between devices: 43.8 us -> 21.9 us  [send(): return lax.ppermute(value, 'expert', pairs)]
    ppermute x9 -> x10, starting transfers between devices: 22.9 us -> 31 us  [send(): return lax.ppermute(value, 'expert', pairs)]
    unnamed x16 -> x2, local copies, waits for them, and re-layouts: 6.51 us -> 0.01 us
    pallas_call x8 -> x7, Pallas kernels: 9.77 us -> 15.4 us  [the longest x2 5.69 us: per_device(): call(functools.partial(group_kernel, size, base), (pack, pack) + (payload...]
    ppermute x3, waiting for transfers between devices: 6.46 us -> 5.28 us  [mirror(): lax.ppermute(value, 'pipe', [(i, ranks - 1 - i) for i in range(ranks)])]
  transfers between devices with their start and end apart: 12 -> 13, of which waited for: 7 -> 5; matrix products, arithmetic and copies ran while one was open for 0% -> 0% of each run, Pallas kernels for 2% -> 13%
where the time goes in v2:
time: 77.2 us; the launch traced here: 77.1 us
  starting transfers between devices  33.7 us (44%)
  waiting for transfers between devices  27.2 us (35%)
  Pallas kernels  15.4 us (20%)
    ppermute x10, starting transfers between devices, send(): return lax.ppermute(value, 'expert', pairs)  31 us
    ppermute x10, waiting for transfers between devices, send(): return lax.ppermute(value, 'expert', pairs)  21.9 us
    pallas_call x2, Pallas kernels, per_device(): call(functools.partial(group_kernel, size, base), (pack, pack) + (payload...  5.69 us
    ppermute x3, waiting for transfers between devices, mirror(): lax.ppermute(value, 'pipe', [(i, ranks - 1 - i) for i in range(ranks)])  5.28 us
    pallas_call x1, Pallas kernels, per_device(): call(functools.partial(grad_kernel, len(groups)), (jax.ShapeDtypeStruct((...  3.49 us
    pallas_call x1, Pallas kernels, per_device(): call(functools.partial(pre_kernel, sizes), (held((rows, hidden), F32), ha...  3.18 us
    ppermute x3, starting transfers between devices, mirror(): lax.ppermute(value, 'pipe', [(i, ranks - 1 - i) for i in range(ranks)])  2.66 us
    pallas_call x1, Pallas kernels, per_device(): call(route_kernel, (payload,) * 4, small, small, in_specs=[smem()] + [hbm...  1.78 us
  transfers between devices with their start and end apart: 13, of which 5 were waited for; matrix products, arithmetic and copies ran while one was open for 0% of the time, Pallas kernels for 13%

profile of v2, /device:TPU:0, one launch (start us, length us, event | category | flops | bytes accessed | tf_op | source)
XLA Modules:
  0.0 77.1 jit_solution(8367735297402024893)
XLA Ops:
  0.6 1.8 %shard_map.85 = (bf16[136,896]{1,0:T(8,128)(2,1)S(1)}, bf16[136,896]{1,0:T(8,128)(2,1)S(1)}, bf16[136,896]{1,0:T(8,128)(2,1)S(1)}, bf16[136,896]{1,0:T(8,128)(2,1)S(1)}) custom-call(s32[1]{0:T(128)} %bitcast.mine_ref, s32[1,64]{1,0:T(1,128)} %bitcast.10, f32[1,64]{1,0:T(1,128)} %gate_hbm.1, bf16[64,3584]{1,0:T(8,128)(2,1)} %bitcast.14, bf16[64,3584]{1,0:T(8,128)(2,1)} %bitcast.15), custom_call_target="tpu_custom_call" | custom-call | flops 1048576 | bytes 1048576 | tf_op jit(solution)/shard_map/pallas_call | solution.py:274
  2.4 5.1 %collective-permute-start.3 = (bf16[136,896]{1,0:T(8,128)(2,1)S(1)}, bf16[136,896]{1,0:T(8,128)(2,1)S(1)}, u32[]{:S(2)}, u32[]{:S(2)}) collective-permute-start(bf16[136,896]{1,0:T(8,128)(2,1)S(1)} %get-tuple-element.25), channel_id=1, source_target_pairs={{0,3},{1,2},{2,1},{3,0},{4,7},{5,6},{6,5},{7,4},{8,11},{9,10},{10,... | collective-permute-start | bytes 731144 | tf_op jit(solution)/shard_map/ppermute | solution.py:256
  7.6 0.1 collective-permute-start.1
  7.7 0.0 collective-permute-start.2
  7.7 6.9 %collective-permute-done.3.refs_2_ = bf16[136,896]{1,0:T(8,128)(2,1)S(1)} collective-permute-done((bf16[136,896]{1,0:T(8,128)(2,1)S(1)}, bf16[136,896]{1,0:T(8,128)(2,1)S(1)}, u32[]{:S(2)}, u32[]{:S(2)}) %collective-permute-start.3) | collective-permute-done | bytes 243744 | tf_op jit(solution)/shard_map/ppermute | solution.py:256
  14.6 11.3 %collective-permute-start.4 = (bf16[136,896]{1,0:T(8,128)(2,1)S(1)}, bf16[136,896]{1,0:T(8,128)(2,1)S(1)}, u32[]{:S(2)}, u32[]{:S(2)}) collective-permute-start(bf16[136,896]{1,0:T(8,128)(2,1)S(1)} %broadcast_select_fusion.1), channel_id=1, source_target_pairs={{0,2},{3,1},{1,0},{2,3},{4,6},{7,5},{5,4},{6,7},{8,10},{11,9},{9,8... | collective-permute-start | bytes 731144 | tf_op jit(solution)/shard_map/ppermute | solution.py:256
  25.9 0.0 collective-permute-start
  25.9 0.0 collective-permute-done.1.refs_2_
  25.9 9.3 %collective-permute-start.7 = (bf16[136,896]{1,0:T(8,128)(2,1)S(1)}, bf16[136,896]{1,0:T(8,128)(2,1)S(1)}, u32[]{:S(2)}, u32[]{:S(2)}) collective-permute-start(bf16[136,896]{1,0:T(8,128)(2,1)S(1)} %broadcast_select_fusion), channel_id=1, source_target_pairs={{0,2},{3,1},{1,0},{2,3},{4,6},{7,5},{5,4},{6,7},{8,10},{11,9},{9,8... | collective-permute-start | bytes 731144 | tf_op jit(solution)/shard_map/ppermute | solution.py:256
  35.2 0.0 collective-permute-done.2.refs_1_
  35.2 0.0 collective-permute-done.4.refs_3_
  35.2 3.2 %shard_map.86 = (f32[144,512]{1,0:T(8,128)S(1)}, bf16[2,144,896]{2,1,0:T(8,128)(2,1)S(1)}, bf16[2,144,896]{2,1,0:T(8,128)(2,1)S(1)}, bf16[3584,512]{1,0:T(8,128)(2,1)S(1)}, bf16[512,3584]{1,0:T(8,128)(2,1)S(1)}) custom-call(s32[1]{0:T(128)} %bitcast.2.upper_ref, bf16[136,896]{1,0:T(8,128)(2,1)S(1)} %get-tuple-element.24.refs_0_, ...), custom_call_target="tpu_custom_call" | custom-call | flops 528482304 | bytes 3670016 | tf_op jit(solution)/shard_map/pallas_call | solution.py:291
  38.4 0.0 collective-permute-done.refs_1_
  38.4 2.9 %shard_map.87 = (bf16[2,104,1408]{2,1,0:T(8,128)(2,1)S(1)}, bf16[2,104,1408]{2,1,0:T(8,128)(2,1)S(1)}, bf16[136,896]{1,0:T(8,128)(2,1)S(1)}, bf16[136,896]{1,0:T(8,128)(2,1)S(1)}, bf16[136,896]{1,0:T(8,128)(2,1)S(1)}) custom-call(s32[1]{0:T(128)} %bitcast.2.upper_ref, bf16[136,896]{1,0:T(8,128)(2,1)S(1)} %get-tuple-element.22.refs_0_, ...), custom_call_target="tpu_custom_call" | custom-call | flops 1056964608 | bytes 7340032 | tf_op jit(solution)/shard_map/pallas_call | solution.py:305
  41.3 0.0 collective-permute-start.11
  41.3 2.7 %collective-permute-start.10 = (bf16[2,144,896]{2,1,0:T(8,128)(2,1)S(1)}, bf16[2,144,896]{2,1,0:T(8,128)(2,1)S(1)}, u32[]{:S(2)}, u32[]{:S(2)}) collective-permute-start(bf16[2,144,896]{2,1,0:T(8,128)(2,1)S(1)} %get-tuple-element.34), channel_id=1, source_target_pairs={{0,28},{4,24},{8,20},{12,16},{16,12},{20,8},{24,4},{28,0},{1,29},{... | collective-permute-start | bytes 1548296 | tf_op jit(solution)/shard_map/ppermute | solution.py:262
  44.0 2.0 %collective-permute-start.8 = (bf16[136,896]{1,0:T(8,128)(2,1)S(1)}, bf16[136,896]{1,0:T(8,128)(2,1)S(1)}, u32[]{:S(2)}, u32[]{:S(2)}) collective-permute-start(bf16[136,896]{1,0:T(8,128)(2,1)S(1)} %get-tuple-element.31), channel_id=1, source_target_pairs={{0,1},{3,2},{4,5},{7,6},{8,9},{11,10},{12,13},{15,14},{16,17},{19,... | collective-permute-start | bytes 731144 | tf_op jit(solution)/shard_map/ppermute | solution.py:256
  46.0 0.0 copy-start
  46.0 0.1 collective-permute-start.5
  46.1 0.0 collective-permute-done.7.refs_0_
  46.1 0.7 collective-permute-start.6
  46.7 2.8 %shard_map.88 = (bf16[2,40,1408]{2,1,0:T(8,128)(2,1)S(1)}, bf16[2,40,1408]{2,1,0:T(8,128)(2,1)S(1)}, bf16[136,896]{1,0:T(8,128)(2,1)S(1)}) custom-call(s32[1]{0:T(128)} %bitcast.2.upper_ref, bf16[136,896]{1,0:T(8,128)(2,1)S(1)} %collective-permute-done.7.refs_0_, f32[144,512]{1,0:T(8,128)S(1)} %get-tuple-element.26.refs_3_.refs_1_, ...), custom_call_target="tpu_custom_call" | custom-call | flops 1056964608 | bytes 7340032 | tf_op jit(solution)/shard_map/pallas_call | solution.py:305
  49.5 2.7 %collective-permute-done.8.b_ref = bf16[136,896]{1,0:T(8,128)(2,1)S(1)} collective-permute-done((bf16[136,896]{1,0:T(8,128)(2,1)S(1)}, bf16[136,896]{1,0:T(8,128)(2,1)S(1)}, u32[]{:S(2)}, u32[]{:S(2)}) %collective-permute-start.8) | collective-permute-done | bytes 243744 | tf_op jit(solution)/shard_map/ppermute | solution.py:256
  52.2 0.1 shard_map.89
  52.3 2.5 %collective-permute-start.9 = (bf16[136,896]{1,0:T(8,128)(2,1)S(1)}, bf16[136,896]{1,0:T(8,128)(2,1)S(1)}, u32[]{:S(2)}, u32[]{:S(2)}) collective-permute-start(bf16[136,896]{1,0:T(8,128)(2,1)S(1)} %shard_map.89), channel_id=1, source_target_pairs={{0,2},{1,3},{2,0},{3,1},{4,6},{5,7},{6,4},{7,5},{8,10},{9,11},{10,... | collective-permute-start | bytes 731144 | tf_op jit(solution)/shard_map/ppermute | solution.py:256
  54.8 2.6 %collective-permute-done.5.refs_1_ = bf16[136,896]{1,0:T(8,128)(2,1)S(1)} collective-permute-done((bf16[136,896]{1,0:T(8,128)(2,1)S(1)}, bf16[136,896]{1,0:T(8,128)(2,1)S(1)}, u32[]{:S(2)}, u32[]{:S(2)}) %collective-permute-start.5) | collective-permute-done | bytes 243744 | tf_op jit(solution)/shard_map/ppermute | solution.py:256
  57.5 0.0 collective-permute-start.12
  57.5 0.0 collective-permute-done.6.refs_2_
  57.5 9.6 %collective-permute-done.9.refs_3_ = bf16[136,896]{1,0:T(8,128)(2,1)S(1)} collective-permute-done((bf16[136,896]{1,0:T(8,128)(2,1)S(1)}, bf16[136,896]{1,0:T(8,128)(2,1)S(1)}, u32[]{:S(2)}, u32[]{:S(2)}) %collective-permute-start.9) | collective-permute-done | bytes 243744 | tf_op jit(solution)/shard_map/ppermute | solution.py:256
  67.1 0.0 copy-done
  67.1 1.2 %shard_map.90 = bf16[64,3584]{1,0:T(8,128)(2,1)} custom-call(s32[1]{0:T(128)} %bitcast.mine_ref, s32[1,64]{1,0:T(1,128)S(1)} %bitcast.11, bf16[136,896]{1,0:T(8,128)(2,1)S(1)} %get-tuple-element.29.refs_0_, bf16[136,896]{1,0:T(8,128)(2,1)S(1)} %collective-permute-done.5.refs_1_, bf16[136,896]{1,0:T(8,128)(2,1)S(1)} %collective-permute-done.6.refs_2_, ...), custom_call_target="tpu_custom_call" | custom-call | flops 1048576 | bytes 1048576 | tf_op jit(solution)/shard_map/pallas_call | solution.py:337
  68.3 5.3 %collective-permute-done.12.refs_3_ = bf16[2,40,1408]{2,1,0:T(8,128)(2,1)S(1)} collective-permute-done((bf16[2,40,1408]{2,1,0:T(8,128)(2,1)S(1)}, bf16[2,40,1408]{2,1,0:T(8,128)(2,1)S(1)}, u32[]{:S(2)}, u32[]{:S(2)}) %collective-permute-start.12) | collective-permute-done | bytes 225312 | tf_op jit(solution)/shard_map/ppermute | solution.py:262
  73.6 0.0 collective-permute-done.10.x_far
  73.6 0.0 collective-permute-done.11.refs_2_
  73.6 3.5 %shard_map.91 = (bf16[1792,512]{1,0:T(8,128)(2,1)}, bf16[512,1792]{1,0:T(8,128)(2,1)}) custom-call(bf16[2,144,896]{2,1,0:T(8,128)(2,1)S(1)} %get-tuple-element.33.x_keep, bf16[2,144,896]{2,1,0:T(8,128)(2,1)S(1)} %collective-permute-done.10.x_far, bf16[2,104,1408]{2,1,0:T(8,128)(2,1)S(1)} %get-tuple-element.35.refs_0_, ...), custom_call_target="tpu_custom_call" | custom-call | flops 1056964608 | bytes 3670016 | tf_op jit(solution)/shard_map/pallas_call | solution.py:329
  (2 shorter events, 0.1 us)
Async XLA Ops:
  2.4 12.1 %collective-permute-start.3 = (bf16[136,896]{1,0:T(8,128)(2,1)S(1)}, bf16[136,896]{1,0:T(8,128)(2,1)S(1)}, u32[]{:S(2)}, u32[]{:S(2)}) collective-permute-start(bf16[136,896]{1,0:T(8,128)(2,1)S(1)} %get-tuple-element.25), channel_id=1, source_target_pairs={{0,3},{1,2},{2,1},{3,0},{4,7},{5,6},{6,5},{7,4},{8,11},{9,10},{10,... | collective-permute-start | bytes 731144 | tf_op jit(solution)/shard_map/ppermute | solution.py:256
  7.6 18.3 %collective-permute-start.1 = (bf16[136,896]{1,0:T(8,128)(2,1)S(1)}, bf16[136,896]{1,0:T(8,128)(2,1)S(1)}, u32[]{:S(2)}, u32[]{:S(2)}) collective-permute-start(bf16[136,896]{1,0:T(8,128)(2,1)S(1)} %get-tuple-element.23), channel_id=1, source_target_pairs={{0,3},{1,2},{2,1},{3,0},{4,7},{5,6},{6,5},{7,4},{8,11},{9,10},{10,... | collective-permute-start | bytes 731144 | tf_op jit(solution)/shard_map/ppermute | solution.py:256
  7.7 27.5 %collective-permute-start.2 = (bf16[136,896]{1,0:T(8,128)(2,1)S(1)}, bf16[136,896]{1,0:T(8,128)(2,1)S(1)}, u32[]{:S(2)}, u32[]{:S(2)}) collective-permute-start(bf16[136,896]{1,0:T(8,128)(2,1)S(1)} %get-tuple-element.24.refs_0_), channel_id=1, source_target_pairs={{0,1},{1,0},{2,3},{3,2},{4,5},{5,4},{6,7},{7,6},{8,9},{9,8},{10,11... | collective-permute-start | bytes 731144 | tf_op jit(solution)/shard_map/ppermute | solution.py:256
  14.6 20.6 %collective-permute-start.4 = (bf16[136,896]{1,0:T(8,128)(2,1)S(1)}, bf16[136,896]{1,0:T(8,128)(2,1)S(1)}, u32[]{:S(2)}, u32[]{:S(2)}) collective-permute-start(bf16[136,896]{1,0:T(8,128)(2,1)S(1)} %broadcast_select_fusion.1), channel_id=1, source_target_pairs={{0,2},{3,1},{1,0},{2,3},{4,6},{7,5},{5,4},{6,7},{8,10},{11,9},{9,8... | collective-permute-start | bytes 731144 | tf_op jit(solution)/shard_map/ppermute | solution.py:256
  25.9 12.5 %collective-permute-start = (bf16[136,896]{1,0:T(8,128)(2,1)S(1)}, bf16[136,896]{1,0:T(8,128)(2,1)S(1)}, u32[]{:S(2)}, u32[]{:S(2)}) collective-permute-start(bf16[136,896]{1,0:T(8,128)(2,1)S(1)} %get-tuple-element.22.refs_0_), channel_id=1, source_target_pairs={{0,1},{1,0},{2,3},{3,2},{4,5},{5,4},{6,7},{7,6},{8,9},{9,8},{10,11... | collective-permute-start | bytes 731144 | tf_op jit(solution)/shard_map/ppermute | solution.py:256
  25.9 20.1 %collective-permute-start.7 = (bf16[136,896]{1,0:T(8,128)(2,1)S(1)}, bf16[136,896]{1,0:T(8,128)(2,1)S(1)}, u32[]{:S(2)}, u32[]{:S(2)}) collective-permute-start(bf16[136,896]{1,0:T(8,128)(2,1)S(1)} %broadcast_select_fusion), channel_id=1, source_target_pairs={{0,2},{3,1},{1,0},{2,3},{4,6},{7,5},{5,4},{6,7},{8,10},{11,9},{9,8... | collective-permute-start | bytes 731144 | tf_op jit(solution)/shard_map/ppermute | solution.py:256
  41.3 32.2 %collective-permute-start.11 = (bf16[2,104,1408]{2,1,0:T(8,128)(2,1)S(1)}, bf16[2,104,1408]{2,1,0:T(8,128)(2,1)S(1)}, u32[]{:S(2)}, u32[]{:S(2)}) collective-permute-start(bf16[2,104,1408]{2,1,0:T(8,128)(2,1)S(1)} %get-tuple-element.37), channel_id=1, source_target_pairs={{0,28},{4,24},{8,20},{12,16},{16,12},{20,8},{24,4},{28,0},{1,29},{... | collective-permute-start | bytes 1757192 | tf_op jit(solution)/shard_map/ppermute | solution.py:262
  41.3 32.2 %collective-permute-start.10 = (bf16[2,144,896]{2,1,0:T(8,128)(2,1)S(1)}, bf16[2,144,896]{2,1,0:T(8,128)(2,1)S(1)}, u32[]{:S(2)}, u32[]{:S(2)}) collective-permute-start(bf16[2,144,896]{2,1,0:T(8,128)(2,1)S(1)} %get-tuple-element.34), channel_id=1, source_target_pairs={{0,28},{4,24},{8,20},{12,16},{16,12},{20,8},{24,4},{28,0},{1,29},{... | collective-permute-start | bytes 1548296 | tf_op jit(solution)/shard_map/ppermute | solution.py:262
  44.0 8.2 %collective-permute-start.8 = (bf16[136,896]{1,0:T(8,128)(2,1)S(1)}, bf16[136,896]{1,0:T(8,128)(2,1)S(1)}, u32[]{:S(2)}, u32[]{:S(2)}) collective-permute-start(bf16[136,896]{1,0:T(8,128)(2,1)S(1)} %get-tuple-element.31), channel_id=1, source_target_pairs={{0,1},{3,2},{4,5},{7,6},{8,9},{11,10},{12,13},{15,14},{16,17},{19,... | collective-permute-start | bytes 731144 | tf_op jit(solution)/shard_map/ppermute | solution.py:256
  46.0 21.1 %copy-start = (s32[1,64,1]{1,2,0:T(1,128)S(1)}, s32[1,64,1]{1,2,0:T(1,128)}, u32[]{:S(2)}) copy-start(s32[1,64,1]{1,2,0:T(1,128)} %param.9) | copy-start | bytes 772
  46.0 11.5 %collective-permute-start.5 = (bf16[136,896]{1,0:T(8,128)(2,1)S(1)}, bf16[136,896]{1,0:T(8,128)(2,1)S(1)}, u32[]{:S(2)}, u32[]{:S(2)}) collective-permute-start(bf16[136,896]{1,0:T(8,128)(2,1)S(1)} %get-tuple-element.30), channel_id=1, source_target_pairs={{0,1},{1,0},{2,3},{3,2},{4,5},{5,4},{6,7},{7,6},{8,9},{9,8},{10,11... | collective-permute-start | bytes 731144 | tf_op jit(solution)/shard_map/ppermute | solution.py:256
  46.1 11.4 %collective-permute-start.6 = (bf16[136,896]{1,0:T(8,128)(2,1)S(1)}, bf16[136,896]{1,0:T(8,128)(2,1)S(1)}, u32[]{:S(2)}, u32[]{:S(2)}) collective-permute-start(bf16[136,896]{1,0:T(8,128)(2,1)S(1)} %get-tuple-element.31), channel_id=1, source_target_pairs={{1,2},{2,1},{5,6},{6,5},{9,10},{10,9},{13,14},{14,13},{17,18},{18,... | collective-permute-start | bytes 731144 | tf_op jit(solution)/shard_map/ppermute | solution.py:256
  52.3 14.8 %collective-permute-start.9 = (bf16[136,896]{1,0:T(8,128)(2,1)S(1)}, bf16[136,896]{1,0:T(8,128)(2,1)S(1)}, u32[]{:S(2)}, u32[]{:S(2)}) collective-permute-start(bf16[136,896]{1,0:T(8,128)(2,1)S(1)} %shard_map.89), channel_id=1, source_target_pairs={{0,2},{1,3},{2,0},{3,1},{4,6},{5,7},{6,4},{7,5},{8,10},{9,11},{10,... | collective-permute-start | bytes 731144 | tf_op jit(solution)/shard_map/ppermute | solution.py:256
  57.5 16.1 %collective-permute-start.12 = (bf16[2,40,1408]{2,1,0:T(8,128)(2,1)S(1)}, bf16[2,40,1408]{2,1,0:T(8,128)(2,1)S(1)}, u32[]{:S(2)}, u32[]{:S(2)}) collective-permute-start(bf16[2,40,1408]{2,1,0:T(8,128)(2,1)S(1)} %get-tuple-element.38), channel_id=1, source_target_pairs={{0,28},{4,24},{8,20},{12,16},{16,12},{20,8},{24,4},{28,0},{1,29},{... | collective-permute-start | bytes 675848 | tf_op jit(solution)/shard_map/ppermute | solution.py:262

commit v3 on v2

v3 whole, which is shorter than its diff:
```python
import functools

import jax
import jax.numpy as jnp
from jax import lax
from jax.experimental import pallas as pl
from jax.experimental.pallas import tpu as pltpu
from jax.sharding import PartitionSpec as P


EXPERTS = 2
CAP = 34
FOLD = 8
MAIN = CAP // FOLD * FOLD
REM = CAP - MAIN
CHUNKS = FOLD // REM
LINE = 4
VMEM_LIMIT = 24 * 1024 * 1024
F32 = jnp.float32
BF16 = jnp.bfloat16


def dot(a, b, dims=((1,), (0,))):
    return lax.dot_general(a, b, (dims, ((), ())), preferred_element_type=F32)


def vmem():
    return pl.BlockSpec(memory_space=pltpu.VMEM)


def smem():
    return pl.BlockSpec(memory_space=pltpu.SMEM)


def in_hbm(value):
    return pltpu.with_memory_space_constraint(value, pltpu.HBM)


def call(kernel, outs, flops, moved, **more):
    return pl.pallas_call(
        kernel,
        out_shape=outs,
        compiler_params=pltpu.CompilerParams(vmem_limit_bytes=VMEM_LIMIT),
        cost_estimate=pl.CostEstimate(flops=flops, bytes_accessed=moved, transcendentals=0),
        **more,
    )


def route_masks(mine_ref, routes_ref):
    routes = routes_ref[...]
    tok = routes.shape[1]
    own = routes == mine_ref[0]
    own_f = jnp.where(own, 1.0, 0.0).astype(F32)
    earlier = lax.broadcasted_iota(jnp.int32, (tok, tok), 0) < lax.broadcasted_iota(jnp.int32, (tok, tok), 1)
    count_own = dot(jnp.broadcast_to(own_f, (8, tok)).astype(BF16), jnp.where(earlier, 1.0, 0.0).astype(BF16))[0:1]
    index = lax.broadcasted_iota(jnp.int32, (1, tok), 1)
    count_own = count_own.astype(jnp.int32)
    slot = jnp.where(own, count_own, index - count_own)
    rows = 2 * MAIN + 2 * FOLD
    row = lax.broadcasted_iota(jnp.int32, (rows, tok), 0)
    slot = jnp.broadcast_to(slot, (rows, tok))
    own = jnp.broadcast_to(jnp.where(own, 1, 0), (rows, tok))
    side = jnp.where(row < 2 * MAIN, row // MAIN, (row - 2 * MAIN) // FOLD)
    place = lax.rem(row, FOLD)
    hit_side = own == 1 - side
    masks = []
    for chunk in range(CHUNKS):
        folded = jnp.where(place // REM == chunk, MAIN + lax.rem(place, REM), -1)
        wanted = jnp.where(row < 2 * MAIN, lax.rem(row, MAIN), folded)
        masks.append(jnp.where(jnp.logical_and(hit_side, slot == wanted), 1.0, 0.0).astype(BF16))
    return masks


def split_rows(masks, source, own_ref, other_ref):
    width = source.shape[1] // CHUNKS
    fold_own = fold_other = None
    for chunk in range(CHUNKS):
        part = dot(masks[chunk], source[:, chunk * width:(chunk + 1) * width])
        own_ref[chunk * MAIN:(chunk + 1) * MAIN, :] = part[:MAIN].astype(BF16)
        other_ref[chunk * MAIN:(chunk + 1) * MAIN, :] = part[MAIN:2 * MAIN].astype(BF16)
        a, b = part[2 * MAIN:2 * MAIN + FOLD], part[2 * MAIN + FOLD:]
        fold_own = a if fold_own is None else fold_own + a
        fold_other = b if fold_other is None else fold_other + b
    own_ref[CHUNKS * MAIN:, :] = fold_own.astype(BF16)
    other_ref[CHUNKS * MAIN:, :] = fold_other.astype(BF16)


def hbm():
    return pl.BlockSpec(memory_space=pltpu.HBM)


def route_x_kernel(mine_ref, ids_hbm, gate_hbm, tokens_hbm, cot_hbm, own, other, masks_ref, gate, cot, ids, tokens, sems):
    copies = [
        pltpu.make_async_copy(src, dst, sems.at[i])
        for i, (src, dst) in enumerate([(ids_hbm, ids), (tokens_hbm, tokens), (gate_hbm, gate), (cot_hbm, cot)])
    ]
    for copy in copies:
        copy.start()
    copies[0].wait()
    masks = route_masks(mine_ref, ids)
    for chunk in range(CHUNKS):
        masks_ref[chunk] = masks[chunk]
    copies[1].wait()
    split_rows(masks, tokens[...], own, other)
    copies[2].wait()
    copies[3].wait()


def route_g_kernel(masks_ref, gate, cot, own, other):
    tok = gate.shape[1]
    eye = lax.broadcasted_iota(jnp.int32, (tok, tok), 0) == lax.broadcasted_iota(jnp.int32, (tok, tok), 1)
    column = jnp.sum(jnp.where(eye, jnp.broadcast_to(gate[...], (tok, tok)), 0.0), axis=1, keepdims=True)
    scaled = (column * cot[...].astype(F32)).astype(BF16)
    split_rows([masks_ref[chunk] for chunk in range(CHUNKS)], scaled, own, other)


def fold_rows(count):
    return -(-count * REM // FOLD) * FOLD


def row_count(count):
    return count * MAIN + fold_rows(count)


def fold_pick(count, chunk):
    shape = (fold_rows(count), count * FOLD)
    row = lax.broadcasted_iota(jnp.int32, shape, 0)
    col = lax.broadcasted_iota(jnp.int32, shape, 1)
    want = row // REM * FOLD + chunk * REM + lax.rem(row, REM)
    return jnp.where(col == want, 1.0, 0.0).astype(BF16)


def join_rows(payloads, rows_ref, base=0):
    count = len(payloads)
    folds = jnp.concatenate([ref[CHUNKS * MAIN:, :].astype(F32) for ref in payloads], axis=0).astype(BF16)
    last = base + count * MAIN
    for chunk in range(CHUNKS):
        for r, ref in enumerate(payloads):
            rows_ref[chunk, base + r * MAIN:base + (r + 1) * MAIN, :] = ref[chunk * MAIN:(chunk + 1) * MAIN, :]
        rows_ref[chunk, last:last + fold_rows(count), :] = dot(fold_pick(count, chunk), folds).astype(BF16)


def pick_halves(upper_ref, rows, keep_ref, send_ref):
    half = CHUNKS // 2
    upper = upper_ref[0]
    keep_ref[...] = rows[pl.ds(upper * half, half)]
    send_ref[...] = rows[pl.ds((1 - upper) * half, half)]


def times_up(rows, up_ref):
    width = rows.shape[2]
    return sum(dot(rows[chunk], up_ref[chunk * width:(chunk + 1) * width, :]) for chunk in range(CHUNKS))


def hidden_values(rows, pre, down_ref):
    width = rows.shape[2]
    dact = sum(dot(rows[chunk], down_ref[chunk * width:(chunk + 1) * width, :]) for chunk in range(CHUNKS))
    sigma = 1.0 / (1.0 + jnp.exp(-pre))
    return (dact * sigma * (1.0 + pre * (1.0 - sigma))).astype(BF16), (pre * sigma).astype(BF16)


def back_rows(dpre, up_ref, outs):
    size = len(outs)
    width = up_ref.shape[1] // CHUNKS
    folds = None
    for chunk in range(CHUNKS):
        part = dot(dpre, up_ref[:, chunk * width:(chunk + 1) * width]).astype(BF16)
        for r in range(size):
            outs[r][chunk * MAIN:(chunk + 1) * MAIN, :] = part[r * MAIN:(r + 1) * MAIN]
        fold = dot(fold_pick(size, chunk), part[size * MAIN:], ((0,), (0,)))
        folds = fold if folds is None else folds + fold
    for r in range(size):
        outs[r][CHUNKS * MAIN:, :] = folds[r * FOLD:(r + 1) * FOLD].astype(BF16)


def pre_kernel(size, upper_ref, *refs):
    payloads, (up_hbm, down_hbm, pre_ref, keep_ref, send_ref, up_ref, down_ref, rows, sems) = refs[:size], refs[size:]
    load_up = pltpu.make_async_copy(up_hbm, up_ref, sems.at[0])
    load_down = pltpu.make_async_copy(down_hbm, down_ref, sems.at[1])
    load_up.start()
    load_down.start()
    join_rows(payloads, rows)
    pick_halves(upper_ref, rows, keep_ref, send_ref)
    load_up.wait()
    pre_ref[...] = times_up(rows, up_ref)
    load_down.wait()


def flip_kernel(up_ref, down_ref, up_out, down_out):
    width = up_ref.shape[0] // CHUNKS
    for chunk in range(CHUNKS):
        at = slice(chunk * width, (chunk + 1) * width)
        up_out[:, at] = up_ref[at, :].T
        down_out[at, :] = down_ref[:, at].T


def group_kernel(size, upper_ref, *refs):
    payloads, (pre_ref, up_ref, down_ref, keep_ref, send_ref) = refs[:size], refs[size:size + 5]
    outs, rows = refs[size + 5:-1], refs[-1]
    join_rows(payloads, rows)
    width = rows.shape[2]
    pick_halves(upper_ref, rows, keep_ref.at[:, :, :width], send_ref.at[:, :, :width])
    values = hidden_values(rows, pre_ref[...], down_ref)
    for ref in (keep_ref, send_ref):
        for plane in range(2):
            ref[plane, :, width:] = values[plane]
    back_rows(values[0], up_ref, outs)


def pick_kernel(upper_ref, payload_ref, keep_ref, send_ref, rows):
    width = rows.shape[3]
    for t in range(2):
        join_rows([payload_ref.at[t]], rows.at[t])
        at = slice(t * width, (t + 1) * width)
        pick_halves(upper_ref, rows.at[t], keep_ref.at[:, :, at], send_ref.at[:, :, at])


def last_kernel(rows, up_ref, up_t_ref, down_t_ref, hidden_ref, out_ref):
    values = hidden_values(rows.at[1], times_up(rows.at[0], up_ref), down_t_ref)
    for plane in range(2):
        hidden_ref[plane] = values[plane]
    back_rows(values[0], up_t_ref, [out_ref])


def relay_kernel(inner_ref, own_x, own_g, passed_x, passed_g, out_ref):
    @pl.when(inner_ref[0] == 1)
    def _():
        out_ref[0] = passed_x[...]
        out_ref[1] = passed_g[...]

    @pl.when(inner_ref[0] == 0)
    def _():
        out_ref[0] = own_x[...]
        out_ref[1] = own_g[...]


def add_kernel(a_ref, b_ref, out_ref):
    out_ref[...] = (a_ref[...].astype(F32) + b_ref[...].astype(F32)).astype(BF16)


def grad_kernel(with_last, *refs):
    up_ref, down_ref = refs[-2:]
    xs, packs = refs[0:2], refs[2:4]
    lasts, hiddens = (refs[4:6], refs[6:8]) if with_last else ((), ())
    width = xs[0].shape[2]
    chunk = pl.program_id(0)
    across = ((0,), (0,))

    def joined(pieces):
        return jnp.concatenate(pieces, axis=0)

    x = joined([ref[0] for ref in xs] + [ref[chunk, :, :width] for ref in lasts])
    g = joined([ref[chunk, :, :width] for ref in packs] + [ref[chunk, :, width:] for ref in lasts])
    dpre, act = (joined([ref[t, :, width:] for ref in packs] + [ref[t] for ref in hiddens]) for t in range(2))
    up_ref[...] = dot(x, dpre, across).astype(BF16)
    down_ref[...] = dot(act, g, across).astype(BF16)


def final_kernel(own_count, masks_ref, *refs):
    own_refs, other_refs, out_ref = refs[:own_count], refs[own_count:-1], refs[-1]
    width = out_ref.shape[1] // CHUNKS

    def sides(lo, hi):
        return [sum(ref[lo:hi, :].astype(F32) for ref in side) for side in (own_refs, other_refs)]

    folds = sides(CHUNKS * MAIN, CHUNKS * MAIN + FOLD)
    for chunk in range(CHUNKS):
        rows = jnp.concatenate(sides(chunk * MAIN, (chunk + 1) * MAIN) + folds, axis=0).astype(BF16)
        out_ref[:, chunk * width:(chunk + 1) * width] = dot(masks_ref[chunk], rows, ((0,), (0,))).astype(BF16)


def per_device(tokens, cotangent, router_gate, routes, up_weight, down_weight):
    owners = lax.axis_size("expert")
    ranks = lax.axis_size("pipe")
    group = owners // EXPERTS
    tok, model = tokens.shape[1:]
    hidden = up_weight.shape[2]
    width = model // CHUNKS
    half = CHUNKS // 2
    here = lax.axis_index("expert")
    mine = (here // group).astype(jnp.int32).reshape(1)
    upper = (lax.axis_index("pipe") >= ranks // 2).astype(jnp.int32).reshape(1)
    ids = routes.reshape(1, tok)
    up, down = up_weight[0], down_weight[0]

    line = owners == LINE
    sources = [0, 1, 3] if line else list(range(owners))
    size = len(sources)
    rows = row_count(size)

    def held(shape, dtype=BF16):
        return pltpu.VMEM(shape, dtype)

    payload_shape = (CHUNKS * MAIN + FOLD, width)
    payload = held(payload_shape)
    halves = held((half, rows, width))

    def send(value, pairs):
        return lax.ppermute(value, "expert", pairs)

    def swap(value, r):
        return send(value, [(q, q ^ r) for q in range(owners)])

    def mirror(value):
        return lax.ppermute(value, "pipe", [(i, ranks - 1 - i) for i in range(ranks)])

    small = 1 << 20
    x_own, x_other, masks, gate, cot = call(
        route_x_kernel,
        (payload, payload, held((CHUNKS, 2 * MAIN + 2 * FOLD, tok)), held((1, tok), F32), held((tok, model))),
        small, small,
        in_specs=[smem()] + [hbm()] * 4,
        out_specs=(vmem(),) * 5,
        scratch_shapes=[pltpu.VMEM((1, tok), jnp.int32), pltpu.VMEM((tok, model), BF16), pltpu.SemaphoreType.DMA((4,))],
    )(mine, *map(in_hbm, (ids, router_gate, tokens[0], cotangent[0])))
    g_own, g_other = call(
        route_g_kernel, (payload, payload), small, small, in_specs=[vmem()] * 3, out_specs=(vmem(),) * 2
    )(masks, gate, cot)
    if line:
        x_across, x_beside = swap(x_other, 3), swap(x_own, 1)
        g_across, g_beside = swap(g_other, 3), swap(g_own, 1)
        x_parts, g_parts = [x_own, x_beside, x_across], [g_own, g_beside, g_across]
    else:
        x_parts, g_parts = (
            [own] + [swap(own if r < group else other, r) for r in range(1, owners)]
            for own, other in ((x_own, x_other), (g_own, g_other))
        )

    flops = 2 * rows * model * hidden
    moved = 2 * model * hidden
    pre, x_keep, x_send, up_here, down_here = call(
        functools.partial(pre_kernel, size),
        (held((rows, hidden), F32), halves, halves, held((model, hidden)), held((hidden, model))),
        flops, moved,
        in_specs=[smem()] + [vmem()] * size + [hbm()] * 2,
        out_specs=(vmem(),) * 5,
        scratch_shapes=[pltpu.VMEM((CHUNKS, rows, width), BF16), pltpu.SemaphoreType.DMA((2,))],
    )(upper, *x_parts, in_hbm(up), in_hbm(down))
    if line:
        inner = jnp.logical_and(here > 0, here < owners - 1).astype(jnp.int32).reshape(1)
        relayed = call(
            relay_kernel, held((2,) + payload_shape), small, small, in_specs=[smem()] + [vmem()] * 4, out_specs=vmem()
        )(inner, x_other, g_other, x_across, g_across)
        relayed = send(relayed, [(0, 2), (3, 1), (1, 0), (2, 3)])
    x_far = mirror(x_send)
    up_t, down_t = call(
        flip_kernel, (held((hidden, model)), held((model, hidden))), small, moved, in_specs=[vmem()] * 2, out_specs=(vmem(),) * 2
    )(up_here, down_here)
    pack = held((2, rows, width + hidden))
    keep, sent, *parts = call(
        functools.partial(group_kernel, size), (pack, pack) + (payload,) * size, 2 * flops, 2 * moved,
        in_specs=[smem()] + [vmem()] * (size + 3),
        out_specs=(vmem(),) * (size + 2),
        scratch_shapes=[pltpu.VMEM((CHUNKS, rows, width), BF16)],
    )(upper, *g_parts, pre, up_t, down_t)
    back = dict(zip(sources, parts))
    for_grad = [x_keep, x_far, keep, mirror(sent)]

    if line:
        one = row_count(1)
        pack = held((2, one, 2 * width))
        last_keep, last_sent, last_rows = call(
            pick_kernel, (pack, pack, held((2, CHUNKS, one, width))), small, small,
            in_specs=[smem(), vmem()],
            out_specs=(vmem(),) * 3,
        )(upper, relayed)
        last_far = mirror(last_sent)
        last_hidden, last_back = call(
            last_kernel, (held((2, one, hidden)), payload), flops, 2 * moved,
            in_specs=[vmem()] * 4,
            out_specs=(vmem(),) * 2,
        )(last_rows, up_here, up_t, down_t)
        for_grad += [last_keep, last_far, last_hidden, mirror(last_hidden)]
        for_far = send(back[3], [(0, 1), (3, 2)])
        across = send(back[3], [(1, 2), (2, 1)])
        both = call(add_kernel, payload, small, small, in_specs=[vmem()] * 2, out_specs=vmem())(last_back, for_far)
        skipped = swap(both, 2)
        own_side, other_side = [back[0], swap(back[1], 1)], [across, skipped]
    else:
        got = [back[0]] + [swap(back[r], r) for r in range(1, owners)]
        own_side, other_side = got[:group], got[group:]

    x_chunk = pl.BlockSpec((1, rows, width), lambda k: (k, 0, 0))
    grad_up, grad_down = call(
        functools.partial(grad_kernel, line),
        (jax.ShapeDtypeStruct((model // 2, hidden), BF16), jax.ShapeDtypeStruct((hidden, model // 2), BF16)),
        2 * flops, moved,
        grid=(half,),
        in_specs=[x_chunk, x_chunk] + [vmem()] * (len(for_grad) - 2),
        out_specs=(pl.BlockSpec((width, hidden), lambda k: (k, 0)), pl.BlockSpec((hidden, width), lambda k: (0, k))),
    )(*for_grad)
    input_grad = call(
        functools.partial(final_kernel, len(own_side)), jax.ShapeDtypeStruct((tok, model), BF16), small, small,
        in_specs=[vmem()] * (owners + 1), out_specs=vmem(),
    )(masks, *own_side, *other_side)
    return (input_grad[None], grad_up[None], grad_down[None])


def solution(mesh):
    placed = (
        P("pipe", "expert", None),
        P("pipe", "expert", None),
        P("pipe", "expert"),
        P("pipe", "expert", None),
        P("pipe", None, "expert"),
        P("pipe", "expert", None),
    )

    return jax.shard_map(
        per_device,
        mesh=mesh,
        in_specs=placed,
        out_specs=(P("pipe", "expert", None), P("pipe", None, "expert"), P("pipe", "expert", None)),
        check_vma=False,
    )
```

time: 77.2 us -> 72.5 us (0.939)
  starting transfers between devices: 33.7 us -> 28.9 us
    ppermute x10 -> x9, starting transfers between devices: 31 us -> 23.5 us  [send(): return lax.ppermute(value, 'expert', pairs)]
    ppermute x3 -> x4, starting transfers between devices: 2.66 us -> 5.41 us  [mirror(): lax.ppermute(value, 'pipe', [(i, ranks - 1 - i) for i in range(ranks)])]
    ppermute x3 -> x4, waiting for transfers between devices: 5.28 us -> 2.78 us  [mirror(): lax.ppermute(value, 'pipe', [(i, ranks - 1 - i) for i in range(ranks)])]
    ppermute x10 -> x9, waiting for transfers between devices: 21.9 us -> 23.9 us  [send(): return lax.ppermute(value, 'expert', pairs)]
    pallas_call x5 -> x9, Pallas kernels: 14.2 us -> 14.9 us  [the longest x1 3.4 us: per_device(): call(functools.partial(grad_kernel, line), (jax.ShapeDtypeStruct((model /...]
  transfers between devices with their start and end apart: 13 -> 13, of which waited for: 5 -> 6; matrix products, arithmetic and copies ran while one was open for 0% -> 0% of each run, Pallas kernels for 13% -> 16%
where the time goes in v3:
time: 72.5 us; the launch traced here: 72.3 us
  starting transfers between devices  28.9 us (40%)
  waiting for transfers between devices  26.6 us (37%)
  Pallas kernels  16 us (22%)
  between operations  0.75 us (1%)
    ppermute x9, waiting for transfers between devices, send(): return lax.ppermute(value, 'expert', pairs)  23.9 us
    ppermute x9, starting transfers between devices, send(): return lax.ppermute(value, 'expert', pairs)  23.5 us
    ppermute x4, starting transfers between devices, mirror(): lax.ppermute(value, 'pipe', [(i, ranks - 1 - i) for i in range(ranks)])  5.41 us
    pallas_call x1, Pallas kernels, per_device(): call(functools.partial(grad_kernel, line), (jax.ShapeDtypeStruct((model /...  3.4 us
    pallas_call x1, Pallas kernels, per_device(): call(functools.partial(pre_kernel, size), (held((rows, hidden), F32), hal...  3.18 us
    ppermute x4, waiting for transfers between devices, mirror(): lax.ppermute(value, 'pipe', [(i, ranks - 1 - i) for i in range(ranks)])  2.78 us
    pallas_call x1, Pallas kernels, per_device(): call(last_kernel, (held((2, one, hidden)), payload), flops, 2 * moved, in...  2.41 us
    pallas_call x1, Pallas kernels, per_device(): call(flip_kernel, (held((hidden, model)), held((model, hidden))), small,...  1.94 us
  transfers between devices with their start and end apart: 13, of which 6 were waited for; matrix products, arithmetic and copies ran while one was open for 0% of the time, Pallas kernels for 16%

profile of v3, /device:TPU:0, one launch (start us, length us, event | category | flops | bytes accessed | tf_op | source)
XLA Modules:
  0.0 72.3 jit_solution(1659994686677425997)
XLA Ops:
  0.6 1.4 %shard_map.85 = (bf16[136,896]{1,0:T(8,128)(2,1)S(1)}, bf16[136,896]{1,0:T(8,128)(2,1)S(1)}, bf16[4,80,64]{2,1,0:T(8,128)(2,1)S(1)}, f32[1,64]{1,0:T(1,128)S(1)}, bf16[64,3584]{1,0:T(8,128)(2,1)S(1)}) custom-call(s32[1]{0:T(128)} %bitcast.mine_ref, s32[1,64]{1,0:T(1,128)} %bitcast.16, f32[1,64]{1,0:T(1,128)} %gate_hbm.1, bf16[64,3584]{1,0:T(8,128)(2,1)} %bitcast.13, ...), custom_call_target="tpu_custom_call" | custom-call | flops 1048576 | bytes 1048576 | tf_op jit(solution)/shard_map/pallas_call | solution.py:308
  2.0 5.1 %collective-permute-start.3 = (bf16[136,896]{1,0:T(8,128)(2,1)S(1)}, bf16[136,896]{1,0:T(8,128)(2,1)S(1)}, u32[]{:S(2)}, u32[]{:S(2)}) collective-permute-start(bf16[136,896]{1,0:T(8,128)(2,1)S(1)} %get-tuple-element.35.own_x), channel_id=1, source_target_pairs={{0,3},{1,2},{2,1},{3,0},{4,7},{5,6},{6,5},{7,4},{8,11},{9,10},{10,... | collective-permute-start | bytes 731144 | tf_op jit(solution)/shard_map/ppermute | solution.py:299
  7.2 0.4 shard_map.86
  7.6 0.1 collective-permute-start.1
  7.7 0.1 collective-permute-start.2
  7.7 2.0 %collective-permute-start = (bf16[136,896]{1,0:T(8,128)(2,1)S(1)}, bf16[136,896]{1,0:T(8,128)(2,1)S(1)}, u32[]{:S(2)}, u32[]{:S(2)}) collective-permute-start(bf16[136,896]{1,0:T(8,128)(2,1)S(1)} %get-tuple-element.32.refs_0_), channel_id=1, source_target_pairs={{0,1},{1,0},{2,3},{3,2},{4,5},{5,4},{6,7},{7,6},{8,9},{9,8},{10,11... | collective-permute-start | bytes 731144 | tf_op jit(solution)/shard_map/ppermute | solution.py:299
  9.7 4.4 %collective-permute-done.3.refs_2_.passed_x = bf16[136,896]{1,0:T(8,128)(2,1)S(1)} collective-permute-done((bf16[136,896]{1,0:T(8,128)(2,1)S(1)}, bf16[136,896]{1,0:T(8,128)(2,1)S(1)}, u32[]{:S(2)}, u32[]{:S(2)}) %collective-permute-start.3) | collective-permute-done | bytes 243744 | tf_op jit(solution)/shard_map/ppermute | solution.py:299
  14.1 5.1 %collective-permute-done.1.refs_2_.passed_g = bf16[136,896]{1,0:T(8,128)(2,1)S(1)} collective-permute-done((bf16[136,896]{1,0:T(8,128)(2,1)S(1)}, bf16[136,896]{1,0:T(8,128)(2,1)S(1)}, u32[]{:S(2)}, u32[]{:S(2)}) %collective-permute-start.1) | collective-permute-done | bytes 243744 | tf_op jit(solution)/shard_map/ppermute | solution.py:299
  19.3 10.3 %collective-permute-start.6 = (bf16[2,136,896]{2,1,0:T(8,128)(2,1)S(1)}, bf16[2,136,896]{2,1,0:T(8,128)(2,1)S(1)}, u32[]{:S(2)}, u32[]{:S(2)}) collective-permute-start(bf16[2,136,896]{2,1,0:T(8,128)(2,1)S(1)} %shard_map.90), channel_id=1, source_target_pairs={{0,2},{3,1},{1,0},{2,3},{4,6},{7,5},{5,4},{6,7},{8,10},{11,9},{9,8... | collective-permute-start | bytes 1462280 | tf_op jit(solution)/shard_map/ppermute | solution.py:299
  29.6 0.0 collective-permute-done.2.refs_1_
  29.6 3.2 %shard_map.87 = (f32[104,512]{1,0:T(8,128)S(1)}, bf16[2,104,896]{2,1,0:T(8,128)(2,1)S(1)}, bf16[2,104,896]{2,1,0:T(8,128)(2,1)S(1)}, bf16[3584,512]{1,0:T(8,128)(2,1)S(1)}, bf16[512,3584]{1,0:T(8,128)(2,1)S(1)}) custom-call(s32[1]{0:T(128)} %bitcast.4.upper_ref, bf16[136,896]{1,0:T(8,128)(2,1)S(1)} %get-tuple-element.34.refs_0_, ...), custom_call_target="tpu_custom_call" | custom-call | flops 381681664 | bytes 3670016 | tf_op jit(solution)/shard_map/pallas_call | solution.py:331
  32.8 1.9 %shard_map.88 = (bf16[512,3584]{1,0:T(8,128)(2,1)S(1)}, bf16[3584,512]{1,0:T(8,128)(2,1)S(1)}) custom-call(bf16[3584,512]{1,0:T(8,128)(2,1)S(1)} %get-tuple-element.37.up_ref, bf16[512,3584]{1,0:T(8,128)(2,1)S(1)} %get-tuple-element.38.down_ref), custom_call_target="tpu_custom_call" | custom-call | flops 1048576 | bytes 3670016 | tf_op jit(solution)/shard_map/pallas_call | solution.py:346
  34.7 0.0 collective-permute-done.refs_1_
  34.7 1.9 %shard_map.89 = (bf16[2,104,1408]{2,1,0:T(8,128)(2,1)S(1)}, bf16[2,104,1408]{2,1,0:T(8,128)(2,1)S(1)}, bf16[136,896]{1,0:T(8,128)(2,1)S(1)}, bf16[136,896]{1,0:T(8,128)(2,1)S(1)}, bf16[136,896]{1,0:T(8,128)(2,1)S(1)}) custom-call(s32[1]{0:T(128)} %bitcast.4.upper_ref, bf16[136,896]{1,0:T(8,128)(2,1)S(1)} %get-tuple-element.32.refs_0_, ...), custom_call_target="tpu_custom_call" | custom-call | flops 763363328 | bytes 7340032 | tf_op jit(solution)/shard_map/pallas_call | solution.py:350
  36.6 0.8 %collective-permute-start.10 = (bf16[2,104,1408]{2,1,0:T(8,128)(2,1)S(1)}, bf16[2,104,1408]{2,1,0:T(8,128)(2,1)S(1)}, u32[]{:S(2)}, u32[]{:S(2)}) collective-permute-start(bf16[2,104,1408]{2,1,0:T(8,128)(2,1)S(1)} %get-tuple-element.49), channel_id=1, source_target_pairs={{0,28},{4,24},{8,20},{12,16},{16,12},{20,8},{24,4},{28,0},{1,29},{... | collective-permute-start | bytes 1757192 | tf_op jit(solution)/shard_map/ppermute | solution.py:305
  37.4 1.4 %collective-permute-start.7 = (bf16[136,896]{1,0:T(8,128)(2,1)S(1)}, bf16[136,896]{1,0:T(8,128)(2,1)S(1)}, u32[]{:S(2)}, u32[]{:S(2)}) collective-permute-start(bf16[136,896]{1,0:T(8,128)(2,1)S(1)} %get-tuple-element.43), channel_id=1, source_target_pairs={{0,1},{3,2},{4,5},{7,6},{8,9},{11,10},{12,13},{15,14},{16,17},{19,... | collective-permute-start | bytes 731144 | tf_op jit(solution)/shard_map/ppermute | solution.py:299
  38.9 0.1 collective-permute-start.4
  39.0 1.8 %collective-permute-start.9 = (bf16[2,104,896]{2,1,0:T(8,128)(2,1)S(1)}, bf16[2,104,896]{2,1,0:T(8,128)(2,1)S(1)}, u32[]{:S(2)}, u32[]{:S(2)}) collective-permute-start(bf16[2,104,896]{2,1,0:T(8,128)(2,1)S(1)} %get-tuple-element.47), channel_id=1, source_target_pairs={{0,28},{4,24},{8,20},{12,16},{16,12},{20,8},{24,4},{28,0},{1,29},{... | collective-permute-start | bytes 1118216 | tf_op jit(solution)/shard_map/ppermute | solution.py:305
  40.8 0.0 collective-permute-done.6.payload_ref
  40.8 0.7 collective-permute-start.5
  41.5 0.2 shard_map.91
  41.7 2.5 %collective-permute-done.7.b_ref = bf16[136,896]{1,0:T(8,128)(2,1)S(1)} collective-permute-done((bf16[136,896]{1,0:T(8,128)(2,1)S(1)}, bf16[136,896]{1,0:T(8,128)(2,1)S(1)}, u32[]{:S(2)}, u32[]{:S(2)}) %collective-permute-start.7) | collective-permute-done | bytes 243744 | tf_op jit(solution)/shard_map/ppermute | solution.py:299
  44.2 2.2 %collective-permute-start.11 = (bf16[2,40,1792]{2,1,0:T(8,128)(2,1)S(1)}, bf16[2,40,1792]{2,1,0:T(8,128)(2,1)S(1)}, u32[]{:S(2)}, u32[]{:S(2)}) collective-permute-start(bf16[2,40,1792]{2,1,0:T(8,128)(2,1)S(1)} %get-tuple-element.51), channel_id=1, source_target_pairs={{0,28},{4,24},{8,20},{12,16},{16,12},{20,8},{24,4},{28,0},{1,29},{... | collective-permute-start | bytes 860168 | tf_op jit(solution)/shard_map/ppermute | solution.py:305
  46.3 2.4 %shard_map.92 = (bf16[2,40,512]{2,1,0:T(8,128)(2,1)S(1)}, bf16[136,896]{1,0:T(8,128)(2,1)S(1)}) custom-call(bf16[2,4,40,896]{3,2,1,0:T(8,128)(2,1)S(1)} %get-tuple-element.44.rows, bf16[3584,512]{1,0:T(8,128)(2,1)S(1)} %get-tuple-element.37.up_ref, bf16[512,3584]{1,0:T(8,128)(2,1)S(1)} %get-tuple-element.39.refs_4_.up_t_ref, ...), custom_call_target="tpu_custom_call" | custom-call | flops 381681664 | bytes 7340032 | tf_op jit(solution)/shard_map/pallas_call | solution.py:368
  48.8 0.1 shard_map.93
  48.8 0.6 collective-permute-done.4.refs_1_
  49.4 3.7 %collective-permute-start.8 = (bf16[136,896]{1,0:T(8,128)(2,1)S(1)}, bf16[136,896]{1,0:T(8,128)(2,1)S(1)}, u32[]{:S(2)}, u32[]{:S(2)}) collective-permute-start(bf16[136,896]{1,0:T(8,128)(2,1)S(1)} %shard_map.93), channel_id=1, source_target_pairs={{0,2},{1,3},{2,0},{3,1},{4,6},{5,7},{6,4},{7,5},{8,10},{9,11},{10,... | collective-permute-start | bytes 731144 | tf_op jit(solution)/shard_map/ppermute | solution.py:299
  53.1 0.0 collective-permute-done.5.refs_2_
  53.1 0.6 collective-permute-start.12
  53.7 11.3 %collective-permute-done.8.refs_3_ = bf16[136,896]{1,0:T(8,128)(2,1)S(1)} collective-permute-done((bf16[136,896]{1,0:T(8,128)(2,1)S(1)}, bf16[136,896]{1,0:T(8,128)(2,1)S(1)}, u32[]{:S(2)}, u32[]{:S(2)}) %collective-permute-start.8) | collective-permute-done | bytes 243744 | tf_op jit(solution)/shard_map/ppermute | solution.py:299
  65.0 1.1 %shard_map.94 = bf16[64,3584]{1,0:T(8,128)(2,1)} custom-call(bf16[4,80,64]{2,1,0:T(8,128)(2,1)S(1)} %get-tuple-element.29.masks_ref, bf16[136,896]{1,0:T(8,128)(2,1)S(1)} %get-tuple-element.41.refs_0_, bf16[136,896]{1,0:T(8,128)(2,1)S(1)} %collective-permute-done.4.refs_1_, bf16[136,896]{1,0:T(8,128)(2,1)S(1)} %collective-permute-done.5.refs_2_, ...), custom_call_target="tpu_custom_call" | custom-call | flops 1048576 | bytes 1048576 | tf_op jit(solution)/shard_map/pallas_call | solution.py:392
  66.1 0.0 collective-permute-done.9.refs_1_
  66.1 2.8 %collective-permute-done.12.refs_7_ = bf16[2,40,512]{2,1,0:T(8,128)(2,1)S(1)} collective-permute-done((bf16[2,40,512]{2,1,0:T(8,128)(2,1)S(1)}, bf16[2,40,512]{2,1,0:T(8,128)(2,1)S(1)}, u32[]{:S(2)}, u32[]{:S(2)}) %collective-permute-start.12) | collective-permute-done | bytes 81952 | tf_op jit(solution)/shard_map/ppermute | solution.py:305
  68.9 0.0 collective-permute-done.10.refs_3_
  68.9 0.0 collective-permute-done.11.refs_5_
  68.9 3.4 %shard_map.95 = (bf16[1792,512]{1,0:T(8,128)(2,1)}, bf16[512,1792]{1,0:T(8,128)(2,1)}) custom-call(bf16[2,104,896]{2,1,0:T(8,128)(2,1)S(1)} %get-tuple-element.46.refs_0_, bf16[2,104,896]{2,1,0:T(8,128)(2,1)S(1)} %collective-permute-done.9.refs_1_, bf16[2,104,1408]{2,1,0:T(8,128)(2,1)S(1)} %get-tuple-element.48.refs_2_, ...), custom_call_target="tpu_custom_call" | custom-call | flops 763363328 | bytes 3670016 | tf_op jit(solution)/shard_map/pallas_call | solution.py:384
  (1 shorter events, 0.0 us)
Async XLA Ops:
  2.0 12.1 %collective-permute-start.3 = (bf16[136,896]{1,0:T(8,128)(2,1)S(1)}, bf16[136,896]{1,0:T(8,128)(2,1)S(1)}, u32[]{:S(2)}, u32[]{:S(2)}) collective-permute-start(bf16[136,896]{1,0:T(8,128)(2,1)S(1)} %get-tuple-element.35.own_x), channel_id=1, source_target_pairs={{0,3},{1,2},{2,1},{3,0},{4,7},{5,6},{6,5},{7,4},{8,11},{9,10},{10,... | collective-permute-start | bytes 731144 | tf_op jit(solution)/shard_map/ppermute | solution.py:299
  7.6 11.7 %collective-permute-start.1 = (bf16[136,896]{1,0:T(8,128)(2,1)S(1)}, bf16[136,896]{1,0:T(8,128)(2,1)S(1)}, u32[]{:S(2)}, u32[]{:S(2)}) collective-permute-start(bf16[136,896]{1,0:T(8,128)(2,1)S(1)} %get-tuple-element.33.own_g), channel_id=1, source_target_pairs={{0,3},{1,2},{2,1},{3,0},{4,7},{5,6},{6,5},{7,4},{8,11},{9,10},{10,... | collective-permute-start | bytes 731144 | tf_op jit(solution)/shard_map/ppermute | solution.py:299
  7.7 21.9 %collective-permute-start.2 = (bf16[136,896]{1,0:T(8,128)(2,1)S(1)}, bf16[136,896]{1,0:T(8,128)(2,1)S(1)}, u32[]{:S(2)}, u32[]{:S(2)}) collective-permute-start(bf16[136,896]{1,0:T(8,128)(2,1)S(1)} %get-tuple-element.34.refs_0_), channel_id=1, source_target_pairs={{0,1},{1,0},{2,3},{3,2},{4,5},{5,4},{6,7},{7,6},{8,9},{9,8},{10,11... | collective-permute-start | bytes 731144 | tf_op jit(solution)/shard_map/ppermute | solution.py:299
  7.7 27.0 %collective-permute-start = (bf16[136,896]{1,0:T(8,128)(2,1)S(1)}, bf16[136,896]{1,0:T(8,128)(2,1)S(1)}, u32[]{:S(2)}, u32[]{:S(2)}) collective-permute-start(bf16[136,896]{1,0:T(8,128)(2,1)S(1)} %get-tuple-element.32.refs_0_), channel_id=1, source_target_pairs={{0,1},{1,0},{2,3},{3,2},{4,5},{5,4},{6,7},{7,6},{8,9},{9,8},{10,11... | collective-permute-start | bytes 731144 | tf_op jit(solution)/shard_map/ppermute | solution.py:299
  19.3 21.5 %collective-permute-start.6 = (bf16[2,136,896]{2,1,0:T(8,128)(2,1)S(1)}, bf16[2,136,896]{2,1,0:T(8,128)(2,1)S(1)}, u32[]{:S(2)}, u32[]{:S(2)}) collective-permute-start(bf16[2,136,896]{2,1,0:T(8,128)(2,1)S(1)} %shard_map.90), channel_id=1, source_target_pairs={{0,2},{3,1},{1,0},{2,3},{4,6},{7,5},{5,4},{6,7},{8,10},{11,9},{9,8... | collective-permute-start | bytes 1462280 | tf_op jit(solution)/shard_map/ppermute | solution.py:299
  36.6 32.2 %collective-permute-start.10 = (bf16[2,104,1408]{2,1,0:T(8,128)(2,1)S(1)}, bf16[2,104,1408]{2,1,0:T(8,128)(2,1)S(1)}, u32[]{:S(2)}, u32[]{:S(2)}) collective-permute-start(bf16[2,104,1408]{2,1,0:T(8,128)(2,1)S(1)} %get-tuple-element.49), channel_id=1, source_target_pairs={{0,28},{4,24},{8,20},{12,16},{16,12},{20,8},{24,4},{28,0},{1,29},{... | collective-permute-start | bytes 1757192 | tf_op jit(solution)/shard_map/ppermute | solution.py:305
  37.4 6.7 %collective-permute-start.7 = (bf16[136,896]{1,0:T(8,128)(2,1)S(1)}, bf16[136,896]{1,0:T(8,128)(2,1)S(1)}, u32[]{:S(2)}, u32[]{:S(2)}) collective-permute-start(bf16[136,896]{1,0:T(8,128)(2,1)S(1)} %get-tuple-element.43), channel_id=1, source_target_pairs={{0,1},{3,2},{4,5},{7,6},{8,9},{11,10},{12,13},{15,14},{16,17},{19,... | collective-permute-start | bytes 731144 | tf_op jit(solution)/shard_map/ppermute | solution.py:299
  38.9 10.5 %collective-permute-start.4 = (bf16[136,896]{1,0:T(8,128)(2,1)S(1)}, bf16[136,896]{1,0:T(8,128)(2,1)S(1)}, u32[]{:S(2)}, u32[]{:S(2)}) collective-permute-start(bf16[136,896]{1,0:T(8,128)(2,1)S(1)} %get-tuple-element.42), channel_id=1, source_target_pairs={{0,1},{1,0},{2,3},{3,2},{4,5},{5,4},{6,7},{7,6},{8,9},{9,8},{10,11... | collective-permute-start | bytes 731144 | tf_op jit(solution)/shard_map/ppermute | solution.py:299
  39.0 27.1 %collective-permute-start.9 = (bf16[2,104,896]{2,1,0:T(8,128)(2,1)S(1)}, bf16[2,104,896]{2,1,0:T(8,128)(2,1)S(1)}, u32[]{:S(2)}, u32[]{:S(2)}) collective-permute-start(bf16[2,104,896]{2,1,0:T(8,128)(2,1)S(1)} %get-tuple-element.47), channel_id=1, source_target_pairs={{0,28},{4,24},{8,20},{12,16},{16,12},{20,8},{24,4},{28,0},{1,29},{... | collective-permute-start | bytes 1118216 | tf_op jit(solution)/shard_map/ppermute | solution.py:305
  40.8 12.3 %collective-permute-start.5 = (bf16[136,896]{1,0:T(8,128)(2,1)S(1)}, bf16[136,896]{1,0:T(8,128)(2,1)S(1)}, u32[]{:S(2)}, u32[]{:S(2)}) collective-permute-start(bf16[136,896]{1,0:T(8,128)(2,1)S(1)} %get-tuple-element.43), channel_id=1, source_target_pairs={{1,2},{2,1},{5,6},{6,5},{9,10},{10,9},{13,14},{14,13},{17,18},{18,... | collective-permute-start | bytes 731144 | tf_op jit(solution)/shard_map/ppermute | solution.py:299
  44.2 24.7 %collective-permute-start.11 = (bf16[2,40,1792]{2,1,0:T(8,128)(2,1)S(1)}, bf16[2,40,1792]{2,1,0:T(8,128)(2,1)S(1)}, u32[]{:S(2)}, u32[]{:S(2)}) collective-permute-start(bf16[2,40,1792]{2,1,0:T(8,128)(2,1)S(1)} %get-tuple-element.51), channel_id=1, source_target_pairs={{0,28},{4,24},{8,20},{12,16},{16,12},{20,8},{24,4},{28,0},{1,29},{... | collective-permute-start | bytes 860168 | tf_op jit(solution)/shard_map/ppermute | solution.py:305
  49.4 15.6 %collective-permute-start.8 = (bf16[136,896]{1,0:T(8,128)(2,1)S(1)}, bf16[136,896]{1,0:T(8,128)(2,1)S(1)}, u32[]{:S(2)}, u32[]{:S(2)}) collective-permute-start(bf16[136,896]{1,0:T(8,128)(2,1)S(1)} %shard_map.93), channel_id=1, source_target_pairs={{0,2},{1,3},{2,0},{3,1},{4,6},{5,7},{6,4},{7,5},{8,10},{9,11},{10,... | collective-permute-start | bytes 731144 | tf_op jit(solution)/shard_map/ppermute | solution.py:299
  53.1 15.8 %collective-permute-start.12 = (bf16[2,40,512]{2,1,0:T(8,128)(2,1)S(1)}, bf16[2,40,512]{2,1,0:T(8,128)(2,1)S(1)}, u32[]{:S(2)}, u32[]{:S(2)}) collective-permute-start(bf16[2,40,512]{2,1,0:T(8,128)(2,1)S(1)} %get-tuple-element.52.refs_6_), channel_id=1, source_target_pairs={{0,28},{4,24},{8,20},{12,16},{16,12},{20,8},{24,4},{28,0},{1,29},{... | collective-permute-start | bytes 245768 | tf_op jit(solution)/shard_map/ppermute | solution.py:305

commit v4 on v3

--- a/solution.py
+++ b/solution.py
@@ -15,7 +15,7 @@
 REM = CAP - MAIN
 CHUNKS = FOLD // REM
 LINE = 4
-VMEM_LIMIT = 24 * 1024 * 1024
+VMEM_LIMIT = 12 * 1024 * 1024
 F32 = jnp.float32
 BF16 = jnp.bfloat16
 
@@ -147,33 +147,41 @@
     send_ref[...] = rows[pl.ds((1 - upper) * half, half)]
 
 
-def times_up(rows, up_ref):
-    width = rows.shape[2]
-    return sum(dot(rows[chunk], up_ref[chunk * width:(chunk + 1) * width, :]) for chunk in range(CHUNKS))
-
-
-def hidden_values(rows, pre, down_ref):
-    width = rows.shape[2]
-    dact = sum(dot(rows[chunk], down_ref[chunk * width:(chunk + 1) * width, :]) for chunk in range(CHUNKS))
+def chunk_of(blocks, chunk):
+    return jnp.concatenate([ref[chunk] for ref in blocks], axis=0) if len(blocks) > 1 else blocks[0][chunk]
+
+
+def times_up(blocks, up_ref):
+    width = blocks[0].shape[2]
+    return sum(dot(chunk_of(blocks, chunk), up_ref[chunk * width:(chunk + 1) * width, :]) for chunk in range(CHUNKS))
+
+
+def hidden_values(blocks, pre, down_ref):
+    width = blocks[0].shape[2]
+    dact = sum(dot(chunk_of(blocks, chunk), down_ref[chunk * width:(chunk + 1) * width, :]) for chunk in range(CHUNKS))
     sigma = 1.0 / (1.0 + jnp.exp(-pre))
     return (dact * sigma * (1.0 + pre * (1.0 - sigma))).astype(BF16), (pre * sigma).astype(BF16)
 
 
-def back_rows(dpre, up_ref, outs):
-    size = len(outs)
+def back_rows(dpre, up_ref, blocks):
     width = up_ref.shape[1] // CHUNKS
-    folds = None
+    folds = [None] * len(blocks)
     for chunk in range(CHUNKS):
         part = dot(dpre, up_ref[:, chunk * width:(chunk + 1) * width]).astype(BF16)
-        for r in range(size):
-            outs[r][chunk * MAIN:(chunk + 1) * MAIN, :] = part[r * MAIN:(r + 1) * MAIN]
-        fold = dot(fold_pick(size, chunk), part[size * MAIN:], ((0,), (0,)))
-        folds = fold if folds is None else folds + fold
-    for r in range(size):
-        outs[r][CHUNKS * MAIN:, :] = folds[r * FOLD:(r + 1) * FOLD].astype(BF16)
-
-
-def pre_kernel(size, upper_ref, *refs):
+        base = 0
+        for number, outs in enumerate(blocks):
+            size = len(outs)
+            for r in range(size):
+                outs[r][chunk * MAIN:(chunk + 1) * MAIN, :] = part[base + r * MAIN:base + (r + 1) * MAIN]
+            fold = dot(fold_pick(size, chunk), part[base + size * MAIN:base + row_count(size)], ((0,), (0,)))
+            folds[number] = fold if folds[number] is None else folds[number] + fold
+            base += row_count(size)
+    for outs, fold in zip(blocks, folds):
+        for r, out in enumerate(outs):
+            out[CHUNKS * MAIN:, :] = fold[r * FOLD:(r + 1) * FOLD].astype(BF16)
+
+
+def pre_kernel(size, upper_ref, first_ref, *refs):
     payloads, (up_hbm, down_hbm, pre_ref, keep_ref, send_ref, up_ref, down_ref, rows, sems) = refs[:size], refs[size:]
     load_up = pltpu.make_async_copy(up_hbm, up_ref, sems.at[0])
     load_down = pltpu.make_async_copy(down_hbm, down_ref, sems.at[1])
@@ -182,8 +190,14 @@
     join_rows(payloads, rows)
     pick_halves(upper_ref, rows, keep_ref, send_ref)
     load_up.wait()
-    pre_ref[...] = times_up(rows, up_ref)
+    pre_ref[...] = times_up([first_ref.at[0], rows], up_ref)
     load_down.wait()
+
+
+def join_kernel(size, upper_ref, *refs):
+    payloads, (rows_ref, keep_ref, send_ref) = refs[:size], refs[size:]
+    join_rows(payloads, rows_ref)
+    pick_halves(upper_ref, rows_ref, keep_ref, send_ref)
 
 
 def flip_kernel(up_ref, down_ref, up_out, down_out):
@@ -194,66 +208,70 @@
         down_out[at, :] = down_ref[:, at].T
 
 
-def group_kernel(size, upper_ref, *refs):
-    payloads, (pre_ref, up_ref, down_ref, keep_ref, send_ref) = refs[:size], refs[size:size + 5]
-    outs, rows = refs[size + 5:-1], refs[-1]
-    join_rows(payloads, rows)
-    width = rows.shape[2]
-    pick_halves(upper_ref, rows, keep_ref.at[:, :, :width], send_ref.at[:, :, :width])
-    values = hidden_values(rows, pre_ref[...], down_ref)
-    for ref in (keep_ref, send_ref):
-        for plane in range(2):
-            ref[plane, :, width:] = values[plane]
-    back_rows(values[0], up_ref, outs)
-
-
-def pick_kernel(upper_ref, payload_ref, keep_ref, send_ref, rows):
+def group_kernel(first_ref, rows_ref, pre_ref, up_ref, down_ref, hidden_ref, *outs):
+    hidden_ref[0], hidden_ref[1] = hidden_values([first_ref.at[1], rows_ref], pre_ref[...], down_ref)
+    back_rows(hidden_ref[0], up_ref, [outs[:1], outs[1:]])
+
+
+def pick_kernel(upper_ref, *refs):
+    payloads, (keep_ref, send_ref, rows) = refs[:-3], refs[-3:]
+    if len(payloads) == 1:
+        payloads = [payloads[0].at[t] for t in range(2)]
     width = rows.shape[3]
     for t in range(2):
-        join_rows([payload_ref.at[t]], rows.at[t])
+        join_rows([payloads[t]], rows.at[t])
         at = slice(t * width, (t + 1) * width)
         pick_halves(upper_ref, rows.at[t], keep_ref.at[:, :, at], send_ref.at[:, :, at])
 
 
 def last_kernel(rows, up_ref, up_t_ref, down_t_ref, hidden_ref, out_ref):
-    values = hidden_values(rows.at[1], times_up(rows.at[0], up_ref), down_t_ref)
+    values = hidden_values([rows.at[1]], times_up([rows.at[0]], up_ref), down_t_ref)
     for plane in range(2):
         hidden_ref[plane] = values[plane]
-    back_rows(values[0], up_t_ref, [out_ref])
-
-
-def relay_kernel(inner_ref, own_x, own_g, passed_x, passed_g, out_ref):
-    @pl.when(inner_ref[0] == 1)
-    def _():
-        out_ref[0] = passed_x[...]
-        out_ref[1] = passed_g[...]
-
-    @pl.when(inner_ref[0] == 0)
-    def _():
-        out_ref[0] = own_x[...]
-        out_ref[1] = own_g[...]
+    back_rows(values[0], up_t_ref, [[out_ref]])
+
+
+def stack_kernel(a_ref, b_ref, out_ref):
+    out_ref[0] = a_ref[...]
+    out_ref[1] = b_ref[...]
 
 
 def add_kernel(a_ref, b_ref, out_ref):
     out_ref[...] = (a_ref[...].astype(F32) + b_ref[...].astype(F32)).astype(BF16)
 
 
-def grad_kernel(with_last, *refs):
-    up_ref, down_ref = refs[-2:]
-    xs, packs = refs[0:2], refs[2:4]
-    lasts, hiddens = (refs[4:6], refs[6:8]) if with_last else ((), ())
-    width = xs[0].shape[2]
-    chunk = pl.program_id(0)
-    across = ((0,), (0,))
-
-    def joined(pieces):
-        return jnp.concatenate(pieces, axis=0)
-
-    x = joined([ref[0] for ref in xs] + [ref[chunk, :, :width] for ref in lasts])
-    g = joined([ref[chunk, :, :width] for ref in packs] + [ref[chunk, :, width:] for ref in lasts])
-    dpre, act = (joined([ref[t, :, width:] for ref in packs] + [ref[t] for ref in hiddens]) for t in range(2))
-    up_ref[...] = dot(x, dpre, across).astype(BF16)
-    down_ref[...] = dot(act, g, across).astype(BF16)
+ACROSS_ROWS = ((0,), (0,))
+
+
+def grad_kernel(own_keep, own_far, x_keep, x_far, g_keep, g_far, hid, hid_far, up_ref, down_ref):
+    width = x_keep.shape[2]
+    dpre, act = (jnp.concatenate([ref[t] for ref in (hid, hid_far)], axis=0) for t in range(2))
+    for chunk in range(x_keep.shape[0]):
+        x, g = (
+            jnp.concatenate([own_keep[chunk, :, at], keep[chunk], own_far[chunk, :, at], far[chunk]], axis=0)
+            for keep, far, at in ((x_keep, x_far, slice(0, width)), (g_keep, g_far, slice(width, 2 * width)))
+        )
+        up_ref[chunk] = dot(x, dpre, ACROSS_ROWS).astype(up_ref.dtype)
+        down_ref[chunk] = dot(act, g, ACROSS_ROWS).astype(down_ref.dtype)
+
+
+def grad_last_kernel(up_part, down_part, keep, far, hid, hid_far, up_hbm, down_hbm, up_out, down_out, sems):
+    width = keep.shape[2] // 2
+    dpre, act = (jnp.concatenate([ref[t] for ref in (hid, hid_far)], axis=0) for t in range(2))
+    copies = []
+    for chunk in range(keep.shape[0]):
+        x, g = (
+            jnp.concatenate([ref[chunk, :, t * width:(t + 1) * width] for ref in (keep, far)], axis=0) for t in range(2)
+        )
+        at = slice(chunk * width, (chunk + 1) * width)
+        up_out[chunk] = (up_part[chunk] + dot(x, dpre, ACROSS_ROWS)).astype(BF16)
+        copies.append(pltpu.make_async_copy(up_out.at[chunk], up_hbm.at[at, :], sems.at[2 * chunk]))
+        copies[-1].start()
+        down_out[chunk] = (down_part[chunk] + dot(act, g, ACROSS_ROWS)).astype(BF16)
+        copies.append(pltpu.make_async_copy(down_out.at[chunk], down_hbm.at[:, at], sems.at[2 * chunk + 1]))
+        copies[-1].start()
+    for copy in copies:
+        copy.wait()
 
 
 def final_kernel(own_count, masks_ref, *refs):
@@ -284,16 +302,19 @@
     up, down = up_weight[0], down_weight[0]
 
     line = owners == LINE
-    sources = [0, 1, 3] if line else list(range(owners))
+    sources = [1, 2] if line else list(range(1, owners))
     size = len(sources)
-    rows = row_count(size)
+    one = row_count(1)
+    rows = one + row_count(size)
 
     def held(shape, dtype=BF16):
         return pltpu.VMEM(shape, dtype)
 
     payload_shape = (CHUNKS * MAIN + FOLD, width)
     payload = held(payload_shape)
-    halves = held((half, rows, width))
+    halves = held((half, row_count(size), width))
+    pair = held((half, one, 2 * width))
+    pair_rows = held((2, CHUNKS, one, width))
 
     def send(value, pairs):
         return lax.ppermute(value, "expert", pairs)
@@ -316,82 +337,91 @@
     g_own, g_other = call(
         route_g_kernel, (payload, payload), small, small, in_specs=[vmem()] * 3, out_specs=(vmem(),) * 2
     )(masks, gate, cot)
+    own_keep, own_sent, own_rows = call(
+        pick_kernel, (pair, pair, pair_rows), small, small, in_specs=[smem()] + [vmem()] * 2, out_specs=(vmem(),) * 3
+    )(upper, x_own, g_own)
+    own_far = mirror(own_sent)
     if line:
-        x_across, x_beside = swap(x_other, 3), swap(x_own, 1)
-        g_across, g_beside = swap(g_other, 3), swap(g_own, 1)
-        x_parts, g_parts = [x_own, x_beside, x_across], [g_own, g_beside, g_across]
+        x_across, x_beside = swap(x_other, 2), swap(x_own, 1)
+        g_across, g_beside = swap(g_other, 2), swap(g_own, 1)
+        x_parts, g_parts = [x_beside, x_across], [g_beside, g_across]
     else:
         x_parts, g_parts = (
-            [own] + [swap(own if r < group else other, r) for r in range(1, owners)]
+            [swap(own if r < group else other, r) for r in range(1, owners)]
             for own, other in ((x_own, x_other), (g_own, g_other))
         )
 
     flops = 2 * rows * model * hidden
     moved = 2 * model * hidden
-    pre, x_keep, x_send, up_here, down_here = call(
+    pre, x_keep, x_sent, up_here, down_here = call(
         functools.partial(pre_kernel, size),
         (held((rows, hidden), F32), halves, halves, held((model, hidden)), held((hidden, model))),
         flops, moved,
-        in_specs=[smem()] + [vmem()] * size + [hbm()] * 2,
+        in_specs=[smem()] + [vmem()] * (size + 1) + [hbm()] * 2,
         out_specs=(vmem(),) * 5,
-        scratch_shapes=[pltpu.VMEM((CHUNKS, rows, width), BF16), pltpu.SemaphoreType.DMA((2,))],
-    )(upper, *x_parts, in_hbm(up), in_hbm(down))
+        scratch_shapes=[pltpu.VMEM((CHUNKS, row_count(size), width), BF16), pltpu.SemaphoreType.DMA((2,))],
+    )(upper, own_rows, *x_parts, in_hbm(up), in_hbm(down))
     if line:
-        inner = jnp.logical_and(here > 0, here < owners - 1).astype(jnp.int32).reshape(1)
-        relayed = call(
-            relay_kernel, held((2,) + payload_shape), small, small, in_specs=[smem()] + [vmem()] * 4, out_specs=vmem()
-        )(inner, x_other, g_other, x_across, g_across)
-        relayed = send(relayed, [(0, 2), (3, 1), (1, 0), (2, 3)])
-    x_far = mirror(x_send)
+        passed = call(stack_kernel, held((2,) + payload_shape), small, small, in_specs=[vmem()] * 2, out_specs=vmem())(
+            x_across, g_across
+        )
+        passed = swap(passed, 1)
+    x_far = mirror(x_sent)
     up_t, down_t = call(
         flip_kernel, (held((hidden, model)), held((model, hidden))), small, moved, in_specs=[vmem()] * 2, out_specs=(vmem(),) * 2
     )(up_here, down_here)
-    pack = held((2, rows, width + hidden))
-    keep, sent, *parts = call(
-        functools.partial(group_kernel, size), (pack, pack) + (payload,) * size, 2 * flops, 2 * moved,
-        in_specs=[smem()] + [vmem()] * (size + 3),
-        out_specs=(vmem(),) * (size + 2),
-        scratch_shapes=[pltpu.VMEM((CHUNKS, rows, width), BF16)],
-    )(upper, *g_parts, pre, up_t, down_t)
-    back = dict(zip(sources, parts))
-    for_grad = [x_keep, x_far, keep, mirror(sent)]
+    g_rows, g_keep, g_sent = call(
+        functools.partial(join_kernel, size), (held((CHUNKS, row_count(size), width)), halves, halves), small, small,
+        in_specs=[smem()] + [vmem()] * size, out_specs=(vmem(),) * 3,
+    )(upper, *g_parts)
+    g_far = mirror(g_sent)
+    hid, *parts = call(
+        group_kernel, (held((2, rows, hidden)),) + (payload,) * (size + 1), 2 * flops, 2 * moved,
+        in_specs=[vmem()] * 5, out_specs=(vmem(),) * (size + 2),
+    )(own_rows, g_rows, pre, up_t, down_t)
+    back = dict(zip([0] + sources, parts))
+    for_grad = [own_keep, own_far, x_keep, x_far, g_keep, g_far, hid, mirror(hid)]
 
     if line:
-        one = row_count(1)
-        pack = held((2, one, 2 * width))
         last_keep, last_sent, last_rows = call(
-            pick_kernel, (pack, pack, held((2, CHUNKS, one, width))), small, small,
+            pick_kernel, (pair, pair, pair_rows), small, small,
             in_specs=[smem(), vmem()],
             out_specs=(vmem(),) * 3,
-        )(upper, relayed)
+        )(upper, passed)
         last_far = mirror(last_sent)
         last_hidden, last_back = call(
             last_kernel, (held((2, one, hidden)), payload), flops, 2 * moved,
             in_specs=[vmem()] * 4,
             out_specs=(vmem(),) * 2,
         )(last_rows, up_here, up_t, down_t)
-        for_grad += [last_keep, last_far, last_hidden, mirror(last_hidden)]
-        for_far = send(back[3], [(0, 1), (3, 2)])
-        across = send(back[3], [(1, 2), (2, 1)])
+        for_last = [last_keep, last_far, last_hidden, mirror(last_hidden)]
+        for_far = swap(back[2], 1)
         both = call(add_kernel, payload, small, small, in_specs=[vmem()] * 2, out_specs=vmem())(last_back, for_far)
-        skipped = swap(both, 2)
-        own_side, other_side = [back[0], swap(back[1], 1)], [across, skipped]
+        own_side, other_side = [back[0], swap(back[1], 1)], [swap(both, 3)]
     else:
         got = [back[0]] + [swap(back[r], r) for r in range(1, owners)]
         own_side, other_side = got[:group], got[group:]
 
-    x_chunk = pl.BlockSpec((1, rows, width), lambda k: (k, 0, 0))
+    kept = F32 if line else BF16
     grad_up, grad_down = call(
-        functools.partial(grad_kernel, line),
-        (jax.ShapeDtypeStruct((model // 2, hidden), BF16), jax.ShapeDtypeStruct((hidden, model // 2), BF16)),
-        2 * flops, moved,
-        grid=(half,),
-        in_specs=[x_chunk, x_chunk] + [vmem()] * (len(for_grad) - 2),
-        out_specs=(pl.BlockSpec((width, hidden), lambda k: (k, 0)), pl.BlockSpec((hidden, width), lambda k: (0, k))),
+        grad_kernel, (held((half, width, hidden), kept), held((half, hidden, width), kept)), 2 * flops, moved,
+        in_specs=[vmem()] * 8, out_specs=(vmem(),) * 2,
     )(*for_grad)
+    if line:
+        grad_up, grad_down = call(
+            grad_last_kernel,
+            (jax.ShapeDtypeStruct((model // 2, hidden), BF16), jax.ShapeDtypeStruct((hidden, model // 2), BF16)),
+            flops, moved,
+            in_specs=[vmem()] * 6, out_specs=(hbm(),) * 2,
+            scratch_shapes=[
+                pltpu.VMEM((half, width, hidden), BF16), pltpu.VMEM((half, hidden, width), BF16), pltpu.SemaphoreType.DMA((2 * half,))
+            ],
+        )(grad_up, grad_down, *for_last)
+    else:
+        grad_up, grad_down = grad_up.reshape(model // 2, hidden), grad_down.transpose(1, 0, 2).reshape(hidden, model // 2)
     input_grad = call(
         functools.partial(final_kernel, len(own_side)), jax.ShapeDtypeStruct((tok, model), BF16), small, small,
-        in_specs=[vmem()] * (owners + 1), out_specs=vmem(),
+        in_specs=[vmem()] * (1 + len(own_side) + len(other_side)), out_specs=vmem(),
     )(masks, *own_side, *other_side)
     return (input_grad[None], grad_up[None], grad_down[None])
 

time: 72.5 us -> 70.1 us (0.967)
  starting transfers between devices: 28.9 us -> 20.5 us
  waiting for transfers between devices: 26.6 us -> 32.1 us
    ppermute x9 -> x8, starting transfers between devices: 23.5 us -> 12.4 us  [send(): return lax.ppermute(value, 'expert', pairs)]
    ppermute x9 -> x8, waiting for transfers between devices: 23.9 us -> 31.2 us  [send(): return lax.ppermute(value, 'expert', pairs)]
    ppermute x4 -> x6, starting transfers between devices: 5.41 us -> 8.18 us  [mirror(): lax.ppermute(value, 'pipe', [(i, ranks - 1 - i) for i in range(ranks)])]
    ppermute x4 -> x6, waiting for transfers between devices: 2.78 us -> 0.86 us  [mirror(): lax.ppermute(value, 'pipe', [(i, ranks - 1 - i) for i in range(ranks)])]
    pallas_call x4 -> x7, Pallas kernels: 5.6 us -> 6.11 us  [the longest x1 2.29 us: per_device(): call(grad_last_kernel, (jax.ShapeDtypeStruct((model // 2, hidden), BF16),...]
  transfers between devices with their start and end apart: 13 -> 14, of which waited for: 6 -> 5; matrix products, arithmetic and copies ran while one was open for 0% -> 0% of each run, Pallas kernels for 16% -> 18%
where the time goes in v4:
time: 70.1 us; the launch traced here: 69.9 us
  waiting for transfers between devices  32.1 us (46%)
  starting transfers between devices  20.5 us (29%)
  Pallas kernels  16.6 us (24%)
  between operations  0.75 us (1%)
    ppermute x8, waiting for transfers between devices, send(): return lax.ppermute(value, 'expert', pairs)  31.2 us
    ppermute x8, starting transfers between devices, send(): return lax.ppermute(value, 'expert', pairs)  12.4 us
    ppermute x6, starting transfers between devices, mirror(): lax.ppermute(value, 'pipe', [(i, ranks - 1 - i) for i in range(ranks)])  8.18 us
    pallas_call x1, Pallas kernels, per_device(): call(functools.partial(pre_kernel, size), (held((rows, hidden), F32), hal...  3.18 us
    pallas_call x1, Pallas kernels, per_device(): call(last_kernel, (held((2, one, hidden)), payload), flops, 2 * moved, in...  2.41 us
    pallas_call x1, Pallas kernels, per_device(): call(grad_last_kernel, (jax.ShapeDtypeStruct((model // 2, hidden), BF16),...  2.29 us
    pallas_call x1, Pallas kernels, per_device(): call(flip_kernel, (held((hidden, model)), held((model, hidden))), small,...  1.94 us
    pallas_call x1, Pallas kernels, per_device(): call(group_kernel, (held((2, rows, hidden)),) + (payload,) * (size + 1),...  1.85 us
  transfers between devices with their start and end apart: 14, of which 5 were waited for; matrix products, arithmetic and copies ran while one was open for 0% of the time, Pallas kernels for 18%

profile of v4, /device:TPU:0, one launch (start us, length us, event | category | flops | bytes accessed | tf_op | source)
XLA Modules:
  0.0 69.9 jit_solution(10781719183800656931)
XLA Ops:
  0.6 1.4 %shard_map.85 = (bf16[136,896]{1,0:T(8,128)(2,1)S(1)}, bf16[136,896]{1,0:T(8,128)(2,1)S(1)}, bf16[4,80,64]{2,1,0:T(8,128)(2,1)S(1)}, f32[1,64]{1,0:T(1,128)S(1)}, bf16[64,3584]{1,0:T(8,128)(2,1)S(1)}) custom-call(s32[1]{0:T(128)} %bitcast.mine_ref, s32[1,64]{1,0:T(1,128)} %bitcast.15, f32[1,64]{1,0:T(1,128)} %gate_hbm.1, bf16[64,3584]{1,0:T(8,128)(2,1)} %bitcast.12, ...), custom_call_target="tpu_custom_call" | custom-call | flops 1048576 | bytes 1048576 | tf_op jit(solution)/shard_map/pallas_call | solution.py:329
  2.0 0.4 shard_map.86
  2.4 4.1 %collective-permute-start.1 = (bf16[136,896]{1,0:T(8,128)(2,1)S(1)}, bf16[136,896]{1,0:T(8,128)(2,1)S(1)}, u32[]{:S(2)}, u32[]{:S(2)}) collective-permute-start(bf16[136,896]{1,0:T(8,128)(2,1)S(1)} %get-tuple-element.42), channel_id=1, source_target_pairs={{0,2},{1,3},{2,0},{3,1},{4,6},{5,7},{6,4},{7,5},{8,10},{9,11},{10,... | collective-permute-start | bytes 731144 | tf_op jit(solution)/shard_map/ppermute | solution.py:320
  6.6 0.1 collective-permute-start.3
  6.6 1.8 %collective-permute-start.2 = (bf16[136,896]{1,0:T(8,128)(2,1)S(1)}, bf16[136,896]{1,0:T(8,128)(2,1)S(1)}, u32[]{:S(2)}, u32[]{:S(2)}) collective-permute-start(bf16[136,896]{1,0:T(8,128)(2,1)S(1)} %get-tuple-element.37.refs_0_), channel_id=1, source_target_pairs={{0,1},{1,0},{2,3},{3,2},{4,5},{5,4},{6,7},{7,6},{8,9},{9,8},{10,11... | collective-permute-start | bytes 731144 | tf_op jit(solution)/shard_map/ppermute | solution.py:320
  8.5 0.2 collective-permute-start
  8.7 15.2 %collective-permute-done.1.refs_1_.b_ref = bf16[136,896]{1,0:T(8,128)(2,1)S(1)} collective-permute-done((bf16[136,896]{1,0:T(8,128)(2,1)S(1)}, bf16[136,896]{1,0:T(8,128)(2,1)S(1)}, u32[]{:S(2)}, u32[]{:S(2)}) %collective-permute-start.1) | collective-permute-done | bytes 243744 | tf_op jit(solution)/shard_map/ppermute | solution.py:320
  23.9 4.4 %collective-permute-done.3.refs_1_.a_ref = bf16[136,896]{1,0:T(8,128)(2,1)S(1)} collective-permute-done((bf16[136,896]{1,0:T(8,128)(2,1)S(1)}, bf16[136,896]{1,0:T(8,128)(2,1)S(1)}, u32[]{:S(2)}, u32[]{:S(2)}) %collective-permute-start.3) | collective-permute-done | bytes 243744 | tf_op jit(solution)/shard_map/ppermute | solution.py:320
  28.3 0.7 %collective-permute-start.5 = (bf16[2,136,896]{2,1,0:T(8,128)(2,1)S(1)}, bf16[2,136,896]{2,1,0:T(8,128)(2,1)S(1)}, u32[]{:S(2)}, u32[]{:S(2)}) collective-permute-start(bf16[2,136,896]{2,1,0:T(8,128)(2,1)S(1)} %shard_map.92), channel_id=1, source_target_pairs={{0,1},{1,0},{2,3},{3,2},{4,5},{5,4},{6,7},{7,6},{8,9},{9,8},{10,11... | collective-permute-start | bytes 1462280 | tf_op jit(solution)/shard_map/ppermute | solution.py:320
  29.0 0.2 shard_map.87
  29.3 1.8 %collective-permute-start.8 = (bf16[2,40,1792]{2,1,0:T(8,128)(2,1)S(1)}, bf16[2,40,1792]{2,1,0:T(8,128)(2,1)S(1)}, u32[]{:S(2)}, u32[]{:S(2)}) collective-permute-start(bf16[2,40,1792]{2,1,0:T(8,128)(2,1)S(1)} %get-tuple-element.56), channel_id=1, source_target_pairs={{0,28},{4,24},{8,20},{12,16},{16,12},{20,8},{24,4},{28,0},{1,29},{... | collective-permute-start | bytes 860168 | tf_op jit(solution)/shard_map/ppermute | solution.py:326
  31.1 0.0 collective-permute-done.2.refs_0_
  31.1 3.2 %shard_map.89 = (f32[112,512]{1,0:T(8,128)S(1)}, bf16[2,72,896]{2,1,0:T(8,128)(2,1)S(1)}, bf16[2,72,896]{2,1,0:T(8,128)(2,1)S(1)}, bf16[3584,512]{1,0:T(8,128)(2,1)S(1)}, bf16[512,3584]{1,0:T(8,128)(2,1)S(1)}) custom-call(s32[1]{0:T(128)} %bitcast.4.upper_ref, bf16[2,4,40,896]{3,2,1,0:T(8,128)(2,1)S(1)} %get-tuple-element.41.first_ref, ...), custom_call_target="tpu_custom_call" | custom-call | flops 411041792 | bytes 3670016 | tf_op jit(solution)/shard_map/pallas_call | solution.py:356
  34.3 1.9 %shard_map.90 = (bf16[512,3584]{1,0:T(8,128)(2,1)S(1)}, bf16[3584,512]{1,0:T(8,128)(2,1)S(1)}) custom-call(bf16[3584,512]{1,0:T(8,128)(2,1)S(1)} %get-tuple-element.46.up_ref, bf16[512,3584]{1,0:T(8,128)(2,1)S(1)} %get-tuple-element.47.down_ref), custom_call_target="tpu_custom_call" | custom-call | flops 1048576 | bytes 3670016 | tf_op jit(solution)/shard_map/pallas_call | solution.py:370
  36.3 0.0 collective-permute-done.refs_0_
  36.3 0.2 shard_map.88
  36.5 1.8 %shard_map.91 = (bf16[2,112,512]{2,1,0:T(8,128)(2,1)S(1)}, bf16[136,896]{1,0:T(8,128)(2,1)S(1)}, bf16[136,896]{1,0:T(8,128)(2,1)S(1)}, bf16[136,896]{1,0:T(8,128)(2,1)S(1)}) custom-call(bf16[2,4,40,896]{3,2,1,0:T(8,128)(2,1)S(1)} %get-tuple-element.41.first_ref, bf16[4,72,896]{2,1,0:T(8,128)(2,1)S(1)} %get-tuple-element.43.rows_ref, ...), custom_call_target="tpu_custom_call" | custom-call | flops 822083584 | bytes 7340032 | tf_op jit(solution)/shard_map/pallas_call | solution.py:378
  38.3 0.4 collective-permute-start.6
  38.7 1.6 %collective-permute-start.11 = (bf16[2,112,512]{2,1,0:T(8,128)(2,1)S(1)}, bf16[2,112,512]{2,1,0:T(8,128)(2,1)S(1)}, u32[]{:S(2)}, u32[]{:S(2)}) collective-permute-start(bf16[2,112,512]{2,1,0:T(8,128)(2,1)S(1)} %get-tuple-element.61.hid), channel_id=1, source_target_pairs={{0,28},{4,24},{8,20},{12,16},{16,12},{20,8},{24,4},{28,0},{1,29},{... | collective-permute-start | bytes 688136 | tf_op jit(solution)/shard_map/ppermute | solution.py:326
  40.3 1.1 %collective-permute-start.9 = (bf16[2,72,896]{2,1,0:T(8,128)(2,1)S(1)}, bf16[2,72,896]{2,1,0:T(8,128)(2,1)S(1)}, u32[]{:S(2)}, u32[]{:S(2)}) collective-permute-start(bf16[2,72,896]{2,1,0:T(8,128)(2,1)S(1)} %get-tuple-element.58), channel_id=1, source_target_pairs={{0,28},{4,24},{8,20},{12,16},{16,12},{20,8},{24,4},{28,0},{1,29},{... | collective-permute-start | bytes 774152 | tf_op jit(solution)/shard_map/ppermute | solution.py:326
  41.4 0.0 collective-permute-done.5.refs_0_
  41.4 1.6 %collective-permute-start.10 = (bf16[2,72,896]{2,1,0:T(8,128)(2,1)S(1)}, bf16[2,72,896]{2,1,0:T(8,128)(2,1)S(1)}, u32[]{:S(2)}, u32[]{:S(2)}) collective-permute-start(bf16[2,72,896]{2,1,0:T(8,128)(2,1)S(1)} %get-tuple-element.60), channel_id=1, source_target_pairs={{0,28},{4,24},{8,20},{12,16},{16,12},{20,8},{24,4},{28,0},{1,29},{... | collective-permute-start | bytes 774152 | tf_op jit(solution)/shard_map/ppermute | solution.py:326
  43.0 0.2 shard_map.93
  43.2 3.7 %collective-permute-done.6.b_ref = bf16[136,896]{1,0:T(8,128)(2,1)S(1)} collective-permute-done((bf16[136,896]{1,0:T(8,128)(2,1)S(1)}, bf16[136,896]{1,0:T(8,128)(2,1)S(1)}, u32[]{:S(2)}, u32[]{:S(2)}) %collective-permute-start.6) | collective-permute-done | bytes 243744 | tf_op jit(solution)/shard_map/ppermute | solution.py:320
  47.0 0.2 collective-permute-start.12
  47.2 2.4 %shard_map.94 = (bf16[2,40,512]{2,1,0:T(8,128)(2,1)S(1)}, bf16[136,896]{1,0:T(8,128)(2,1)S(1)}) custom-call(bf16[2,4,40,896]{3,2,1,0:T(8,128)(2,1)S(1)} %get-tuple-element.52.rows, bf16[3584,512]{1,0:T(8,128)(2,1)S(1)} %get-tuple-element.46.up_ref, bf16[512,3584]{1,0:T(8,128)(2,1)S(1)} %get-tuple-element.48.up_ref.up_t_ref, ...), custom_call_target="tpu_custom_call" | custom-call | flops 411041792 | bytes 7340032 | tf_op jit(solution)/shard_map/pallas_call | solution.py:392
  49.6 0.1 shard_map.95
  49.7 0.0 collective-permute-done.8.own_far
  49.7 1.4 %collective-permute-start.4 = (bf16[136,896]{1,0:T(8,128)(2,1)S(1)}, bf16[136,896]{1,0:T(8,128)(2,1)S(1)}, u32[]{:S(2)}, u32[]{:S(2)}) collective-permute-start(bf16[136,896]{1,0:T(8,128)(2,1)S(1)} %get-tuple-element.51), channel_id=1, source_target_pairs={{0,1},{1,0},{2,3},{3,2},{4,5},{5,4},{6,7},{7,6},{8,9},{9,8},{10,11... | collective-permute-start | bytes 731144 | tf_op jit(solution)/shard_map/ppermute | solution.py:320
  51.1 0.0 collective-permute-done.11.hid_far
  51.1 3.5 %collective-permute-start.7 = (bf16[136,896]{1,0:T(8,128)(2,1)S(1)}, bf16[136,896]{1,0:T(8,128)(2,1)S(1)}, u32[]{:S(2)}, u32[]{:S(2)}) collective-permute-start(bf16[136,896]{1,0:T(8,128)(2,1)S(1)} %shard_map.95), channel_id=1, source_target_pairs={{0,3},{1,2},{2,1},{3,0},{4,7},{5,6},{6,5},{7,4},{8,11},{9,10},{10,... | collective-permute-start | bytes 731144 | tf_op jit(solution)/shard_map/ppermute | solution.py:320
  54.6 0.0 collective-permute-done.9.x_far
  54.6 1.9 %collective-permute-start.13 = (bf16[2,40,512]{2,1,0:T(8,128)(2,1)S(1)}, bf16[2,40,512]{2,1,0:T(8,128)(2,1)S(1)}, u32[]{:S(2)}, u32[]{:S(2)}) collective-permute-start(bf16[2,40,512]{2,1,0:T(8,128)(2,1)S(1)} %get-tuple-element.66.hid), channel_id=1, source_target_pairs={{0,28},{4,24},{8,20},{12,16},{16,12},{20,8},{24,4},{28,0},{1,29},{... | collective-permute-start | bytes 245768 | tf_op jit(solution)/shard_map/ppermute | solution.py:326
  56.5 0.8 %collective-permute-done.10.g_far = bf16[2,72,896]{2,1,0:T(8,128)(2,1)S(1)} collective-permute-done((bf16[2,72,896]{2,1,0:T(8,128)(2,1)S(1)}, bf16[2,72,896]{2,1,0:T(8,128)(2,1)S(1)}, u32[]{:S(2)}, u32[]{:S(2)}) %collective-permute-start.10) | collective-permute-done | bytes 258080 | tf_op jit(solution)/shard_map/ppermute | solution.py:326
  57.4 1.2 %shard_map.97 = (f32[2,896,512]{2,1,0:T(8,128)S(1)}, f32[2,512,896]{2,1,0:T(8,128)S(1)}) custom-call(bf16[2,40,1792]{2,1,0:T(8,128)(2,1)S(1)} %get-tuple-element.55.own_keep, bf16[2,40,1792]{2,1,0:T(8,128)(2,1)S(1)} %collective-permute-done.8.own_far, bf16[2,72,896]{2,1,0:T(8,128)(2,1)S(1)} %get-tuple-element.57.x_keep, ...), custom_call_target="tpu_custom_call" | custom-call | flops 822083584 | bytes 3670016 | tf_op jit(solution)/shard_map/pallas_call | solution.py:406
  58.6 0.0 collective-permute-done.4.refs_1_
  58.6 7.9 %collective-permute-done.7.refs_2_ = bf16[136,896]{1,0:T(8,128)(2,1)S(1)} collective-permute-done((bf16[136,896]{1,0:T(8,128)(2,1)S(1)}, bf16[136,896]{1,0:T(8,128)(2,1)S(1)}, u32[]{:S(2)}, u32[]{:S(2)}) %collective-permute-start.7) | collective-permute-done | bytes 243744 | tf_op jit(solution)/shard_map/ppermute | solution.py:320
  66.5 1.1 %shard_map.96 = bf16[64,3584]{1,0:T(8,128)(2,1)} custom-call(bf16[4,80,64]{2,1,0:T(8,128)(2,1)S(1)} %get-tuple-element.36.masks_ref, bf16[136,896]{1,0:T(8,128)(2,1)S(1)} %get-tuple-element.50.refs_0_, bf16[136,896]{1,0:T(8,128)(2,1)S(1)} %collective-permute-done.4.refs_1_, bf16[136,896]{1,0:T(8,128)(2,1)S(1)} %collective-permute-done.7.refs_2_), custom_call_target="tpu_custom_call" | custom-call | flops 1048576 | bytes 1048576 | tf_op jit(solution)/shard_map/pallas_call | solution.py:422
  67.6 0.0 collective-permute-done.13.hid_far
  67.6 0.0 collective-permute-done.12.far
  67.6 2.3 %shard_map.98 = (bf16[1792,512]{1,0:T(8,128)(2,1)}, bf16[512,1792]{1,0:T(8,128)(2,1)}) custom-call(f32[2,896,512]{2,1,0:T(8,128)S(1)} %get-tuple-element.62.up_part, f32[2,512,896]{2,1,0:T(8,128)S(1)} %get-tuple-element.63.down_part, bf16[2,40,1792]{2,1,0:T(8,128)(2,1)S(1)} %get-tuple-element.64.keep, bf16[2,40,1792]{2,1,0:T(8,128)(2,1)S(1)} %collective-permute-done.12.far, ...), custom_call_target="tpu_custom_call" | custom-call | flops 411041792 | bytes 3670016 | tf_op jit(solution)/shard_map/pallas_call | solution.py:411
  (1 shorter events, 0.0 us)
Async XLA Ops:
  2.4 21.4 %collective-permute-start.1 = (bf16[136,896]{1,0:T(8,128)(2,1)S(1)}, bf16[136,896]{1,0:T(8,128)(2,1)S(1)}, u32[]{:S(2)}, u32[]{:S(2)}) collective-permute-start(bf16[136,896]{1,0:T(8,128)(2,1)S(1)} %get-tuple-element.42), channel_id=1, source_target_pairs={{0,2},{1,3},{2,0},{3,1},{4,6},{5,7},{6,4},{7,5},{8,10},{9,11},{10,... | collective-permute-start | bytes 731144 | tf_op jit(solution)/shard_map/ppermute | solution.py:320
  6.6 21.7 %collective-permute-start.3 = (bf16[136,896]{1,0:T(8,128)(2,1)S(1)}, bf16[136,896]{1,0:T(8,128)(2,1)S(1)}, u32[]{:S(2)}, u32[]{:S(2)}) collective-permute-start(bf16[136,896]{1,0:T(8,128)(2,1)S(1)} %get-tuple-element.44), channel_id=1, source_target_pairs={{0,2},{1,3},{2,0},{3,1},{4,6},{5,7},{6,4},{7,5},{8,10},{9,11},{10,... | collective-permute-start | bytes 731144 | tf_op jit(solution)/shard_map/ppermute | solution.py:320
  6.6 24.5 %collective-permute-start.2 = (bf16[136,896]{1,0:T(8,128)(2,1)S(1)}, bf16[136,896]{1,0:T(8,128)(2,1)S(1)}, u32[]{:S(2)}, u32[]{:S(2)}) collective-permute-start(bf16[136,896]{1,0:T(8,128)(2,1)S(1)} %get-tuple-element.37.refs_0_), channel_id=1, source_target_pairs={{0,1},{1,0},{2,3},{3,2},{4,5},{5,4},{6,7},{7,6},{8,9},{9,8},{10,11... | collective-permute-start | bytes 731144 | tf_op jit(solution)/shard_map/ppermute | solution.py:320
  8.5 27.8 %collective-permute-start = (bf16[136,896]{1,0:T(8,128)(2,1)S(1)}, bf16[136,896]{1,0:T(8,128)(2,1)S(1)}, u32[]{:S(2)}, u32[]{:S(2)}) collective-permute-start(bf16[136,896]{1,0:T(8,128)(2,1)S(1)} %get-tuple-element.40.refs_1_), channel_id=1, source_target_pairs={{0,1},{1,0},{2,3},{3,2},{4,5},{5,4},{6,7},{7,6},{8,9},{9,8},{10,11... | collective-permute-start | bytes 731144 | tf_op jit(solution)/shard_map/ppermute | solution.py:320
  28.3 13.1 %collective-permute-start.5 = (bf16[2,136,896]{2,1,0:T(8,128)(2,1)S(1)}, bf16[2,136,896]{2,1,0:T(8,128)(2,1)S(1)}, u32[]{:S(2)}, u32[]{:S(2)}) collective-permute-start(bf16[2,136,896]{2,1,0:T(8,128)(2,1)S(1)} %shard_map.92), channel_id=1, source_target_pairs={{0,1},{1,0},{2,3},{3,2},{4,5},{5,4},{6,7},{7,6},{8,9},{9,8},{10,11... | collective-permute-start | bytes 1462280 | tf_op jit(solution)/shard_map/ppermute | solution.py:320
  29.3 20.4 %collective-permute-start.8 = (bf16[2,40,1792]{2,1,0:T(8,128)(2,1)S(1)}, bf16[2,40,1792]{2,1,0:T(8,128)(2,1)S(1)}, u32[]{:S(2)}, u32[]{:S(2)}) collective-permute-start(bf16[2,40,1792]{2,1,0:T(8,128)(2,1)S(1)} %get-tuple-element.56), channel_id=1, source_target_pairs={{0,28},{4,24},{8,20},{12,16},{16,12},{20,8},{24,4},{28,0},{1,29},{... | collective-permute-start | bytes 860168 | tf_op jit(solution)/shard_map/ppermute | solution.py:326
  38.3 8.6 %collective-permute-start.6 = (bf16[136,896]{1,0:T(8,128)(2,1)S(1)}, bf16[136,896]{1,0:T(8,128)(2,1)S(1)}, u32[]{:S(2)}, u32[]{:S(2)}) collective-permute-start(bf16[136,896]{1,0:T(8,128)(2,1)S(1)} %get-tuple-element.54), channel_id=1, source_target_pairs={{0,1},{1,0},{2,3},{3,2},{4,5},{5,4},{6,7},{7,6},{8,9},{9,8},{10,11... | collective-permute-start | bytes 731144 | tf_op jit(solution)/shard_map/ppermute | solution.py:320
  38.7 12.4 %collective-permute-start.11 = (bf16[2,112,512]{2,1,0:T(8,128)(2,1)S(1)}, bf16[2,112,512]{2,1,0:T(8,128)(2,1)S(1)}, u32[]{:S(2)}, u32[]{:S(2)}) collective-permute-start(bf16[2,112,512]{2,1,0:T(8,128)(2,1)S(1)} %get-tuple-element.61.hid), channel_id=1, source_target_pairs={{0,28},{4,24},{8,20},{12,16},{16,12},{20,8},{24,4},{28,0},{1,29},{... | collective-permute-start | bytes 688136 | tf_op jit(solution)/shard_map/ppermute | solution.py:326
  40.3 14.3 %collective-permute-start.9 = (bf16[2,72,896]{2,1,0:T(8,128)(2,1)S(1)}, bf16[2,72,896]{2,1,0:T(8,128)(2,1)S(1)}, u32[]{:S(2)}, u32[]{:S(2)}) collective-permute-start(bf16[2,72,896]{2,1,0:T(8,128)(2,1)S(1)} %get-tuple-element.58), channel_id=1, source_target_pairs={{0,28},{4,24},{8,20},{12,16},{16,12},{20,8},{24,4},{28,0},{1,29},{... | collective-permute-start | bytes 774152 | tf_op jit(solution)/shard_map/ppermute | solution.py:326
  41.4 16.0 %collective-permute-start.10 = (bf16[2,72,896]{2,1,0:T(8,128)(2,1)S(1)}, bf16[2,72,896]{2,1,0:T(8,128)(2,1)S(1)}, u32[]{:S(2)}, u32[]{:S(2)}) collective-permute-start(bf16[2,72,896]{2,1,0:T(8,128)(2,1)S(1)} %get-tuple-element.60), channel_id=1, source_target_pairs={{0,28},{4,24},{8,20},{12,16},{16,12},{20,8},{24,4},{28,0},{1,29},{... | collective-permute-start | bytes 774152 | tf_op jit(solution)/shard_map/ppermute | solution.py:326
  47.0 20.6 %collective-permute-start.12 = (bf16[2,40,1792]{2,1,0:T(8,128)(2,1)S(1)}, bf16[2,40,1792]{2,1,0:T(8,128)(2,1)S(1)}, u32[]{:S(2)}, u32[]{:S(2)}) collective-permute-start(bf16[2,40,1792]{2,1,0:T(8,128)(2,1)S(1)} %get-tuple-element.65), channel_id=1, source_target_pairs={{0,28},{4,24},{8,20},{12,16},{16,12},{20,8},{24,4},{28,0},{1,29},{... | collective-permute-start | bytes 860168 | tf_op jit(solution)/shard_map/ppermute | solution.py:326
  49.7 9.0 %collective-permute-start.4 = (bf16[136,896]{1,0:T(8,128)(2,1)S(1)}, bf16[136,896]{1,0:T(8,128)(2,1)S(1)}, u32[]{:S(2)}, u32[]{:S(2)}) collective-permute-start(bf16[136,896]{1,0:T(8,128)(2,1)S(1)} %get-tuple-element.51), channel_id=1, source_target_pairs={{0,1},{1,0},{2,3},{3,2},{4,5},{5,4},{6,7},{7,6},{8,9},{9,8},{10,11... | collective-permute-start | bytes 731144 | tf_op jit(solution)/shard_map/ppermute | solution.py:320
  51.1 15.4 %collective-permute-start.7 = (bf16[136,896]{1,0:T(8,128)(2,1)S(1)}, bf16[136,896]{1,0:T(8,128)(2,1)S(1)}, u32[]{:S(2)}, u32[]{:S(2)}) collective-permute-start(bf16[136,896]{1,0:T(8,128)(2,1)S(1)} %shard_map.95), channel_id=1, source_target_pairs={{0,3},{1,2},{2,1},{3,0},{4,7},{5,6},{6,5},{7,4},{8,11},{9,10},{10,... | collective-permute-start | bytes 731144 | tf_op jit(solution)/shard_map/ppermute | solution.py:320
  54.6 13.0 %collective-permute-start.13 = (bf16[2,40,512]{2,1,0:T(8,128)(2,1)S(1)}, bf16[2,40,512]{2,1,0:T(8,128)(2,1)S(1)}, u32[]{:S(2)}, u32[]{:S(2)}) collective-permute-start(bf16[2,40,512]{2,1,0:T(8,128)(2,1)S(1)} %get-tuple-element.66.hid), channel_id=1, source_target_pairs={{0,28},{4,24},{8,20},{12,16},{16,12},{20,8},{24,4},{28,0},{1,29},{... | collective-permute-start | bytes 245768 | tf_op jit(solution)/shard_map/ppermute | solution.py:326

commit v5 on v4

--- a/solution.py
+++ b/solution.py
@@ -224,16 +224,15 @@
         pick_halves(upper_ref, rows.at[t], keep_ref.at[:, :, at], send_ref.at[:, :, at])
 
 
-def last_kernel(rows, up_ref, up_t_ref, down_t_ref, hidden_ref, out_ref):
-    values = hidden_values([rows.at[1]], times_up([rows.at[0]], up_ref), down_t_ref)
-    for plane in range(2):
-        hidden_ref[plane] = values[plane]
-    back_rows(values[0], up_t_ref, [[out_ref]])
-
-
-def stack_kernel(a_ref, b_ref, out_ref):
-    out_ref[0] = a_ref[...]
-    out_ref[1] = b_ref[...]
+def pre_last_kernel(upper_ref, payload_ref, up_ref, pre_ref, keep_ref, send_ref, rows):
+    join_rows([payload_ref], rows)
+    pick_halves(upper_ref, rows, keep_ref, send_ref)
+    pre_ref[...] = times_up([rows], up_ref)
+
+
+def last_kernel(rows, pre_ref, up_ref, down_ref, hidden_ref, out_ref):
+    hidden_ref[0], hidden_ref[1] = hidden_values([rows], pre_ref[...], down_ref)
+    back_rows(hidden_ref[0], up_ref, [[out_ref]])
 
 
 def add_kernel(a_ref, b_ref, out_ref):
@@ -243,26 +242,29 @@
 ACROSS_ROWS = ((0,), (0,))
 
 
-def grad_kernel(own_keep, own_far, x_keep, x_far, g_keep, g_far, hid, hid_far, up_ref, down_ref):
+def grad_kernel(own_keep, own_far, x_keep, x_far, g_keep, g_far, hid, hid_far, *refs):
+    last, (up_ref, down_ref) = refs[:-2], refs[-2:]
     width = x_keep.shape[2]
-    dpre, act = (jnp.concatenate([ref[t] for ref in (hid, hid_far)], axis=0) for t in range(2))
+    dpre, act = (jnp.concatenate([ref[t] for ref in (hid, hid_far) + last[2:]], axis=0) for t in range(2))
     for chunk in range(x_keep.shape[0]):
         x, g = (
-            jnp.concatenate([own_keep[chunk, :, at], keep[chunk], own_far[chunk, :, at], far[chunk]], axis=0)
-            for keep, far, at in ((x_keep, x_far, slice(0, width)), (g_keep, g_far, slice(width, 2 * width)))
+            jnp.concatenate(
+                [own_keep[chunk, :, at], keep[chunk], own_far[chunk, :, at], far[chunk]] + [ref[chunk] for ref in more], axis=0
+            )
+            for keep, far, at, more in (
+                (x_keep, x_far, slice(0, width), last[0:1]), (g_keep, g_far, slice(width, 2 * width), last[1:2])
+            )
         )
         up_ref[chunk] = dot(x, dpre, ACROSS_ROWS).astype(up_ref.dtype)
         down_ref[chunk] = dot(act, g, ACROSS_ROWS).astype(down_ref.dtype)
 
 
-def grad_last_kernel(up_part, down_part, keep, far, hid, hid_far, up_hbm, down_hbm, up_out, down_out, sems):
-    width = keep.shape[2] // 2
-    dpre, act = (jnp.concatenate([ref[t] for ref in (hid, hid_far)], axis=0) for t in range(2))
+def grad_last_kernel(up_part, down_part, x_far, g_far, hid_far, up_hbm, down_hbm, up_out, down_out, sems):
+    width = x_far.shape[2]
+    dpre, act = hid_far[0], hid_far[1]
     copies = []
-    for chunk in range(keep.shape[0]):
-        x, g = (
-            jnp.concatenate([ref[chunk, :, t * width:(t + 1) * width] for ref in (keep, far)], axis=0) for t in range(2)
-        )
+    for chunk in range(x_far.shape[0]):
+        x, g = x_far[chunk], g_far[chunk]
         at = slice(chunk * width, (chunk + 1) * width)
         up_out[chunk] = (up_part[chunk] + dot(x, dpre, ACROSS_ROWS)).astype(BF16)
         copies.append(pltpu.make_async_copy(up_out.at[chunk], up_hbm.at[at, :], sems.at[2 * chunk]))
@@ -275,8 +277,9 @@
 
 
 def final_kernel(own_count, masks_ref, *refs):
-    own_refs, other_refs, out_ref = refs[:own_count], refs[own_count:-1], refs[-1]
-    width = out_ref.shape[1] // CHUNKS
+    own_refs, other_refs, (out_hbm, out_ref, sems) = refs[:own_count], refs[own_count:-3], refs[-3:]
+    width = out_ref.shape[2]
+    copies = []
 
     def sides(lo, hi):
         return [sum(ref[lo:hi, :].astype(F32) for ref in side) for side in (own_refs, other_refs)]
@@ -284,7 +287,12 @@
     folds = sides(CHUNKS * MAIN, CHUNKS * MAIN + FOLD)
     for chunk in range(CHUNKS):
         rows = jnp.concatenate(sides(chunk * MAIN, (chunk + 1) * MAIN) + folds, axis=0).astype(BF16)
-        out_ref[:, chunk * width:(chunk + 1) * width] = dot(masks_ref[chunk], rows, ((0,), (0,))).astype(BF16)
+        out_ref[chunk] = dot(masks_ref[chunk], rows, ((0,), (0,))).astype(BF16)
+        at = slice(chunk * width, (chunk + 1) * width)
+        copies.append(pltpu.make_async_copy(out_ref.at[chunk], out_hbm.at[:, at], sems.at[chunk]))
+        copies[-1].start()
+    for copy in copies:
+        copy.wait()
 
 
 def per_device(tokens, cotangent, router_gate, routes, up_weight, down_weight):
@@ -362,10 +370,7 @@
         scratch_shapes=[pltpu.VMEM((CHUNKS, row_count(size), width), BF16), pltpu.SemaphoreType.DMA((2,))],
     )(upper, own_rows, *x_parts, in_hbm(up), in_hbm(down))
     if line:
-        passed = call(stack_kernel, held((2,) + payload_shape), small, small, in_specs=[vmem()] * 2, out_specs=vmem())(
-            x_across, g_across
-        )
-        passed = swap(passed, 1)
+        x_passed, g_passed = swap(x_across, 1), swap(g_across, 1)
     x_far = mirror(x_sent)
     up_t, down_t = call(
         flip_kernel, (held((hidden, model)), held((model, hidden))), small, moved, in_specs=[vmem()] * 2, out_specs=(vmem(),) * 2
@@ -383,18 +388,25 @@
     for_grad = [own_keep, own_far, x_keep, x_far, g_keep, g_far, hid, mirror(hid)]
 
     if line:
-        last_keep, last_sent, last_rows = call(
-            pick_kernel, (pair, pair, pair_rows), small, small,
-            in_specs=[smem(), vmem()],
-            out_specs=(vmem(),) * 3,
-        )(upper, passed)
-        last_far = mirror(last_sent)
+        single = held((half, one, width))
+        last_pre, xl_keep, xl_sent = call(
+            pre_last_kernel, (held((one, hidden), F32), single, single), flops, moved,
+            in_specs=[smem()] + [vmem()] * 2, out_specs=(vmem(),) * 3,
+            scratch_shapes=[pltpu.VMEM((CHUNKS, one, width), BF16)],
+        )(upper, x_passed, up_here)
+        xl_far = mirror(xl_sent)
+        last_rows, gl_keep, gl_sent = call(
+            functools.partial(join_kernel, 1), (held((CHUNKS, one, width)), single, single), small, small,
+            in_specs=[smem(), vmem()], out_specs=(vmem(),) * 3,
+        )(upper, g_passed)
+        gl_far = mirror(gl_sent)
         last_hidden, last_back = call(
             last_kernel, (held((2, one, hidden)), payload), flops, 2 * moved,
             in_specs=[vmem()] * 4,
             out_specs=(vmem(),) * 2,
-        )(last_rows, up_here, up_t, down_t)
-        for_last = [last_keep, last_far, last_hidden, mirror(last_hidden)]
+        )(last_rows, last_pre, up_t, down_t)
+        for_grad += [xl_keep, gl_keep, last_hidden]
+        for_last = [xl_far, gl_far, mirror(last_hidden)]
         for_far = swap(back[2], 1)
         both = call(add_kernel, payload, small, small, in_specs=[vmem()] * 2, out_specs=vmem())(last_back, for_far)
         own_side, other_side = [back[0], swap(back[1], 1)], [swap(both, 3)]
@@ -405,14 +417,14 @@
     kept = F32 if line else BF16
     grad_up, grad_down = call(
         grad_kernel, (held((half, width, hidden), kept), held((half, hidden, width), kept)), 2 * flops, moved,
-        in_specs=[vmem()] * 8, out_specs=(vmem(),) * 2,
+        in_specs=[vmem()] * len(for_grad), out_specs=(vmem(),) * 2,
     )(*for_grad)
     if line:
         grad_up, grad_down = call(
             grad_last_kernel,
             (jax.ShapeDtypeStruct((model // 2, hidden), BF16), jax.ShapeDtypeStruct((hidden, model // 2), BF16)),
             flops, moved,
-            in_specs=[vmem()] * 6, out_specs=(hbm(),) * 2,
+            in_specs=[vmem()] * 5, out_specs=(hbm(),) * 2,
             scratch_shapes=[
                 pltpu.VMEM((half, width, hidden), BF16), pltpu.VMEM((half, hidden, width), BF16), pltpu.SemaphoreType.DMA((2 * half,))
             ],
@@ -421,7 +433,8 @@
         grad_up, grad_down = grad_up.reshape(model // 2, hidden), grad_down.transpose(1, 0, 2).reshape(hidden, model // 2)
     input_grad = call(
         functools.partial(final_kernel, len(own_side)), jax.ShapeDtypeStruct((tok, model), BF16), small, small,
-        in_specs=[vmem()] * (1 + len(own_side) + len(other_side)), out_specs=vmem(),
+        in_specs=[vmem()] * (1 + len(own_side) + len(other_side)), out_specs=hbm(),
+        scratch_shapes=[pltpu.VMEM((CHUNKS, tok, width), BF16), pltpu.SemaphoreType.DMA((CHUNKS,))],
     )(masks, *own_side, *other_side)
     return (input_grad[None], grad_up[None], grad_down[None])
 

time: 70.1 us -> 68.9 us (0.983); the launches traced: 69.9 us -> 67.7 us
  waiting for transfers between devices: 32.1 us -> 24.9 us
  starting transfers between devices: 20.5 us -> 24.5 us
  Pallas kernels: 16.6 us -> 17.5 us
    ppermute x8 -> x9, waiting for transfers between devices: 31.2 us -> 20.3 us  [send(): return lax.ppermute(value, 'expert', pairs)]
    ppermute x6 -> x7, starting transfers between devices: 8.18 us -> 12.2 us  [mirror(): lax.ppermute(value, 'pipe', [(i, ranks - 1 - i) for i in range(ranks)])]
    ppermute x6 -> x7, waiting for transfers between devices: 0.86 us -> 4.61 us  [mirror(): lax.ppermute(value, 'pipe', [(i, ranks - 1 - i) for i in range(ranks)])]
    pallas_call x1 -> x2, Pallas kernels: 0.04 us -> 1.02 us  [the longest x1 0.83 us: per_device(): call(pre_last_kernel, (held((one, hidden), F32), single, single), flops,...]
    pallas_call x1, Pallas kernels: 1.24 us -> 2.18 us  [per_device(): call(grad_kernel, (held((half, width, hidden), kept), held((half, hidden,...]
    ppermute x8 -> x9, starting transfers between devices: 12.4 us -> 12.3 us  [send(): return lax.ppermute(value, 'expert', pairs)]
  transfers between devices with their start and end apart: 14 -> 16, of which waited for: 5 -> 5; matrix products, arithmetic and copies ran while one was open for 0% -> 0% of each run, Pallas kernels for 18% -> 22%
where the time goes in v5:
time: 68.9 us; the launch traced here: 67.7 us
  waiting for transfers between devices  24.9 us (36%)
  starting transfers between devices  24.5 us (36%)
  Pallas kernels  17.5 us (25%)
  between operations  0.78 us (1%)
    ppermute x9, waiting for transfers between devices, send(): return lax.ppermute(value, 'expert', pairs)  20.3 us
    ppermute x9, starting transfers between devices, send(): return lax.ppermute(value, 'expert', pairs)  12.3 us
    ppermute x7, starting transfers between devices, mirror(): lax.ppermute(value, 'pipe', [(i, ranks - 1 - i) for i in range(ranks)])  12.2 us
    ppermute x7, waiting for transfers between devices, mirror(): lax.ppermute(value, 'pipe', [(i, ranks - 1 - i) for i in range(ranks)])  4.61 us
    pallas_call x1, Pallas kernels, per_device(): call(functools.partial(pre_kernel, size), (held((rows, hidden), F32), hal...  3.18 us
    pallas_call x1, Pallas kernels, per_device(): call(grad_last_kernel, (jax.ShapeDtypeStruct((model // 2, hidden), BF16),...  2.29 us
    pallas_call x1, Pallas kernels, per_device(): call(grad_kernel, (held((half, width, hidden), kept), held((half, hidden,...  2.18 us
    pallas_call x1, Pallas kernels, per_device(): call(flip_kernel, (held((hidden, model)), held((model, hidden))), small,...  1.94 us
  transfers between devices with their start and end apart: 16, of which 5 were waited for; matrix products, arithmetic and copies ran while one was open for 0% of the time, Pallas kernels for 22%

profile of v5, /device:TPU:0, one launch (start us, length us, event | category | flops | bytes accessed | tf_op | source)
XLA Modules:
  0.0 67.7 jit_solution(7858518878740705194)
XLA Ops:
  0.6 1.4 %shard_map.85 = (bf16[136,896]{1,0:T(8,128)(2,1)S(1)}, bf16[136,896]{1,0:T(8,128)(2,1)S(1)}, bf16[4,80,64]{2,1,0:T(8,128)(2,1)S(1)}, f32[1,64]{1,0:T(1,128)S(1)}, bf16[64,3584]{1,0:T(8,128)(2,1)S(1)}) custom-call(s32[1]{0:T(128)} %bitcast.mine_ref, s32[1,64]{1,0:T(1,128)} %bitcast.15, f32[1,64]{1,0:T(1,128)} %gate_hbm.1, bf16[64,3584]{1,0:T(8,128)(2,1)} %bitcast.12, ...), custom_call_target="tpu_custom_call" | custom-call | flops 1048576 | bytes 1048576 | tf_op jit(solution)/shard_map/pallas_call | solution.py:337
  2.0 4.1 %collective-permute-start.3 = (bf16[136,896]{1,0:T(8,128)(2,1)S(1)}, bf16[136,896]{1,0:T(8,128)(2,1)S(1)}, u32[]{:S(2)}, u32[]{:S(2)}) collective-permute-start(bf16[136,896]{1,0:T(8,128)(2,1)S(1)} %get-tuple-element.47), channel_id=1, source_target_pairs={{0,2},{1,3},{2,0},{3,1},{4,6},{5,7},{6,4},{7,5},{8,10},{9,11},{10,... | collective-permute-start | bytes 731144 | tf_op jit(solution)/shard_map/ppermute | solution.py:328
  6.2 0.4 shard_map.86
  6.6 0.1 collective-permute-start.1
  6.6 1.9 %collective-permute-start.2 = (bf16[136,896]{1,0:T(8,128)(2,1)S(1)}, bf16[136,896]{1,0:T(8,128)(2,1)S(1)}, u32[]{:S(2)}, u32[]{:S(2)}) collective-permute-start(bf16[136,896]{1,0:T(8,128)(2,1)S(1)} %get-tuple-element.40.refs_0_), channel_id=1, source_target_pairs={{0,1},{1,0},{2,3},{3,2},{4,5},{5,4},{6,7},{7,6},{8,9},{9,8},{10,11... | collective-permute-start | bytes 731144 | tf_op jit(solution)/shard_map/ppermute | solution.py:328
  8.5 0.2 collective-permute-start
  8.7 14.7 %collective-permute-done.3.refs_1_ = bf16[136,896]{1,0:T(8,128)(2,1)S(1)} collective-permute-done((bf16[136,896]{1,0:T(8,128)(2,1)S(1)}, bf16[136,896]{1,0:T(8,128)(2,1)S(1)}, u32[]{:S(2)}, u32[]{:S(2)}) %collective-permute-start.3) | collective-permute-done | bytes 243744 | tf_op jit(solution)/shard_map/ppermute | solution.py:328
  23.5 0.0 collective-permute-start.6
  23.5 4.4 %collective-permute-done.1.refs_1_ = bf16[136,896]{1,0:T(8,128)(2,1)S(1)} collective-permute-done((bf16[136,896]{1,0:T(8,128)(2,1)S(1)}, bf16[136,896]{1,0:T(8,128)(2,1)S(1)}, u32[]{:S(2)}, u32[]{:S(2)}) %collective-permute-start.1) | collective-permute-done | bytes 243744 | tf_op jit(solution)/shard_map/ppermute | solution.py:328
  27.9 0.7 collective-permute-start.5
  28.5 0.2 shard_map.87
  28.8 1.9 %collective-permute-start.9 = (bf16[2,40,1792]{2,1,0:T(8,128)(2,1)S(1)}, bf16[2,40,1792]{2,1,0:T(8,128)(2,1)S(1)}, u32[]{:S(2)}, u32[]{:S(2)}) collective-permute-start(bf16[2,40,1792]{2,1,0:T(8,128)(2,1)S(1)} %get-tuple-element.60), channel_id=1, source_target_pairs={{0,28},{4,24},{8,20},{12,16},{16,12},{20,8},{24,4},{28,0},{1,29},{... | collective-permute-start | bytes 860168 | tf_op jit(solution)/shard_map/ppermute | solution.py:334
  30.6 0.0 collective-permute-done.2.refs_0_
  30.6 3.2 %shard_map.89 = (f32[112,512]{1,0:T(8,128)S(1)}, bf16[2,72,896]{2,1,0:T(8,128)(2,1)S(1)}, bf16[2,72,896]{2,1,0:T(8,128)(2,1)S(1)}, bf16[3584,512]{1,0:T(8,128)(2,1)S(1)}, bf16[512,3584]{1,0:T(8,128)(2,1)S(1)}) custom-call(s32[1]{0:T(128)} %bitcast.4.upper_ref, bf16[2,4,40,896]{3,2,1,0:T(8,128)(2,1)S(1)} %get-tuple-element.44.first_ref, ...), custom_call_target="tpu_custom_call" | custom-call | flops 411041792 | bytes 3670016 | tf_op jit(solution)/shard_map/pallas_call | solution.py:364
  33.8 1.9 %shard_map.90 = (bf16[512,3584]{1,0:T(8,128)(2,1)S(1)}, bf16[3584,512]{1,0:T(8,128)(2,1)S(1)}) custom-call(bf16[3584,512]{1,0:T(8,128)(2,1)S(1)} %get-tuple-element.49.up_ref, bf16[512,3584]{1,0:T(8,128)(2,1)S(1)} %get-tuple-element.50.down_ref), custom_call_target="tpu_custom_call" | custom-call | flops 1048576 | bytes 3670016 | tf_op jit(solution)/shard_map/pallas_call | solution.py:375
  35.8 0.0 collective-permute-done.refs_0_
  35.8 0.2 shard_map.88
  36.0 1.8 %shard_map.91 = (bf16[2,112,512]{2,1,0:T(8,128)(2,1)S(1)}, bf16[136,896]{1,0:T(8,128)(2,1)S(1)}, bf16[136,896]{1,0:T(8,128)(2,1)S(1)}, bf16[136,896]{1,0:T(8,128)(2,1)S(1)}) custom-call(bf16[2,4,40,896]{3,2,1,0:T(8,128)(2,1)S(1)} %get-tuple-element.44.first_ref, bf16[4,72,896]{2,1,0:T(8,128)(2,1)S(1)} %get-tuple-element.46.rows_ref, ...), custom_call_target="tpu_custom_call" | custom-call | flops 822083584 | bytes 7340032 | tf_op jit(solution)/shard_map/pallas_call | solution.py:383
  37.8 0.4 collective-permute-start.7
  38.2 1.6 %collective-permute-start.10 = (bf16[2,72,896]{2,1,0:T(8,128)(2,1)S(1)}, bf16[2,72,896]{2,1,0:T(8,128)(2,1)S(1)}, u32[]{:S(2)}, u32[]{:S(2)}) collective-permute-start(bf16[2,72,896]{2,1,0:T(8,128)(2,1)S(1)} %get-tuple-element.62), channel_id=1, source_target_pairs={{0,28},{4,24},{8,20},{12,16},{16,12},{20,8},{24,4},{28,0},{1,29},{... | collective-permute-start | bytes 774152 | tf_op jit(solution)/shard_map/ppermute | solution.py:334
  39.8 0.0 collective-permute-done.6.payload_ref
  39.8 1.0 %collective-permute-start.12 = (bf16[2,112,512]{2,1,0:T(8,128)(2,1)S(1)}, bf16[2,112,512]{2,1,0:T(8,128)(2,1)S(1)}, u32[]{:S(2)}, u32[]{:S(2)}) collective-permute-start(bf16[2,112,512]{2,1,0:T(8,128)(2,1)S(1)} %get-tuple-element.65.hid), channel_id=1, source_target_pairs={{0,28},{4,24},{8,20},{12,16},{16,12},{20,8},{24,4},{28,0},{1,29},{... | collective-permute-start | bytes 688136 | tf_op jit(solution)/shard_map/ppermute | solution.py:334
  40.9 0.0 collective-permute-done.5.refs_0_
  40.9 1.6 %collective-permute-start.11 = (bf16[2,72,896]{2,1,0:T(8,128)(2,1)S(1)}, bf16[2,72,896]{2,1,0:T(8,128)(2,1)S(1)}, u32[]{:S(2)}, u32[]{:S(2)}) collective-permute-start(bf16[2,72,896]{2,1,0:T(8,128)(2,1)S(1)} %get-tuple-element.64), channel_id=1, source_target_pairs={{0,28},{4,24},{8,20},{12,16},{16,12},{20,8},{24,4},{28,0},{1,29},{... | collective-permute-start | bytes 774152 | tf_op jit(solution)/shard_map/ppermute | solution.py:334
  42.5 0.2 shard_map.92
  42.7 0.8 %shard_map.93 = (f32[40,512]{1,0:T(8,128)S(1)}, bf16[2,40,896]{2,1,0:T(8,128)(2,1)S(1)}, bf16[2,40,896]{2,1,0:T(8,128)(2,1)S(1)}) custom-call(s32[1]{0:T(128)} %bitcast.4.upper_ref, bf16[136,896]{1,0:T(8,128)(2,1)S(1)} %collective-permute-done.6.payload_ref, bf16[3584,512]{1,0:T(8,128)(2,1)S(1)} %get-tuple-element.49.up_ref), custom_call_target="tpu_custom_call" | custom-call | flops 411041792 | bytes 3670016 | tf_op jit(solution)/shard_map/pallas_call | solution.py:392
  43.5 1.8 %shard_map.94 = (bf16[2,40,512]{2,1,0:T(8,128)(2,1)S(1)}, bf16[136,896]{1,0:T(8,128)(2,1)S(1)}) custom-call(bf16[4,40,896]{2,1,0:T(8,128)(2,1)S(1)} %get-tuple-element.55.rows, f32[40,512]{1,0:T(8,128)S(1)} %get-tuple-element.56.pre_ref, bf16[512,3584]{1,0:T(8,128)(2,1)S(1)} %get-tuple-element.51.up_ref, bf16[3584,512]{1,0:T(8,128)(2,1)S(1)} %get-tuple-element.52.down_ref), custom_call_target="tpu_custom_call" | custom-call | flops 411041792 | bytes 7340032 | tf_op jit(solution)/shard_map/pallas_call | solution.py:403
  45.3 1.2 %collective-permute-done.7.b_ref = bf16[136,896]{1,0:T(8,128)(2,1)S(1)} collective-permute-done((bf16[136,896]{1,0:T(8,128)(2,1)S(1)}, bf16[136,896]{1,0:T(8,128)(2,1)S(1)}, u32[]{:S(2)}, u32[]{:S(2)}) %collective-permute-start.7) | collective-permute-done | bytes 243744 | tf_op jit(solution)/shard_map/ppermute | solution.py:328
  46.5 0.0 collective-permute-start.4
  46.5 0.1 shard_map.95
  46.5 0.0 collective-permute-done.9.own_far
  46.5 5.0 %collective-permute-start.8 = (bf16[136,896]{1,0:T(8,128)(2,1)S(1)}, bf16[136,896]{1,0:T(8,128)(2,1)S(1)}, u32[]{:S(2)}, u32[]{:S(2)}) collective-permute-start(bf16[136,896]{1,0:T(8,128)(2,1)S(1)} %shard_map.95), channel_id=1, source_target_pairs={{0,3},{1,2},{2,1},{3,0},{4,7},{5,6},{6,5},{7,4},{8,11},{9,10},{10,... | collective-permute-start | bytes 731144 | tf_op jit(solution)/shard_map/ppermute | solution.py:328
  51.5 0.0 collective-permute-done.12.hid_far
  51.5 2.9 %collective-permute-start.13 = (bf16[2,40,896]{2,1,0:T(8,128)(2,1)S(1)}, bf16[2,40,896]{2,1,0:T(8,128)(2,1)S(1)}, u32[]{:S(2)}, u32[]{:S(2)}) collective-permute-start(bf16[2,40,896]{2,1,0:T(8,128)(2,1)S(1)} %get-tuple-element.71), channel_id=1, source_target_pairs={{0,28},{4,24},{8,20},{12,16},{16,12},{20,8},{24,4},{28,0},{1,29},{... | collective-permute-start | bytes 430088 | tf_op jit(solution)/shard_map/ppermute | solution.py:334
  54.4 0.0 collective-permute-done.10.x_far
  54.4 0.0 collective-permute-start.14
  54.5 2.4 %collective-permute-done.11.g_far = bf16[2,72,896]{2,1,0:T(8,128)(2,1)S(1)} collective-permute-done((bf16[2,72,896]{2,1,0:T(8,128)(2,1)S(1)}, bf16[2,72,896]{2,1,0:T(8,128)(2,1)S(1)}, u32[]{:S(2)}, u32[]{:S(2)}) %collective-permute-start.11) | collective-permute-done | bytes 258080 | tf_op jit(solution)/shard_map/ppermute | solution.py:334
  56.9 3.1 %collective-permute-start.15 = (bf16[2,40,512]{2,1,0:T(8,128)(2,1)S(1)}, bf16[2,40,512]{2,1,0:T(8,128)(2,1)S(1)}, u32[]{:S(2)}, u32[]{:S(2)}) collective-permute-start(bf16[2,40,512]{2,1,0:T(8,128)(2,1)S(1)} %get-tuple-element.68.refs_2_), channel_id=1, source_target_pairs={{0,28},{4,24},{8,20},{12,16},{16,12},{20,8},{24,4},{28,0},{1,29},{... | collective-permute-start | bytes 245768 | tf_op jit(solution)/shard_map/ppermute | solution.py:334
  60.0 2.2 %shard_map.97 = (f32[2,896,512]{2,1,0:T(8,128)S(1)}, f32[2,512,896]{2,1,0:T(8,128)S(1)}) custom-call(bf16[2,40,1792]{2,1,0:T(8,128)(2,1)S(1)} %get-tuple-element.59.own_keep, bf16[2,40,1792]{2,1,0:T(8,128)(2,1)S(1)} %collective-permute-done.9.own_far, bf16[2,72,896]{2,1,0:T(8,128)(2,1)S(1)} %get-tuple-element.61.x_keep, ...), custom_call_target="tpu_custom_call" | custom-call | flops 822083584 | bytes 3670016 | tf_op jit(solution)/shard_map/pallas_call | solution.py:418
  62.1 2.2 %collective-permute-done.15.hid_far = bf16[2,40,512]{2,1,0:T(8,128)(2,1)S(1)} collective-permute-done((bf16[2,40,512]{2,1,0:T(8,128)(2,1)S(1)}, bf16[2,40,512]{2,1,0:T(8,128)(2,1)S(1)}, u32[]{:S(2)}, u32[]{:S(2)}) %collective-permute-start.15) | collective-permute-done | bytes 81952 | tf_op jit(solution)/shard_map/ppermute | solution.py:334
  64.4 0.0 collective-permute-done.13.x_far
  64.4 0.0 collective-permute-done.14.g_far
  64.4 2.3 %shard_map.98 = (bf16[1792,512]{1,0:T(8,128)(2,1)}, bf16[512,1792]{1,0:T(8,128)(2,1)}) custom-call(f32[2,896,512]{2,1,0:T(8,128)S(1)} %get-tuple-element.69.up_part, f32[2,512,896]{2,1,0:T(8,128)S(1)} %get-tuple-element.70.down_part, bf16[2,40,896]{2,1,0:T(8,128)(2,1)S(1)} %collective-permute-done.13.x_far, ...), custom_call_target="tpu_custom_call" | custom-call | flops 411041792 | bytes 3670016 | tf_op jit(solution)/shard_map/pallas_call | solution.py:423
  66.7 0.0 collective-permute-done.4.refs_1_
  66.7 0.0 collective-permute-done.8.refs_2_
  66.7 1.0 %shard_map.96 = bf16[64,3584]{1,0:T(8,128)(2,1)} custom-call(bf16[4,80,64]{2,1,0:T(8,128)(2,1)S(1)} %get-tuple-element.39.masks_ref, bf16[136,896]{1,0:T(8,128)(2,1)S(1)} %get-tuple-element.53.refs_0_, bf16[136,896]{1,0:T(8,128)(2,1)S(1)} %collective-permute-done.4.refs_1_, bf16[136,896]{1,0:T(8,128)(2,1)S(1)} %collective-permute-done.8.refs_2_), custom_call_target="tpu_custom_call" | custom-call | flops 1048576 | bytes 1048576 | tf_op jit(solution)/shard_map/pallas_call | solution.py:434
Async XLA Ops:
  2.0 21.4 %collective-permute-start.3 = (bf16[136,896]{1,0:T(8,128)(2,1)S(1)}, bf16[136,896]{1,0:T(8,128)(2,1)S(1)}, u32[]{:S(2)}, u32[]{:S(2)}) collective-permute-start(bf16[136,896]{1,0:T(8,128)(2,1)S(1)} %get-tuple-element.47), channel_id=1, source_target_pairs={{0,2},{1,3},{2,0},{3,1},{4,6},{5,7},{6,4},{7,5},{8,10},{9,11},{10,... | collective-permute-start | bytes 731144 | tf_op jit(solution)/shard_map/ppermute | solution.py:328
  6.6 21.3 %collective-permute-start.1 = (bf16[136,896]{1,0:T(8,128)(2,1)S(1)}, bf16[136,896]{1,0:T(8,128)(2,1)S(1)}, u32[]{:S(2)}, u32[]{:S(2)}) collective-permute-start(bf16[136,896]{1,0:T(8,128)(2,1)S(1)} %get-tuple-element.45), channel_id=1, source_target_pairs={{0,2},{1,3},{2,0},{3,1},{4,6},{5,7},{6,4},{7,5},{8,10},{9,11},{10,... | collective-permute-start | bytes 731144 | tf_op jit(solution)/shard_map/ppermute | solution.py:328
  6.6 24.0 %collective-permute-start.2 = (bf16[136,896]{1,0:T(8,128)(2,1)S(1)}, bf16[136,896]{1,0:T(8,128)(2,1)S(1)}, u32[]{:S(2)}, u32[]{:S(2)}) collective-permute-start(bf16[136,896]{1,0:T(8,128)(2,1)S(1)} %get-tuple-element.40.refs_0_), channel_id=1, source_target_pairs={{0,1},{1,0},{2,3},{3,2},{4,5},{5,4},{6,7},{7,6},{8,9},{9,8},{10,11... | collective-permute-start | bytes 731144 | tf_op jit(solution)/shard_map/ppermute | solution.py:328
  8.5 27.2 %collective-permute-start = (bf16[136,896]{1,0:T(8,128)(2,1)S(1)}, bf16[136,896]{1,0:T(8,128)(2,1)S(1)}, u32[]{:S(2)}, u32[]{:S(2)}) collective-permute-start(bf16[136,896]{1,0:T(8,128)(2,1)S(1)} %get-tuple-element.43.refs_1_), channel_id=1, source_target_pairs={{0,1},{1,0},{2,3},{3,2},{4,5},{5,4},{6,7},{7,6},{8,9},{9,8},{10,11... | collective-permute-start | bytes 731144 | tf_op jit(solution)/shard_map/ppermute | solution.py:328
  23.5 16.3 %collective-permute-start.6 = (bf16[136,896]{1,0:T(8,128)(2,1)S(1)}, bf16[136,896]{1,0:T(8,128)(2,1)S(1)}, u32[]{:S(2)}, u32[]{:S(2)}) collective-permute-start(bf16[136,896]{1,0:T(8,128)(2,1)S(1)} %collective-permute-done.3.refs_1_), channel_id=1, source_target_pairs={{0,1},{1,0},{2,3},{3,2},{4,5},{5,4},{6,7},{7,6},{8,9},{9,8},{10,11... | collective-permute-start | bytes 731144 | tf_op jit(solution)/shard_map/ppermute | solution.py:328
  27.9 13.0 %collective-permute-start.5 = (bf16[136,896]{1,0:T(8,128)(2,1)S(1)}, bf16[136,896]{1,0:T(8,128)(2,1)S(1)}, u32[]{:S(2)}, u32[]{:S(2)}) collective-permute-start(bf16[136,896]{1,0:T(8,128)(2,1)S(1)} %collective-permute-done.1.refs_1_), channel_id=1, source_target_pairs={{0,1},{1,0},{2,3},{3,2},{4,5},{5,4},{6,7},{7,6},{8,9},{9,8},{10,11... | collective-permute-start | bytes 731144 | tf_op jit(solution)/shard_map/ppermute | solution.py:328
  28.8 17.8 %collective-permute-start.9 = (bf16[2,40,1792]{2,1,0:T(8,128)(2,1)S(1)}, bf16[2,40,1792]{2,1,0:T(8,128)(2,1)S(1)}, u32[]{:S(2)}, u32[]{:S(2)}) collective-permute-start(bf16[2,40,1792]{2,1,0:T(8,128)(2,1)S(1)} %get-tuple-element.60), channel_id=1, source_target_pairs={{0,28},{4,24},{8,20},{12,16},{16,12},{20,8},{24,4},{28,0},{1,29},{... | collective-permute-start | bytes 860168 | tf_op jit(solution)/shard_map/ppermute | solution.py:334
  37.8 8.7 %collective-permute-start.7 = (bf16[136,896]{1,0:T(8,128)(2,1)S(1)}, bf16[136,896]{1,0:T(8,128)(2,1)S(1)}, u32[]{:S(2)}, u32[]{:S(2)}) collective-permute-start(bf16[136,896]{1,0:T(8,128)(2,1)S(1)} %get-tuple-element.58), channel_id=1, source_target_pairs={{0,1},{1,0},{2,3},{3,2},{4,5},{5,4},{6,7},{7,6},{8,9},{9,8},{10,11... | collective-permute-start | bytes 731144 | tf_op jit(solution)/shard_map/ppermute | solution.py:328
  38.2 16.2 %collective-permute-start.10 = (bf16[2,72,896]{2,1,0:T(8,128)(2,1)S(1)}, bf16[2,72,896]{2,1,0:T(8,128)(2,1)S(1)}, u32[]{:S(2)}, u32[]{:S(2)}) collective-permute-start(bf16[2,72,896]{2,1,0:T(8,128)(2,1)S(1)} %get-tuple-element.62), channel_id=1, source_target_pairs={{0,28},{4,24},{8,20},{12,16},{16,12},{20,8},{24,4},{28,0},{1,29},{... | collective-permute-start | bytes 774152 | tf_op jit(solution)/shard_map/ppermute | solution.py:334
  39.8 11.7 %collective-permute-start.12 = (bf16[2,112,512]{2,1,0:T(8,128)(2,1)S(1)}, bf16[2,112,512]{2,1,0:T(8,128)(2,1)S(1)}, u32[]{:S(2)}, u32[]{:S(2)}) collective-permute-start(bf16[2,112,512]{2,1,0:T(8,128)(2,1)S(1)} %get-tuple-element.65.hid), channel_id=1, source_target_pairs={{0,28},{4,24},{8,20},{12,16},{16,12},{20,8},{24,4},{28,0},{1,29},{... | collective-permute-start | bytes 688136 | tf_op jit(solution)/shard_map/ppermute | solution.py:334
  40.9 16.0 %collective-permute-start.11 = (bf16[2,72,896]{2,1,0:T(8,128)(2,1)S(1)}, bf16[2,72,896]{2,1,0:T(8,128)(2,1)S(1)}, u32[]{:S(2)}, u32[]{:S(2)}) collective-permute-start(bf16[2,72,896]{2,1,0:T(8,128)(2,1)S(1)} %get-tuple-element.64), channel_id=1, source_target_pairs={{0,28},{4,24},{8,20},{12,16},{16,12},{20,8},{24,4},{28,0},{1,29},{... | collective-permute-start | bytes 774152 | tf_op jit(solution)/shard_map/ppermute | solution.py:334
  46.5 20.2 %collective-permute-start.4 = (bf16[136,896]{1,0:T(8,128)(2,1)S(1)}, bf16[136,896]{1,0:T(8,128)(2,1)S(1)}, u32[]{:S(2)}, u32[]{:S(2)}) collective-permute-start(bf16[136,896]{1,0:T(8,128)(2,1)S(1)} %get-tuple-element.54), channel_id=1, source_target_pairs={{0,1},{1,0},{2,3},{3,2},{4,5},{5,4},{6,7},{7,6},{8,9},{9,8},{10,11... | collective-permute-start | bytes 731144 | tf_op jit(solution)/shard_map/ppermute | solution.py:328
  46.5 20.1 %collective-permute-start.8 = (bf16[136,896]{1,0:T(8,128)(2,1)S(1)}, bf16[136,896]{1,0:T(8,128)(2,1)S(1)}, u32[]{:S(2)}, u32[]{:S(2)}) collective-permute-start(bf16[136,896]{1,0:T(8,128)(2,1)S(1)} %shard_map.95), channel_id=1, source_target_pairs={{0,3},{1,2},{2,1},{3,0},{4,7},{5,6},{6,5},{7,4},{8,11},{9,10},{10,... | collective-permute-start | bytes 731144 | tf_op jit(solution)/shard_map/ppermute | solution.py:328
  51.5 12.9 %collective-permute-start.13 = (bf16[2,40,896]{2,1,0:T(8,128)(2,1)S(1)}, bf16[2,40,896]{2,1,0:T(8,128)(2,1)S(1)}, u32[]{:S(2)}, u32[]{:S(2)}) collective-permute-start(bf16[2,40,896]{2,1,0:T(8,128)(2,1)S(1)} %get-tuple-element.71), channel_id=1, source_target_pairs={{0,28},{4,24},{8,20},{12,16},{16,12},{20,8},{24,4},{28,0},{1,29},{... | collective-permute-start | bytes 430088 | tf_op jit(solution)/shard_map/ppermute | solution.py:334
  54.4 9.9 %collective-permute-start.14 = (bf16[2,40,896]{2,1,0:T(8,128)(2,1)S(1)}, bf16[2,40,896]{2,1,0:T(8,128)(2,1)S(1)}, u32[]{:S(2)}, u32[]{:S(2)}) collective-permute-start(bf16[2,40,896]{2,1,0:T(8,128)(2,1)S(1)} %get-tuple-element.72), channel_id=1, source_target_pairs={{0,28},{4,24},{8,20},{12,16},{16,12},{20,8},{24,4},{28,0},{1,29},{... | collective-permute-start | bytes 430088 | tf_op jit(solution)/shard_map/ppermute | solution.py:334
  56.9 7.5 %collective-permute-start.15 = (bf16[2,40,512]{2,1,0:T(8,128)(2,1)S(1)}, bf16[2,40,512]{2,1,0:T(8,128)(2,1)S(1)}, u32[]{:S(2)}, u32[]{:S(2)}) collective-permute-start(bf16[2,40,512]{2,1,0:T(8,128)(2,1)S(1)} %get-tuple-element.68.refs_2_), channel_id=1, source_target_pairs={{0,28},{4,24},{8,20},{12,16},{16,12},{20,8},{24,4},{28,0},{1,29},{... | collective-permute-start | bytes 245768 | tf_op jit(solution)/shard_map/ppermute | solution.py:334

commit v6 on v5

--- a/solution.py
+++ b/solution.py
@@ -242,29 +242,24 @@
 ACROSS_ROWS = ((0,), (0,))
 
 
-def grad_kernel(own_keep, own_far, x_keep, x_far, g_keep, g_far, hid, hid_far, *refs):
-    last, (up_ref, down_ref) = refs[:-2], refs[-2:]
+def grad_kernel(own_keep, own_far, x_keep, x_far, g_keep, g_far, hid, hid_far, up_ref, down_ref):
     width = x_keep.shape[2]
-    dpre, act = (jnp.concatenate([ref[t] for ref in (hid, hid_far) + last[2:]], axis=0) for t in range(2))
+    dpre, act = (jnp.concatenate([ref[t] for ref in (hid, hid_far)], axis=0) for t in range(2))
     for chunk in range(x_keep.shape[0]):
         x, g = (
-            jnp.concatenate(
-                [own_keep[chunk, :, at], keep[chunk], own_far[chunk, :, at], far[chunk]] + [ref[chunk] for ref in more], axis=0
-            )
-            for keep, far, at, more in (
-                (x_keep, x_far, slice(0, width), last[0:1]), (g_keep, g_far, slice(width, 2 * width), last[1:2])
-            )
+            jnp.concatenate([own_keep[chunk, :, at], keep[chunk], own_far[chunk, :, at], far[chunk]], axis=0)
+            for keep, far, at in ((x_keep, x_far, slice(0, width)), (g_keep, g_far, slice(width, 2 * width)))
         )
         up_ref[chunk] = dot(x, dpre, ACROSS_ROWS).astype(up_ref.dtype)
         down_ref[chunk] = dot(act, g, ACROSS_ROWS).astype(down_ref.dtype)
 
 
-def grad_last_kernel(up_part, down_part, x_far, g_far, hid_far, up_hbm, down_hbm, up_out, down_out, sems):
-    width = x_far.shape[2]
-    dpre, act = hid_far[0], hid_far[1]
+def grad_last_kernel(up_part, down_part, x_keep, x_far, g_keep, g_far, hid, hid_far, up_hbm, down_hbm, up_out, down_out, sems):
+    width = x_keep.shape[2]
+    dpre, act = (jnp.concatenate([ref[t] for ref in (hid, hid_far)], axis=0) for t in range(2))
     copies = []
-    for chunk in range(x_far.shape[0]):
-        x, g = x_far[chunk], g_far[chunk]
+    for chunk in range(x_keep.shape[0]):
+        x, g = (jnp.concatenate([ref[chunk] for ref in refs], axis=0) for refs in ((x_keep, x_far), (g_keep, g_far)))
         at = slice(chunk * width, (chunk + 1) * width)
         up_out[chunk] = (up_part[chunk] + dot(x, dpre, ACROSS_ROWS)).astype(BF16)
         copies.append(pltpu.make_async_copy(up_out.at[chunk], up_hbm.at[at, :], sems.at[2 * chunk]))
@@ -277,9 +272,8 @@
 
 
 def final_kernel(own_count, masks_ref, *refs):
-    own_refs, other_refs, (out_hbm, out_ref, sems) = refs[:own_count], refs[own_count:-3], refs[-3:]
-    width = out_ref.shape[2]
-    copies = []
+    own_refs, other_refs, out_ref = refs[:own_count], refs[own_count:-1], refs[-1]
+    width = out_ref.shape[1] // CHUNKS
 
     def sides(lo, hi):
         return [sum(ref[lo:hi, :].astype(F32) for ref in side) for side in (own_refs, other_refs)]
@@ -287,12 +281,7 @@
     folds = sides(CHUNKS * MAIN, CHUNKS * MAIN + FOLD)
     for chunk in range(CHUNKS):
         rows = jnp.concatenate(sides(chunk * MAIN, (chunk + 1) * MAIN) + folds, axis=0).astype(BF16)
-        out_ref[chunk] = dot(masks_ref[chunk], rows, ((0,), (0,))).astype(BF16)
-        at = slice(chunk * width, (chunk + 1) * width)
-        copies.append(pltpu.make_async_copy(out_ref.at[chunk], out_hbm.at[:, at], sems.at[chunk]))
-        copies[-1].start()
-    for copy in copies:
-        copy.wait()
+        out_ref[:, chunk * width:(chunk + 1) * width] = dot(masks_ref[chunk], rows, ((0,), (0,))).astype(BF16)
 
 
 def per_device(tokens, cotangent, router_gate, routes, up_weight, down_weight):
@@ -405,8 +394,7 @@
             in_specs=[vmem()] * 4,
             out_specs=(vmem(),) * 2,
         )(last_rows, last_pre, up_t, down_t)
-        for_grad += [xl_keep, gl_keep, last_hidden]
-        for_last = [xl_far, gl_far, mirror(last_hidden)]
+        for_last = [xl_keep, xl_far, gl_keep, gl_far, last_hidden, mirror(last_hidden)]
         for_far = swap(back[2], 1)
         both = call(add_kernel, payload, small, small, in_specs=[vmem()] * 2, out_specs=vmem())(last_back, for_far)
         own_side, other_side = [back[0], swap(back[1], 1)], [swap(both, 3)]
@@ -417,14 +405,14 @@
     kept = F32 if line else BF16
     grad_up, grad_down = call(
         grad_kernel, (held((half, width, hidden), kept), held((half, hidden, width), kept)), 2 * flops, moved,
-        in_specs=[vmem()] * len(for_grad), out_specs=(vmem(),) * 2,
+        in_specs=[vmem()] * 8, out_specs=(vmem(),) * 2,
     )(*for_grad)
     if line:
         grad_up, grad_down = call(
             grad_last_kernel,
             (jax.ShapeDtypeStruct((model // 2, hidden), BF16), jax.ShapeDtypeStruct((hidden, model // 2), BF16)),
             flops, moved,
-            in_specs=[vmem()] * 5, out_specs=(hbm(),) * 2,
+            in_specs=[vmem()] * 8, out_specs=(hbm(),) * 2,
             scratch_shapes=[
                 pltpu.VMEM((half, width, hidden), BF16), pltpu.VMEM((half, hidden, width), BF16), pltpu.SemaphoreType.DMA((2 * half,))
             ],
@@ -433,8 +421,7 @@
         grad_up, grad_down = grad_up.reshape(model // 2, hidden), grad_down.transpose(1, 0, 2).reshape(hidden, model // 2)
     input_grad = call(
         functools.partial(final_kernel, len(own_side)), jax.ShapeDtypeStruct((tok, model), BF16), small, small,
-        in_specs=[vmem()] * (1 + len(own_side) + len(other_side)), out_specs=hbm(),
-        scratch_shapes=[pltpu.VMEM((CHUNKS, tok, width), BF16), pltpu.SemaphoreType.DMA((CHUNKS,))],
+        in_specs=[vmem()] * (1 + len(own_side) + len(other_side)), out_specs=vmem(),
     )(masks, *own_side, *other_side)
     return (input_grad[None], grad_up[None], grad_down[None])
 

time: 68.9 us -> 69.3 us (level)
  waiting for transfers between devices: 24.9 us -> 26.3 us
  Pallas kernels: 17.5 us -> 16.6 us
    pallas_call x1, Pallas kernels: 2.18 us -> 1.24 us  [per_device(): call(grad_kernel, (held((half, width, hidden), kept), held((half, hidden,...]
    ppermute x7, waiting for transfers between devices: 4.61 us -> 5.55 us  [mirror(): lax.ppermute(value, 'pipe', [(i, ranks - 1 - i) for i in range(ranks)])]
  transfers between devices with their start and end apart: 16 -> 16, of which waited for: 5 -> 5; matrix products, arithmetic and copies ran while one was open for 0% -> 0% of each run, Pallas kernels for 22% -> 20%
where the time goes in v6:
time: 69.3 us; the launch traced here: 68.1 us
  waiting for transfers between devices  26.3 us (38%)
  starting transfers between devices  24.4 us (35%)
  Pallas kernels  16.6 us (24%)
  between operations  0.77 us (1%)
    ppermute x9, waiting for transfers between devices, send(): return lax.ppermute(value, 'expert', pairs)  20.8 us
    ppermute x9, starting transfers between devices, send(): return lax.ppermute(value, 'expert', pairs)  12.3 us
    ppermute x7, starting transfers between devices, mirror(): lax.ppermute(value, 'pipe', [(i, ranks - 1 - i) for i in range(ranks)])  12.2 us
    ppermute x7, waiting for transfers between devices, mirror(): lax.ppermute(value, 'pipe', [(i, ranks - 1 - i) for i in range(ranks)])  5.55 us
    pallas_call x1, Pallas kernels, per_device(): call(functools.partial(pre_kernel, size), (held((rows, hidden), F32), hal...  3.18 us
    pallas_call x1, Pallas kernels, per_device(): call(grad_last_kernel, (jax.ShapeDtypeStruct((model // 2, hidden), BF16),...  2.29 us
    pallas_call x1, Pallas kernels, per_device(): call(flip_kernel, (held((hidden, model)), held((model, hidden))), small,...  1.94 us
    pallas_call x1, Pallas kernels, per_device(): call(group_kernel, (held((2, rows, hidden)),) + (payload,) * (size + 1),...  1.82 us
  transfers between devices with their start and end apart: 16, of which 5 were waited for; matrix products, arithmetic and copies ran while one was open for 0% of the time, Pallas kernels for 20%

profile of v6, /device:TPU:0, one launch (start us, length us, event | category | flops | bytes accessed | tf_op | source)
XLA Modules:
  0.0 68.1 jit_solution(7179456116179661221)
XLA Ops:
  0.6 1.4 %shard_map.85 = (bf16[136,896]{1,0:T(8,128)(2,1)S(1)}, bf16[136,896]{1,0:T(8,128)(2,1)S(1)}, bf16[4,80,64]{2,1,0:T(8,128)(2,1)S(1)}, f32[1,64]{1,0:T(1,128)S(1)}, bf16[64,3584]{1,0:T(8,128)(2,1)S(1)}) custom-call(s32[1]{0:T(128)} %bitcast.mine_ref, s32[1,64]{1,0:T(1,128)} %bitcast.15, f32[1,64]{1,0:T(1,128)} %gate_hbm.1, bf16[64,3584]{1,0:T(8,128)(2,1)} %bitcast.12, ...), custom_call_target="tpu_custom_call" | custom-call | flops 1048576 | bytes 1048576 | tf_op jit(solution)/shard_map/pallas_call | solution.py:326
  2.0 0.4 shard_map.86
  2.4 4.1 %collective-permute-start.1 = (bf16[136,896]{1,0:T(8,128)(2,1)S(1)}, bf16[136,896]{1,0:T(8,128)(2,1)S(1)}, u32[]{:S(2)}, u32[]{:S(2)}) collective-permute-start(bf16[136,896]{1,0:T(8,128)(2,1)S(1)} %get-tuple-element.45), channel_id=1, source_target_pairs={{0,2},{1,3},{2,0},{3,1},{4,6},{5,7},{6,4},{7,5},{8,10},{9,11},{10,... | collective-permute-start | bytes 731144 | tf_op jit(solution)/shard_map/ppermute | solution.py:317
  6.6 0.1 collective-permute-start.3
  6.6 1.8 %collective-permute-start.2 = (bf16[136,896]{1,0:T(8,128)(2,1)S(1)}, bf16[136,896]{1,0:T(8,128)(2,1)S(1)}, u32[]{:S(2)}, u32[]{:S(2)}) collective-permute-start(bf16[136,896]{1,0:T(8,128)(2,1)S(1)} %get-tuple-element.40.refs_0_), channel_id=1, source_target_pairs={{0,1},{1,0},{2,3},{3,2},{4,5},{5,4},{6,7},{7,6},{8,9},{9,8},{10,11... | collective-permute-start | bytes 731144 | tf_op jit(solution)/shard_map/ppermute | solution.py:317
  8.5 0.2 collective-permute-start
  8.7 15.2 %collective-permute-done.1.refs_1_ = bf16[136,896]{1,0:T(8,128)(2,1)S(1)} collective-permute-done((bf16[136,896]{1,0:T(8,128)(2,1)S(1)}, bf16[136,896]{1,0:T(8,128)(2,1)S(1)}, u32[]{:S(2)}, u32[]{:S(2)}) %collective-permute-start.1) | collective-permute-done | bytes 243744 | tf_op jit(solution)/shard_map/ppermute | solution.py:317
  23.9 0.0 collective-permute-start.5
  23.9 4.4 %collective-permute-done.3.refs_1_ = bf16[136,896]{1,0:T(8,128)(2,1)S(1)} collective-permute-done((bf16[136,896]{1,0:T(8,128)(2,1)S(1)}, bf16[136,896]{1,0:T(8,128)(2,1)S(1)}, u32[]{:S(2)}, u32[]{:S(2)}) %collective-permute-start.3) | collective-permute-done | bytes 243744 | tf_op jit(solution)/shard_map/ppermute | solution.py:317
  28.2 0.7 collective-permute-start.6
  28.9 0.2 shard_map.87
  29.2 1.8 %collective-permute-start.9 = (bf16[2,40,1792]{2,1,0:T(8,128)(2,1)S(1)}, bf16[2,40,1792]{2,1,0:T(8,128)(2,1)S(1)}, u32[]{:S(2)}, u32[]{:S(2)}) collective-permute-start(bf16[2,40,1792]{2,1,0:T(8,128)(2,1)S(1)} %get-tuple-element.60), channel_id=1, source_target_pairs={{0,28},{4,24},{8,20},{12,16},{16,12},{20,8},{24,4},{28,0},{1,29},{... | collective-permute-start | bytes 860168 | tf_op jit(solution)/shard_map/ppermute | solution.py:323
  31.0 0.0 collective-permute-done.2.refs_0_
  31.0 3.2 %shard_map.89 = (f32[112,512]{1,0:T(8,128)S(1)}, bf16[2,72,896]{2,1,0:T(8,128)(2,1)S(1)}, bf16[2,72,896]{2,1,0:T(8,128)(2,1)S(1)}, bf16[3584,512]{1,0:T(8,128)(2,1)S(1)}, bf16[512,3584]{1,0:T(8,128)(2,1)S(1)}) custom-call(s32[1]{0:T(128)} %bitcast.4.upper_ref, bf16[2,4,40,896]{3,2,1,0:T(8,128)(2,1)S(1)} %get-tuple-element.44.first_ref, ...), custom_call_target="tpu_custom_call" | custom-call | flops 411041792 | bytes 3670016 | tf_op jit(solution)/shard_map/pallas_call | solution.py:353
  34.2 1.9 %shard_map.90 = (bf16[512,3584]{1,0:T(8,128)(2,1)S(1)}, bf16[3584,512]{1,0:T(8,128)(2,1)S(1)}) custom-call(bf16[3584,512]{1,0:T(8,128)(2,1)S(1)} %get-tuple-element.49.up_ref, bf16[512,3584]{1,0:T(8,128)(2,1)S(1)} %get-tuple-element.50.down_ref), custom_call_target="tpu_custom_call" | custom-call | flops 1048576 | bytes 3670016 | tf_op jit(solution)/shard_map/pallas_call | solution.py:364
  36.1 0.0 collective-permute-done.refs_0_
  36.2 0.2 shard_map.88
  36.4 1.8 %shard_map.91 = (bf16[2,112,512]{2,1,0:T(8,128)(2,1)S(1)}, bf16[136,896]{1,0:T(8,128)(2,1)S(1)}, bf16[136,896]{1,0:T(8,128)(2,1)S(1)}, bf16[136,896]{1,0:T(8,128)(2,1)S(1)}) custom-call(bf16[2,4,40,896]{3,2,1,0:T(8,128)(2,1)S(1)} %get-tuple-element.44.first_ref, bf16[4,72,896]{2,1,0:T(8,128)(2,1)S(1)} %get-tuple-element.46.rows_ref, ...), custom_call_target="tpu_custom_call" | custom-call | flops 822083584 | bytes 7340032 | tf_op jit(solution)/shard_map/pallas_call | solution.py:372
  38.2 0.4 collective-permute-start.7
  38.6 1.6 %collective-permute-start.10 = (bf16[2,72,896]{2,1,0:T(8,128)(2,1)S(1)}, bf16[2,72,896]{2,1,0:T(8,128)(2,1)S(1)}, u32[]{:S(2)}, u32[]{:S(2)}) collective-permute-start(bf16[2,72,896]{2,1,0:T(8,128)(2,1)S(1)} %get-tuple-element.62), channel_id=1, source_target_pairs={{0,28},{4,24},{8,20},{12,16},{16,12},{20,8},{24,4},{28,0},{1,29},{... | collective-permute-start | bytes 774152 | tf_op jit(solution)/shard_map/ppermute | solution.py:323
  40.2 0.0 collective-permute-done.5.refs_0_
  40.2 1.0 %collective-permute-start.12 = (bf16[2,112,512]{2,1,0:T(8,128)(2,1)S(1)}, bf16[2,112,512]{2,1,0:T(8,128)(2,1)S(1)}, u32[]{:S(2)}, u32[]{:S(2)}) collective-permute-start(bf16[2,112,512]{2,1,0:T(8,128)(2,1)S(1)} %get-tuple-element.65.hid), channel_id=1, source_target_pairs={{0,28},{4,24},{8,20},{12,16},{16,12},{20,8},{24,4},{28,0},{1,29},{... | collective-permute-start | bytes 688136 | tf_op jit(solution)/shard_map/ppermute | solution.py:323
  41.3 0.0 collective-permute-done.6.payload_ref
  41.3 1.6 %collective-permute-start.11 = (bf16[2,72,896]{2,1,0:T(8,128)(2,1)S(1)}, bf16[2,72,896]{2,1,0:T(8,128)(2,1)S(1)}, u32[]{:S(2)}, u32[]{:S(2)}) collective-permute-start(bf16[2,72,896]{2,1,0:T(8,128)(2,1)S(1)} %get-tuple-element.64), channel_id=1, source_target_pairs={{0,28},{4,24},{8,20},{12,16},{16,12},{20,8},{24,4},{28,0},{1,29},{... | collective-permute-start | bytes 774152 | tf_op jit(solution)/shard_map/ppermute | solution.py:323
  42.9 0.2 shard_map.92
  43.0 0.8 %shard_map.93 = (f32[40,512]{1,0:T(8,128)S(1)}, bf16[2,40,896]{2,1,0:T(8,128)(2,1)S(1)}, bf16[2,40,896]{2,1,0:T(8,128)(2,1)S(1)}) custom-call(s32[1]{0:T(128)} %bitcast.4.upper_ref, bf16[136,896]{1,0:T(8,128)(2,1)S(1)} %collective-permute-done.6.payload_ref, bf16[3584,512]{1,0:T(8,128)(2,1)S(1)} %get-tuple-element.49.up_ref), custom_call_target="tpu_custom_call" | custom-call | flops 411041792 | bytes 3670016 | tf_op jit(solution)/shard_map/pallas_call | solution.py:381
  43.9 1.8 %shard_map.94 = (bf16[2,40,512]{2,1,0:T(8,128)(2,1)S(1)}, bf16[136,896]{1,0:T(8,128)(2,1)S(1)}) custom-call(bf16[4,40,896]{2,1,0:T(8,128)(2,1)S(1)} %get-tuple-element.55.rows, f32[40,512]{1,0:T(8,128)S(1)} %get-tuple-element.56.pre_ref, bf16[512,3584]{1,0:T(8,128)(2,1)S(1)} %get-tuple-element.51.up_ref, bf16[3584,512]{1,0:T(8,128)(2,1)S(1)} %get-tuple-element.52.down_ref), custom_call_target="tpu_custom_call" | custom-call | flops 411041792 | bytes 7340032 | tf_op jit(solution)/shard_map/pallas_call | solution.py:392
  45.7 1.2 %collective-permute-done.7.b_ref = bf16[136,896]{1,0:T(8,128)(2,1)S(1)} collective-permute-done((bf16[136,896]{1,0:T(8,128)(2,1)S(1)}, bf16[136,896]{1,0:T(8,128)(2,1)S(1)}, u32[]{:S(2)}, u32[]{:S(2)}) %collective-permute-start.7) | collective-permute-done | bytes 243744 | tf_op jit(solution)/shard_map/ppermute | solution.py:317
  46.8 0.0 collective-permute-start.4
  46.8 0.1 shard_map.95
  46.9 0.0 collective-permute-done.9.own_far
  46.9 5.0 %collective-permute-start.8 = (bf16[136,896]{1,0:T(8,128)(2,1)S(1)}, bf16[136,896]{1,0:T(8,128)(2,1)S(1)}, u32[]{:S(2)}, u32[]{:S(2)}) collective-permute-start(bf16[136,896]{1,0:T(8,128)(2,1)S(1)} %shard_map.95), channel_id=1, source_target_pairs={{0,3},{1,2},{2,1},{3,0},{4,7},{5,6},{6,5},{7,4},{8,11},{9,10},{10,... | collective-permute-start | bytes 731144 | tf_op jit(solution)/shard_map/ppermute | solution.py:317
  51.9 0.0 collective-permute-done.12.hid_far
  51.9 2.9 %collective-permute-start.13 = (bf16[2,40,896]{2,1,0:T(8,128)(2,1)S(1)}, bf16[2,40,896]{2,1,0:T(8,128)(2,1)S(1)}, u32[]{:S(2)}, u32[]{:S(2)}) collective-permute-start(bf16[2,40,896]{2,1,0:T(8,128)(2,1)S(1)} %get-tuple-element.69), channel_id=1, source_target_pairs={{0,28},{4,24},{8,20},{12,16},{16,12},{20,8},{24,4},{28,0},{1,29},{... | collective-permute-start | bytes 430088 | tf_op jit(solution)/shard_map/ppermute | solution.py:323
  54.8 0.0 collective-permute-done.10.x_far
  54.8 0.0 collective-permute-start.14
  54.9 2.4 %collective-permute-done.11.g_far = bf16[2,72,896]{2,1,0:T(8,128)(2,1)S(1)} collective-permute-done((bf16[2,72,896]{2,1,0:T(8,128)(2,1)S(1)}, bf16[2,72,896]{2,1,0:T(8,128)(2,1)S(1)}, u32[]{:S(2)}, u32[]{:S(2)}) %collective-permute-start.11) | collective-permute-done | bytes 258080 | tf_op jit(solution)/shard_map/ppermute | solution.py:323
  57.3 3.1 %collective-permute-start.15 = (bf16[2,40,512]{2,1,0:T(8,128)(2,1)S(1)}, bf16[2,40,512]{2,1,0:T(8,128)(2,1)S(1)}, u32[]{:S(2)}, u32[]{:S(2)}) collective-permute-start(bf16[2,40,512]{2,1,0:T(8,128)(2,1)S(1)} %get-tuple-element.72.hid), channel_id=1, source_target_pairs={{0,28},{4,24},{8,20},{12,16},{16,12},{20,8},{24,4},{28,0},{1,29},{... | collective-permute-start | bytes 245768 | tf_op jit(solution)/shard_map/ppermute | solution.py:323
  60.4 1.2 %shard_map.97 = (f32[2,896,512]{2,1,0:T(8,128)S(1)}, f32[2,512,896]{2,1,0:T(8,128)S(1)}) custom-call(bf16[2,40,1792]{2,1,0:T(8,128)(2,1)S(1)} %get-tuple-element.59.own_keep, bf16[2,40,1792]{2,1,0:T(8,128)(2,1)S(1)} %collective-permute-done.9.own_far, bf16[2,72,896]{2,1,0:T(8,128)(2,1)S(1)} %get-tuple-element.61.x_keep, ...), custom_call_target="tpu_custom_call" | custom-call | flops 822083584 | bytes 3670016 | tf_op jit(solution)/shard_map/pallas_call | solution.py:406
  61.6 3.1 %collective-permute-done.15.hid_far = bf16[2,40,512]{2,1,0:T(8,128)(2,1)S(1)} collective-permute-done((bf16[2,40,512]{2,1,0:T(8,128)(2,1)S(1)}, bf16[2,40,512]{2,1,0:T(8,128)(2,1)S(1)}, u32[]{:S(2)}, u32[]{:S(2)}) %collective-permute-start.15) | collective-permute-done | bytes 81952 | tf_op jit(solution)/shard_map/ppermute | solution.py:323
  64.7 0.0 collective-permute-done.13.x_far
  64.7 0.0 collective-permute-done.14.g_far
  64.7 2.3 %shard_map.98 = (bf16[1792,512]{1,0:T(8,128)(2,1)}, bf16[512,1792]{1,0:T(8,128)(2,1)}) custom-call(f32[2,896,512]{2,1,0:T(8,128)S(1)} %get-tuple-element.66.up_part, f32[2,512,896]{2,1,0:T(8,128)S(1)} %get-tuple-element.67.down_part, bf16[2,40,896]{2,1,0:T(8,128)(2,1)S(1)} %get-tuple-element.68.x_keep, ...), custom_call_target="tpu_custom_call" | custom-call | flops 411041792 | bytes 3670016 | tf_op jit(solution)/shard_map/pallas_call | solution.py:411
  67.0 0.0 collective-permute-done.4.refs_1_
  67.1 0.0 collective-permute-done.8.refs_2_
  67.1 1.1 %shard_map.96 = bf16[64,3584]{1,0:T(8,128)(2,1)} custom-call(bf16[4,80,64]{2,1,0:T(8,128)(2,1)S(1)} %get-tuple-element.39.masks_ref, bf16[136,896]{1,0:T(8,128)(2,1)S(1)} %get-tuple-element.53.refs_0_, bf16[136,896]{1,0:T(8,128)(2,1)S(1)} %collective-permute-done.4.refs_1_, bf16[136,896]{1,0:T(8,128)(2,1)S(1)} %collective-permute-done.8.refs_2_), custom_call_target="tpu_custom_call" | custom-call | flops 1048576 | bytes 1048576 | tf_op jit(solution)/shard_map/pallas_call | solution.py:422
Async XLA Ops:
  2.4 21.4 %collective-permute-start.1 = (bf16[136,896]{1,0:T(8,128)(2,1)S(1)}, bf16[136,896]{1,0:T(8,128)(2,1)S(1)}, u32[]{:S(2)}, u32[]{:S(2)}) collective-permute-start(bf16[136,896]{1,0:T(8,128)(2,1)S(1)} %get-tuple-element.45), channel_id=1, source_target_pairs={{0,2},{1,3},{2,0},{3,1},{4,6},{5,7},{6,4},{7,5},{8,10},{9,11},{10,... | collective-permute-start | bytes 731144 | tf_op jit(solution)/shard_map/ppermute | solution.py:317
  6.6 21.7 %collective-permute-start.3 = (bf16[136,896]{1,0:T(8,128)(2,1)S(1)}, bf16[136,896]{1,0:T(8,128)(2,1)S(1)}, u32[]{:S(2)}, u32[]{:S(2)}) collective-permute-start(bf16[136,896]{1,0:T(8,128)(2,1)S(1)} %get-tuple-element.47), channel_id=1, source_target_pairs={{0,2},{1,3},{2,0},{3,1},{4,6},{5,7},{6,4},{7,5},{8,10},{9,11},{10,... | collective-permute-start | bytes 731144 | tf_op jit(solution)/shard_map/ppermute | solution.py:317
  6.6 24.4 %collective-permute-start.2 = (bf16[136,896]{1,0:T(8,128)(2,1)S(1)}, bf16[136,896]{1,0:T(8,128)(2,1)S(1)}, u32[]{:S(2)}, u32[]{:S(2)}) collective-permute-start(bf16[136,896]{1,0:T(8,128)(2,1)S(1)} %get-tuple-element.40.refs_0_), channel_id=1, source_target_pairs={{0,1},{1,0},{2,3},{3,2},{4,5},{5,4},{6,7},{7,6},{8,9},{9,8},{10,11... | collective-permute-start | bytes 731144 | tf_op jit(solution)/shard_map/ppermute | solution.py:317
  8.5 27.7 %collective-permute-start = (bf16[136,896]{1,0:T(8,128)(2,1)S(1)}, bf16[136,896]{1,0:T(8,128)(2,1)S(1)}, u32[]{:S(2)}, u32[]{:S(2)}) collective-permute-start(bf16[136,896]{1,0:T(8,128)(2,1)S(1)} %get-tuple-element.43.refs_1_), channel_id=1, source_target_pairs={{0,1},{1,0},{2,3},{3,2},{4,5},{5,4},{6,7},{7,6},{8,9},{9,8},{10,11... | collective-permute-start | bytes 731144 | tf_op jit(solution)/shard_map/ppermute | solution.py:317
  23.9 16.3 %collective-permute-start.5 = (bf16[136,896]{1,0:T(8,128)(2,1)S(1)}, bf16[136,896]{1,0:T(8,128)(2,1)S(1)}, u32[]{:S(2)}, u32[]{:S(2)}) collective-permute-start(bf16[136,896]{1,0:T(8,128)(2,1)S(1)} %collective-permute-done.1.refs_1_), channel_id=1, source_target_pairs={{0,1},{1,0},{2,3},{3,2},{4,5},{5,4},{6,7},{7,6},{8,9},{9,8},{10,11... | collective-permute-start | bytes 731144 | tf_op jit(solution)/shard_map/ppermute | solution.py:317
  28.2 13.0 %collective-permute-start.6 = (bf16[136,896]{1,0:T(8,128)(2,1)S(1)}, bf16[136,896]{1,0:T(8,128)(2,1)S(1)}, u32[]{:S(2)}, u32[]{:S(2)}) collective-permute-start(bf16[136,896]{1,0:T(8,128)(2,1)S(1)} %collective-permute-done.3.refs_1_), channel_id=1, source_target_pairs={{0,1},{1,0},{2,3},{3,2},{4,5},{5,4},{6,7},{7,6},{8,9},{9,8},{10,11... | collective-permute-start | bytes 731144 | tf_op jit(solution)/shard_map/ppermute | solution.py:317
  29.2 17.7 %collective-permute-start.9 = (bf16[2,40,1792]{2,1,0:T(8,128)(2,1)S(1)}, bf16[2,40,1792]{2,1,0:T(8,128)(2,1)S(1)}, u32[]{:S(2)}, u32[]{:S(2)}) collective-permute-start(bf16[2,40,1792]{2,1,0:T(8,128)(2,1)S(1)} %get-tuple-element.60), channel_id=1, source_target_pairs={{0,28},{4,24},{8,20},{12,16},{16,12},{20,8},{24,4},{28,0},{1,29},{... | collective-permute-start | bytes 860168 | tf_op jit(solution)/shard_map/ppermute | solution.py:323
  38.2 8.7 %collective-permute-start.7 = (bf16[136,896]{1,0:T(8,128)(2,1)S(1)}, bf16[136,896]{1,0:T(8,128)(2,1)S(1)}, u32[]{:S(2)}, u32[]{:S(2)}) collective-permute-start(bf16[136,896]{1,0:T(8,128)(2,1)S(1)} %get-tuple-element.58), channel_id=1, source_target_pairs={{0,1},{1,0},{2,3},{3,2},{4,5},{5,4},{6,7},{7,6},{8,9},{9,8},{10,11... | collective-permute-start | bytes 731144 | tf_op jit(solution)/shard_map/ppermute | solution.py:317
  38.6 16.2 %collective-permute-start.10 = (bf16[2,72,896]{2,1,0:T(8,128)(2,1)S(1)}, bf16[2,72,896]{2,1,0:T(8,128)(2,1)S(1)}, u32[]{:S(2)}, u32[]{:S(2)}) collective-permute-start(bf16[2,72,896]{2,1,0:T(8,128)(2,1)S(1)} %get-tuple-element.62), channel_id=1, source_target_pairs={{0,28},{4,24},{8,20},{12,16},{16,12},{20,8},{24,4},{28,0},{1,29},{... | collective-permute-start | bytes 774152 | tf_op jit(solution)/shard_map/ppermute | solution.py:323
  40.2 11.7 %collective-permute-start.12 = (bf16[2,112,512]{2,1,0:T(8,128)(2,1)S(1)}, bf16[2,112,512]{2,1,0:T(8,128)(2,1)S(1)}, u32[]{:S(2)}, u32[]{:S(2)}) collective-permute-start(bf16[2,112,512]{2,1,0:T(8,128)(2,1)S(1)} %get-tuple-element.65.hid), channel_id=1, source_target_pairs={{0,28},{4,24},{8,20},{12,16},{16,12},{20,8},{24,4},{28,0},{1,29},{... | collective-permute-start | bytes 688136 | tf_op jit(solution)/shard_map/ppermute | solution.py:323
  41.3 16.0 %collective-permute-start.11 = (bf16[2,72,896]{2,1,0:T(8,128)(2,1)S(1)}, bf16[2,72,896]{2,1,0:T(8,128)(2,1)S(1)}, u32[]{:S(2)}, u32[]{:S(2)}) collective-permute-start(bf16[2,72,896]{2,1,0:T(8,128)(2,1)S(1)} %get-tuple-element.64), channel_id=1, source_target_pairs={{0,28},{4,24},{8,20},{12,16},{16,12},{20,8},{24,4},{28,0},{1,29},{... | collective-permute-start | bytes 774152 | tf_op jit(solution)/shard_map/ppermute | solution.py:323
  46.8 20.2 %collective-permute-start.4 = (bf16[136,896]{1,0:T(8,128)(2,1)S(1)}, bf16[136,896]{1,0:T(8,128)(2,1)S(1)}, u32[]{:S(2)}, u32[]{:S(2)}) collective-permute-start(bf16[136,896]{1,0:T(8,128)(2,1)S(1)} %get-tuple-element.54), channel_id=1, source_target_pairs={{0,1},{1,0},{2,3},{3,2},{4,5},{5,4},{6,7},{7,6},{8,9},{9,8},{10,11... | collective-permute-start | bytes 731144 | tf_op jit(solution)/shard_map/ppermute | solution.py:317
  46.9 20.1 %collective-permute-start.8 = (bf16[136,896]{1,0:T(8,128)(2,1)S(1)}, bf16[136,896]{1,0:T(8,128)(2,1)S(1)}, u32[]{:S(2)}, u32[]{:S(2)}) collective-permute-start(bf16[136,896]{1,0:T(8,128)(2,1)S(1)} %shard_map.95), channel_id=1, source_target_pairs={{0,3},{1,2},{2,1},{3,0},{4,7},{5,6},{6,5},{7,4},{8,11},{9,10},{10,... | collective-permute-start | bytes 731144 | tf_op jit(solution)/shard_map/ppermute | solution.py:317
  51.9 12.9 %collective-permute-start.13 = (bf16[2,40,896]{2,1,0:T(8,128)(2,1)S(1)}, bf16[2,40,896]{2,1,0:T(8,128)(2,1)S(1)}, u32[]{:S(2)}, u32[]{:S(2)}) collective-permute-start(bf16[2,40,896]{2,1,0:T(8,128)(2,1)S(1)} %get-tuple-element.69), channel_id=1, source_target_pairs={{0,28},{4,24},{8,20},{12,16},{16,12},{20,8},{24,4},{28,0},{1,29},{... | collective-permute-start | bytes 430088 | tf_op jit(solution)/shard_map/ppermute | solution.py:323
  54.8 9.9 %collective-permute-start.14 = (bf16[2,40,896]{2,1,0:T(8,128)(2,1)S(1)}, bf16[2,40,896]{2,1,0:T(8,128)(2,1)S(1)}, u32[]{:S(2)}, u32[]{:S(2)}) collective-permute-start(bf16[2,40,896]{2,1,0:T(8,128)(2,1)S(1)} %get-tuple-element.71), channel_id=1, source_target_pairs={{0,28},{4,24},{8,20},{12,16},{16,12},{20,8},{24,4},{28,0},{1,29},{... | collective-permute-start | bytes 430088 | tf_op jit(solution)/shard_map/ppermute | solution.py:323
  57.3 7.5 %collective-permute-start.15 = (bf16[2,40,512]{2,1,0:T(8,128)(2,1)S(1)}, bf16[2,40,512]{2,1,0:T(8,128)(2,1)S(1)}, u32[]{:S(2)}, u32[]{:S(2)}) collective-permute-start(bf16[2,40,512]{2,1,0:T(8,128)(2,1)S(1)} %get-tuple-element.72.hid), channel_id=1, source_target_pairs={{0,28},{4,24},{8,20},{12,16},{16,12},{20,8},{24,4},{28,0},{1,29},{... | collective-permute-start | bytes 245768 | tf_op jit(solution)/shard_map/ppermute | solution.py:323
